TPU v7x, 256 devices: a whole 4x4x8 slice. The times are simulated.
256 devices in a mesh: seq: 32 (over x, y, core), head: 8 (over z).
Axes of the slice: x: 4, y: 4, z: 8, core: 2. Of those that a mesh axis runs over, the one named last changes fastest.
Arguments:
- tokens: bfloat16 [32768, 2048], P('seq', 'head'), may hold values from -6 to 6
- seg_ids: int32 [32768], replicated, may hold values from 0 to 31, never falling along the last dimension, each value on 1 to 16384 neighbouring positions
- w_gate: bfloat16 [2048, 4096], P(None, 'head'), may hold values from -0.125 to 0.125
- w_x: bfloat16 [2048, 4096], P(None, 'head'), may hold values from -0.125 to 0.125
- w_bc: bfloat16 [2048, 256], replicated, may hold values from -0.125 to 0.125
- w_dt: bfloat16 [2048, 64], P(None, 'head'), may hold values from -0.125 to 0.125
- conv_x: float32 [4, 4096], P(None, 'head'), may hold values from -3 to 3
- conv_bc: float32 [4, 256], replicated, may hold values from -3 to 3
- conv_x_bias: float32 [4096], P('head'), may hold values from -3 to 3
- conv_bc_bias: float32 [256], replicated, may hold values from -3 to 3
- dt_bias: float32 [64], P('head'), may hold values from -4 to -1
- decay_rate: float32 [64], P('head'), may hold values from 0.0002 to 4
- skip_gain: float32 [64], P('head'), may hold values from 0.5 to 1.5
- norm_gain: float32 [4096], P('head'), may hold values from 0.5 to 1.5
- w_out: bfloat16 [4096, 2048], P('head'), may hold values from -0.125 to 0.125
Outputs:
- mixed: bfloat16 [32768, 2048], P('seq', 'head')
- end_state: float32 [32, 64, 64, 128], P('seq', 'head')
Inputs may be any that keep to these rules, and one draw needn't show every extreme that they name: `seg_ids`: prompt numbers never fall along the tokens; each prompt holds 1 to 16384 tokens, one of them exactly 16384.
All inputs are finite; a program needn't handle non-finite values.
Results may differ from a plain program's by a relative error of at most 0.0075.
Values may be sent and summed in bfloat16 or wider, within the bound.
A program may use at most 128 MiB of HBM per device.

v0:
```python
import jax
import jax.numpy as jnp
from jax import lax
from jax.sharding import PartitionSpec as P

GROUP = 256
INNER = 4096


EPSILON = 1e-05
HIGH = lax.Precision.HIGHEST


def shifted(x, axis, by):
    devices = lax.axis_size(axis)
    pairs = [(i, i + by) for i in range(devices) if 0 <= i + by < devices]
    return lax.ppermute(x, axis, pairs)


def carried_in(part, axis, combine, identity):
    place = lax.axis_index(axis)
    gathered = jax.tree.map(lambda a: lax.all_gather(a, axis), part)
    state = jax.tree.map(lambda a, e: jnp.zeros_like(a) + jnp.asarray(e, a.dtype), part, identity)

    def one(hop, state):
        return combine(
            state, jax.tree.map(lambda a: lax.dynamic_index_in_dim(a, hop, 0, False), gathered)
        )

    return lax.fori_loop(0, place, one, state)


def conv_block(projected, edge_rows, weights, offsets, idents, earlier):
    rows_here = projected.shape[0]
    lag_count = edge_rows.shape[0]
    joined = jnp.concatenate([edge_rows, projected], 0).astype(jnp.float32)
    joined_ids = jnp.concatenate([earlier, idents], 0)
    result = joined[lag_count:] * weights[0]
    for shift_by in range(1, lag_count + 1):
        window = joined[lag_count - shift_by : lag_count - shift_by + rows_here]
        matches = joined_ids[lag_count - shift_by : lag_count - shift_by + rows_here] == idents
        result = result + jnp.where(matches[:, None], window, 0.0) * weights[shift_by]
    return result + offsets


def combine(earlier, later):
    return (earlier[0] * later[0], later[0][:, None, None] * earlier[1] + later[1])


def shards(
    tokens,
    seg_ids,
    w_gate,
    w_x,
    w_bc,
    w_dt,
    conv_x,
    conv_bc,
    conv_x_bias,
    conv_bc_bias,
    dt_bias,
    decay_rate,
    skip_gain,
    norm_gain,
    w_out,
):
    rows_here = tokens.shape[0]
    heads_here = w_dt.shape[1]
    inner_here = w_x.shape[1]
    head_width = inner_here // heads_here
    state_width = w_bc.shape[1] // 2
    lag_count = conv_x.shape[0] - 1
    device = lax.axis_index("seq")
    first_row = device * rows_here
    piece = lax.all_gather(tokens, "head", axis=1, tiled=True)

    def partial_product(matrix):
        return jnp.dot(piece, matrix, preferred_element_type=jnp.float32)

    gate_full = partial_product(w_gate)
    x_sum = partial_product(w_x)
    bc_sum = partial_product(w_bc)
    dt_raw = partial_product(w_dt)
    x_pre = x_sum.astype(jnp.bfloat16)
    bc_pre = bc_sum.astype(jnp.bfloat16)
    idents = lax.dynamic_slice_in_dim(seg_ids, first_row, rows_here)
    earlier = lax.dynamic_slice_in_dim(seg_ids, jnp.maximum(first_row - lag_count, 0), lag_count)
    earlier = jnp.where(device > 0, earlier, -1)
    edge_x, edge_bc = shifted(
        (x_pre[rows_here - lag_count :], bc_pre[rows_here - lag_count :]), "seq", 1
    )
    x_conv = jax.nn.silu(conv_block(x_pre, edge_x, conv_x, conv_x_bias, idents, earlier)).astype(
        jnp.bfloat16
    )
    bc_conv = jax.nn.silu(
        conv_block(bc_pre, edge_bc, conv_bc, conv_bc_bias, idents, earlier)
    ).astype(jnp.bfloat16)
    steps_dt = jax.nn.softplus(dt_raw + dt_bias)
    log_decay = -steps_dt * decay_rate
    x_float = x_conv.astype(jnp.float32).reshape(rows_here, heads_here, head_width)
    x_scaled = x_float * steps_dt[:, :, None]
    count = rows_here // GROUP
    group_x = x_scaled.reshape(count, GROUP, heads_here, head_width)
    group_b = bc_conv[:, :state_width].astype(jnp.float32).reshape(count, GROUP, state_width)
    group_c = bc_conv[:, state_width:].astype(jnp.float32).reshape(count, GROUP, state_width)
    group_ids = idents.reshape(count, GROUP)
    cumul = jnp.cumsum(log_decay.reshape(count, GROUP, heads_here), axis=1)
    cumul_heads = jnp.transpose(cumul, (0, 2, 1))
    places = jnp.arange(GROUP)
    causal = places[None, :] <= places[:, None]
    linked = causal[None] & (group_ids[:, :, None] == group_ids[:, None, :])
    gaps = cumul_heads[:, :, :, None] - cumul_heads[:, :, None, :]
    link_heads = linked[:, None, :, :]
    decays = jnp.where(link_heads, jnp.exp(jnp.where(link_heads, gaps, 0.0)), 0.0)
    scores = jnp.einsum("ctn,csn->cts", group_c, group_b, precision=HIGH)
    within = jnp.einsum("chts,cshp->cthp", decays * scores[:, None, :, :], group_x, precision=HIGH)
    last_ids = group_ids[:, -1]
    tails = jnp.where(
        (group_ids == last_ids[:, None])[:, :, None], jnp.exp(cumul[:, -1:, :] - cumul), 0.0
    )
    group_states = jnp.einsum(
        "cshp,csn->chpn", group_x * tails[:, :, :, None], group_b, precision=HIGH
    )
    prior_ids = jnp.concatenate([earlier[-1:], last_ids[:-1]], 0)
    passing = jnp.where((last_ids == prior_ids)[:, None], jnp.exp(cumul[:, -1, :]), 0.0)
    local_list = []
    gain_list = []
    running_state = jnp.zeros((heads_here, head_width, state_width), jnp.float32)
    running_gain = jnp.ones((heads_here,), jnp.float32)
    for group_no in range(count):
        local_list.append(running_state)
        gain_list.append(running_gain)
        running_state = passing[group_no][:, None, None] * running_state + group_states[group_no]
        running_gain = passing[group_no] * running_gain
    identity = (jnp.ones_like(running_gain), jnp.zeros_like(running_state))
    prefix_gain, incoming = carried_in((running_gain, running_state), "seq", combine, identity)
    entering = jnp.stack(gain_list, 0)[:, :, None, None] * incoming[None] + jnp.stack(local_list, 0)
    enter_weight = jnp.where((group_ids == prior_ids[:, None])[:, :, None], jnp.exp(cumul), 0.0)
    carried = (
        jnp.einsum("ctn,chpn->cthp", group_c, entering, precision=HIGH)
        * enter_weight[:, :, :, None]
    )
    end_state = (running_gain[:, None, None] * incoming + running_state)[None]
    ssd_out = (within + carried).reshape(rows_here, heads_here, head_width) + skip_gain[
        None, :, None
    ] * x_float
    gated = ssd_out.reshape(rows_here, inner_here) * jax.nn.silu(gate_full)
    square_total = lax.psum(jnp.sum(gated * gated, axis=1), "head")
    mean_square = (square_total / INNER)[:, None]
    hidden = (gated * lax.rsqrt(mean_square + EPSILON) * norm_gain).astype(jnp.bfloat16)
    partial_out = jnp.dot(hidden, w_out, preferred_element_type=jnp.float32)
    mixed = lax.psum_scatter(partial_out, "head", scatter_dimension=1, tiled=True).astype(
        jnp.bfloat16
    )
    return (mixed, end_state)


def solution(mesh):
    return jax.shard_map(
        shards,
        mesh=mesh,
        in_specs=(
            P("seq", "head"),
            P(),
            P(None, "head"),
            P(None, "head"),
            P(),
            P(None, "head"),
            P(None, "head"),
            P(),
            P("head"),
            P(),
            P("head"),
            P("head"),
            P("head"),
            P("head"),
            P("head", None),
        ),
        out_specs=(P("seq", "head"), P("seq", "head", None, None)),
        check_vma=False,
    )
```

profile of v0, /device:TPU:1, one launch (start us, length us, event | category | flops | bytes accessed | tf_op | source)
XLA Modules:
  0.0 347.8 jit_solution(15108138510818791325)
XLA Ops:
  7.2 0.7 all-gather.4.cloned.1.call-update
  8.0 0.7 dynamic_slice.17
  8.7 0.8 broadcast_select_fusion
  9.4 0.6 slice.151
  10.0 0.2 fusion.60
  10.2 0.7 pad_add_fusion.1
  10.9 0.2 slice_reduce_fusion.1
  11.1 0.8 fusion.53
  12.1 0.8 fusion.61
  12.9 0.9 fusion.59
  13.8 58.4 %all-gather.4.cloned.1.call-done = bf16[1024,2048]{1,0:T(8,128)(2,1)} async-done(((bf16[1024,256]{1,0:T(8,128)(2,1)}), bf16[1024,2048]{1,0:T(8,128)(2,1)}) %all-gather.4.cloned.1.call-update) | async-done | bytes 4194320 | tf_op jit(solution)/shard_map/all_gather | solution.py:75
  72.3 3.9 %convolution_convert_fusion.1 = bf16[1024,256]{1,0:T(8,128)(2,1)S(1)} fusion(bf16[1024,2048]{1,0:T(8,128)(2,1)} %all-gather.4.cloned.1.call-done, bf16[2048,256]{1,0:T(8,128)(2,1)} %param.21), kind=kOutput, calls=%fused_computation.33 | convolution fusion | flops 1074003968 | bytes 5767168 | tf_op jit(solution)/shard_map/dot_general | solution.py:78
  76.2 7.4 %collective-permute-start.1 = (bf16[3,256]{1,0:T(4,128)(2,1)S(1)}, bf16[3,256]{1,0:T(4,128)(2,1)S(1)}, u32[]{:S(2)}, u32[]{:S(2)}) collective-permute-start(bf16[3,256]{1,0:T(4,128)(2,1)S(1)} %slice.175), channel_id=1, source_target_pairs={{0,8},{8,16},{16,24},{24,32},{32,40},{40,48},{48,56},{56,64},{64,7... | collective-permute-start | bytes 4616 | tf_op jit(solution)/shard_map/ppermute | solution.py:17
  83.6 1.2 negate_multiply_fusion
  84.8 2.3 reduce-window.6
  87.2 0.1 copy.66
  87.3 0.1 exponential_select_fusion
  87.4 0.2 slice_reduce_fusion
  87.6 0.1 exponential_select_fusion.1
  87.7 5.2 %convolution_convert_fusion = bf16[1024,512]{1,0:T(8,128)(2,1)S(1)} fusion(bf16[1024,2048]{1,0:T(8,128)(2,1)} %all-gather.4.cloned.1.call-done, bf16[2048,512]{1,0:T(8,128)(2,1)} %param.20), kind=kOutput, calls=%fused_computation.32 | convolution fusion | flops 2148007936 | bytes 7340032 | tf_op jit(solution)/shard_map/dot_general | solution.py:78
  93.0 1.9 collective-permute-start
  95.0 0.1 maximum_convert_fusion.1
  95.1 1.3 multiply_convert_fusion.3
  96.4 0.7 fusion.58
  97.2 0.3 maximum_convert_fusion
  97.5 3.1 fusion.37
  100.7 2.9 copy.64
  103.6 3.2 reshape.162
  106.8 3.8 %broadcast_multiply_fusion = (f32[4,256,8,64]{1,0,3,2:T(4,128)S(1)}, f32[4,256,8,64]{1,0,3,2:T(4,128)}) fusion(f32[4,256,8]{1,0,2:T(4,128)S(1)} %copy.69, f32[4,256,8,64]{1,0,3,2:T(4,128)} %reshape.162, f32[4,256,8]{1,0,2:T(4,128)S(1)} %copy.65), kind=kLoop, calls=%fused_computation.57 | loop fusion | flops 1048576 | bytes 6356992 | tf_op jit(solution)/shard_map/mul | solution.py:122
  110.6 1.3 fusion.18
  111.9 1.1 multiply_add_fusion
  113.1 0.1 mul.359
  113.2 0.2 compare_and_fusion
  113.5 22.6 %all-gather = f32[32,1,8]{2,1,0:T(1,128)S(1)} all-gather(f32[1,1,8]{2,1,0:T(1,128)S(1)} %get-tuple-element.93), channel_id=1, replica_groups=mesh['seq'=32,'head'=8] {'seq'}, dimensions={0}, use_global_device_ids=true | all-gather | bytes 1056 | tf_op jit(solution)/shard_map/all_gather | solution.py:22
  136.3 1.2 fusion.63
  137.5 12.0 %fusion = f32[4,8,64,256]{3,2,1,0:T(8,128)} fusion(f32[4,256,256]{2,1,0:T(8,128)S(1)} %fusion.63, f32[4,8,256]{2,1,0:T(8,128)S(1)} %add_bitcast_fusion.1, pred[4,256,256]{2,1,0:T(8,128)(4,1)S(1)} %compare_and_fusion, f32[4,256,8,64]{1,0,3,2:T(4,128)} %get-tuple-element.69), kind=kOutput, calls=%fused_computation.2 | convolution fusion | flops 1619001344 | bytes 5537792 | tf_op jit(solution)/shard_map/chts,cshp->cthp/dot_general | solution.py:116
  149.6 20.0 %all-gather.6.cloned.1.call-done = f32[32,8,64,128]{3,2,1,0:T(8,128)} async-done(((f32[1,8,64,128]{3,2,1,0:T(8,128)}), f32[32,8,64,128]{3,2,1,0:T(8,128)}) %all-gather.6.cloned.1.call-update) | async-done | bytes 8388624 | tf_op jit(solution)/shard_map/all_gather | solution.py:22
  169.6 1.1 while.12
  169.6 1.1 bitcast_add_fusion.7
  170.7 4.3 %bitcast_add_fusion.1 = f32[4,256,8,64]{1,3,2,0:T(8,128)} fusion(f32[4,8,64,256]{3,2,1,0:T(8,128)} %fusion, bf16[4,256,128,1]{2,1,3,0:T(8,128)(2,1)} %bitcast.114, f32[1,8,64,128]{3,2,1,0:T(8,128)} %get-tuple-element.60, f32[1,8,64,128]{3,2,1,0:T(8,128)} %get-tuple-element.61, f32[1,8,64,128]{3,2,1,0:T(8,128)} %get-tuple-element.62, ...), kind=kOutput, calls=%fused_computation.24 | convolution fusion | flops 807665664 | bytes 5537936 | tf_op jit(solution)/shard_map/ctn,chpn->cthp/dot_general | solution.py:140
  175.0 3.8 %copy.78 = f32[4,256,8,64]{3,2,1,0:T(8,128)} copy(f32[4,256,8,64]{1,3,2,0:T(8,128)} %bitcast_add_fusion.1) | data formatting | bytes 4194304 | tf_op jit(solution)/shard_map/reshape | solution.py:144
  178.8 4.8 %reshape.173 = f32[1024,512]{1,0:T(8,128)} reshape(f32[4,256,8,64]{3,2,1,0:T(8,128)} %copy.78) | data formatting | bytes 4194304 | tf_op jit(solution)/shard_map/reshape | solution.py:144
  183.6 8.1 %multiply_reduce_fusion = (f32[1024]{0:T(1024)S(1)}, f32[1024,512]{1,0:T(8,128)}) fusion(f32[1024,512]{1,0:T(8,128)} %reshape.173, f32[1024,512]{1,0:T(8,128)} %fusion.37, f32[512]{0:T(512)S(1)} %mul.359, bf16[1024,2048]{1,0:T(8,128)(2,1)} %all-gather.4.cloned.1.call-done, bf16[2048,512]{1,0:T(8,128)(2,1)} %param.19), kind=kOutput, calls=%fused_computation.29 | convolution fusion | flops 2152201216 | bytes 12589056 | tf_op jit(solution)/shard_map/dot_general | solution.py:78
  191.7 13.7 %psum.7 = f32[1024]{0:T(1024)S(1)} all-reduce(f32[1024]{0:T(1024)S(1)} %get-tuple-element.57), channel_id=1, replica_groups=mesh['seq'=32,'head'=8] {'head'}, use_global_device_ids=true, to_apply=%region_5.6 | all-reduce | flops 1024 | bytes 8192 | tf_op jit(solution)/shard_map/psum | solution.py:148
  205.4 7.2 %fusion.21 = f32[1024,2048]{1,0:T(8,128)} fusion(bf16[512,2048]{1,0:T(8,128)(2,1)S(1)} %copy-done, f32[1024,512]{1,0:T(8,128)} %get-tuple-element.58, f32[512]{0:T(512)S(1)} %copy-done.3, f32[1024]{0:T(1024)S(1)} %add_rsqrt_fusion), kind=kOutput, calls=%fused_computation.36 | convolution fusion | flops 2149056512 | bytes 12589056 | tf_op jit(solution)/shard_map/dot_general | solution.py:151
  212.7 0.9 fusion.42
  213.5 125.7 %reduce-scatter.2.cloned.1.call-done = f32[1024,256]{1,0:T(8,128)} async-done(((f32[1024,2048]{1,0:T(8,128)}), f32[1024,256]{1,0:T(8,128)}) %reduce-scatter.2.cloned.1.call-update) | async-done | bytes 1048592 | tf_op jit(solution)/shard_map/reduce_scatter | solution.py:152
  339.2 2.1 convert_element_type.37
  (48 shorter events, 0.9 us)
Async XLA Ops:
  7.2 198.2 %copy-start = (bf16[512,2048]{1,0:T(8,128)(2,1)S(1)}, bf16[512,2048]{1,0:T(8,128)(2,1)}, u32[]{:S(2)}) copy-start(bf16[512,2048]{1,0:T(8,128)(2,1)} %param.31) | copy-start | bytes 6291460
  7.2 65.1 %all-gather.4.cloned.1.call-start = ((), (), s32[]{:S(2)}) async-start(), calls=%async_computation.1 | async-start | bytes 4718592 | tf_op jit(solution)/shard_map/all_gather | solution.py:75
  7.9 161.6 %all-gather.6.cloned.1.call-start = ((), (), s32[]{:S(2)}) async-start(), calls=%async_computation.2 | async-start | bytes 8650752 | tf_op jit(solution)/shard_map/all_gather | solution.py:22
  13.8 69.8 %copy-start.2 = (bf16[2048,8]{0,1:T(8,128)(2,1)S(1)}, bf16[2048,8]{0,1:T(8,128)(2,1)}, u32[]{:S(2)}) copy-start(bf16[2048,8]{0,1:T(8,128)(2,1)} %param.22) | copy-start | bytes 98308
  13.8 69.8 %copy-start.5 = (f32[8]{0:T(128)S(1)}, f32[8]{0:T(128)}, u32[]{:S(2)}) copy-start(f32[8]{0:T(128)} %param.28) | copy-start | bytes 100
  13.8 69.8 %copy-start.6 = (f32[8]{0:T(128)S(1)}, f32[8]{0:T(128)}, u32[]{:S(2)}) copy-start(f32[8]{0:T(128)} %param.27) | copy-start | bytes 100
  72.3 11.3 %copy-start.1 = (bf16[1024,2048]{1,0:T(8,128)(2,1)S(1)}, bf16[1024,2048]{1,0:T(8,128)(2,1)}, u32[]{:S(2)}) copy-start(bf16[1024,2048]{1,0:T(8,128)(2,1)} %all-gather.4.cloned.1.call-done) | copy-start | bytes 12582916
  76.2 18.8 %collective-permute-start.1 = (bf16[3,256]{1,0:T(4,128)(2,1)S(1)}, bf16[3,256]{1,0:T(4,128)(2,1)S(1)}, u32[]{:S(2)}, u32[]{:S(2)}) collective-permute-start(bf16[3,256]{1,0:T(4,128)(2,1)S(1)} %slice.175), channel_id=1, source_target_pairs={{0,8},{8,16},{16,24},{24,32},{32,40},{40,48},{48,56},{56,64},{64,7... | collective-permute-start | bytes 4616 | tf_op jit(solution)/shard_map/ppermute | solution.py:17
  87.7 7.3 %copy-start.7 = (f32[256]{0:T(256)S(1)}, f32[256]{0:T(256)}, u32[]{:S(2)}) copy-start(f32[256]{0:T(256)} %param.26) | copy-start | bytes 3076
  93.0 4.2 %collective-permute-start = (bf16[3,512]{1,0:T(4,128)(2,1)S(1)}, bf16[3,512]{1,0:T(4,128)(2,1)S(1)}, u32[]{:S(2)}, u32[]{:S(2)}) collective-permute-start(bf16[3,512]{1,0:T(4,128)(2,1)S(1)} %slice.164), channel_id=1, source_target_pairs={{0,8},{8,16},{16,24},{24,32},{32,40},{40,48},{48,56},{56,64},{64,7... | collective-permute-start | bytes 9224 | tf_op jit(solution)/shard_map/ppermute | solution.py:17
  96.4 1.1 copy-start.4
  110.6 2.4 copy-start.8
  112.9 226.3 %reduce-scatter.2.cloned.1.call-start = ((), (), s32[]{:S(2)}) async-start(), calls=%async_computation.3 | async-start | bytes 9437184 | tf_op jit(solution)/shard_map/reduce_scatter | solution.py:152
  183.6 21.8 %copy-start.3 = (f32[512]{0:T(512)S(1)}, f32[512]{0:T(512)}, u32[]{:S(2)}) copy-start(f32[512]{0:T(512)} %param.30) | copy-start | bytes 6148
Sparse Core Ops, SparseCore 0:
  9.7 62.5 all-gather.3
  113.1 56.4 all-gather.5
  212.8 126.4 reduce-scatter.1
where the time goes:
time: 349 us; the launch traced here: 348 us
  waiting for transfers between devices  205 us (59%)
  matrix products  44.5 us (13%)
  blocking collectives  36.3 us (10%)
  local copies, waits for them, and re-layouts  19.5 us (6%)
  other arithmetic  19.2 us (6%)
  between operations  14.1 us (4%)
  starting transfers between devices  9.41 us (3%)
    reduce_scatter x1, waiting for transfers between devices, shards(): lax.psum_scatter(partial_out, 'head', scatter_dimension=1, tiled=True)  126 us
    all_gather x1, waiting for transfers between devices, shards(): piece = lax.all_gather(tokens, 'head', axis=1, tiled=True)  58.4 us
    all_gather x1, blocking collectives, carried_in(): gathered = jax.tree.map(lambda a: lax.all_gather(a, axis), part)  22.6 us
    all_gather x1, waiting for transfers between devices, carried_in(): gathered = jax.tree.map(lambda a: lax.all_gather(a, axis), part)  20 us
    dot_general x4, matrix products, partial_product(): return jnp.dot(piece, matrix, preferred_element_type=jnp.float32)  18.4 us
    psum x1, blocking collectives, shards(): square_total = lax.psum(jnp.sum(gated * gated, axis=1), 'head')  13.7 us
    dot_general x1, matrix products, shards(): jnp.einsum('chts,cshp->cthp', decays * scores[:, None, :, :], group_x, pr...  12 us
    ppermute x2, starting transfers between devices, shifted(): return lax.ppermute(x, axis, pairs)  9.29 us
  transfers between devices with their start and end apart: 5, of which 3 were waited for; matrix products, arithmetic and copies ran while one was open for 9% of the time, Pallas kernels for 0%

commit v1 on v0

--- a/solution.py
+++ b/solution.py
@@ -132,8 +132,17 @@
         gain_list.append(running_gain)
         running_state = passing[group_no][:, None, None] * running_state + group_states[group_no]
         running_gain = passing[group_no] * running_gain
-    identity = (jnp.ones_like(running_gain), jnp.zeros_like(running_state))
-    prefix_gain, incoming = carried_in((running_gain, running_state), "seq", combine, identity)
+    blocks_n = lax.axis_size("seq")
+    gain_row = jnp.broadcast_to(running_gain[:, None, None], (heads_here, 1, state_width))
+    packed = jnp.concatenate([running_state, gain_row], 1)[None]
+    gathered = lax.all_gather(packed, "seq", tiled=True)
+    all_states = gathered[:, :, :head_width]
+    all_gains = gathered[:, :, head_width, 0]
+    order = jnp.arange(blocks_n)
+    between = (order[:, None] < order[None, :]) & (order[None, :] < device)
+    factors = jnp.where(between[:, :, None], all_gains[None, :, :], 1.0)
+    weights = jnp.where((order < device)[:, None], jnp.prod(factors, axis=1), 0.0)
+    incoming = jnp.einsum("ih,ihpn->hpn", weights, all_states, precision=HIGH)
     entering = jnp.stack(gain_list, 0)[:, :, None, None] * incoming[None] + jnp.stack(local_list, 0)
     enter_weight = jnp.where((group_ids == prior_ids[:, None])[:, :, None], jnp.exp(cumul), 0.0)
     carried = (
@@ -145,13 +154,17 @@
         None, :, None
     ] * x_float
     gated = ssd_out.reshape(rows_here, inner_here) * jax.nn.silu(gate_full)
-    square_total = lax.psum(jnp.sum(gated * gated, axis=1), "head")
-    mean_square = (square_total / INNER)[:, None]
-    hidden = (gated * lax.rsqrt(mean_square + EPSILON) * norm_gain).astype(jnp.bfloat16)
-    partial_out = jnp.dot(hidden, w_out, preferred_element_type=jnp.float32)
-    mixed = lax.psum_scatter(partial_out, "head", scatter_dimension=1, tiled=True).astype(
-        jnp.bfloat16
-    )
+    heads_n = lax.axis_size("head")
+    scaled = (gated * norm_gain).astype(jnp.bfloat16)
+    partial_out = jnp.dot(scaled, w_out, preferred_element_type=jnp.float32)
+    cols = partial_out.shape[1] // heads_n
+    square_rows = jnp.sum(gated * gated, axis=1).reshape(-1, cols)
+    joined = jnp.concatenate([partial_out, jnp.tile(square_rows, (1, heads_n))], 0)
+    summed = lax.psum_scatter(
+        joined.astype(jnp.bfloat16), "head", scatter_dimension=1, tiled=True
+    ).astype(jnp.float32)
+    mean_square = (summed[rows_here:].reshape(rows_here) / INNER)[:, None]
+    mixed = (summed[:rows_here] * lax.rsqrt(mean_square + EPSILON)).astype(jnp.bfloat16)
     return (mixed, end_state)
 
 

time: 349 us -> 283 us (0.81)
  waiting for transfers between devices: 205 us -> 162 us
  blocking collectives: 36.3 us -> 0 us
  local copies, waits for them, and re-layouts: 19.5 us -> 29 us
    reduce_scatter x1, waiting for transfers between devices: 126 us -> 54.5 us  [shards(): lax.psum_scatter(joined.astype(jnp.bfloat16), 'head', scatter_dimension=1...]
    all_gather x1, waiting for transfers between devices: 20 us -> 48.6 us  [shards(): gathered = lax.all_gather(packed, 'seq', tiled=True)]
    all_gather x1 -> x0, blocking collectives: 22.6 us -> none  [carried_in(): gathered = jax.tree.map(lambda a: lax.all_gather(a, axis), part)]
    psum x1 -> x0, blocking collectives: 13.7 us -> none  [shards(): square_total = lax.psum(jnp.sum(gated * gated, axis=1), 'head')]
    slice x2 -> x5, local copies, waits for them, and re-layouts: 0.19 us -> 8.84 us  [the longest x1 7.61 us: shards(): all_states = gathered[:, :, :head_width]]
    dot_general x1 -> x2, matrix products: 7.22 us -> 12.8 us  [the longest x1 8.89 us: shards(): incoming = jnp.einsum('ih,ihpn->hpn', weights, all_states, precision=HIGH)]
where the time goes in v1:
time: 283 us
  waiting for transfers between devices  162 us (57%)
  matrix products  46.3 us (16%)
  local copies, waits for them, and re-layouts  29 us (10%)
  other arithmetic  21.4 us (8%)
  between operations  14.2 us (5%)
  starting transfers between devices  9.6 us (3%)
    all_gather x1, waiting for transfers between devices, shards(): piece = lax.all_gather(tokens, 'head', axis=1, tiled=True)  58.5 us
    reduce_scatter x1, waiting for transfers between devices, shards(): lax.psum_scatter(joined.astype(jnp.bfloat16), 'head', scatter_dimension=1...  54.5 us
    all_gather x1, waiting for transfers between devices, shards(): gathered = lax.all_gather(packed, 'seq', tiled=True)  48.6 us
    dot_general x4, matrix products, partial_product(): return jnp.dot(piece, matrix, preferred_element_type=jnp.float32)  17.5 us
    dot_general x1, matrix products, shards(): jnp.einsum('chts,cshp->cthp', decays * scores[:, None, :, :], group_x, pr...  10.9 us
    ppermute x2, starting transfers between devices, shifted(): return lax.ppermute(x, axis, pairs)  9.3 us
    dot_general x1, matrix products, shards(): incoming = jnp.einsum('ih,ihpn->hpn', weights, all_states, precision=HIGH)  8.89 us
    reshape x2, local copies, waits for them, and re-layouts, shards(): (within + carried).reshape(rows_here, heads_here, head_width)  8.6 us
  transfers between devices with their start and end apart: 5, of which 3 were waited for; matrix products, arithmetic and copies ran while one was open for 9% of the time, Pallas kernels for 0%

profile of v1, /device:TPU:1, one launch (start us, length us, event | category | flops | bytes accessed | tf_op | source)
XLA Modules:
  0.0 282.7 jit_solution(2669317643063796817)
XLA Ops:
  7.2 0.7 all-gather.4.cloned.1.call-update
  8.0 0.7 dynamic_slice.7
  8.7 0.8 broadcast_select_fusion
  9.4 0.6 slice.163
  10.0 0.2 fusion.64
  10.2 0.7 pad_add_fusion.1
  10.9 0.2 slice_reduce_fusion.1
  11.1 0.8 fusion.57
  12.1 0.8 fusion.65
  12.9 0.9 fusion.63
  13.8 58.5 %all-gather.4.cloned.1.call-done = bf16[1024,2048]{1,0:T(8,128)(2,1)} async-done(((bf16[1024,256]{1,0:T(8,128)(2,1)}), bf16[1024,2048]{1,0:T(8,128)(2,1)}) %all-gather.4.cloned.1.call-update) | async-done | bytes 4194320 | tf_op jit(solution)/shard_map/all_gather | solution.py:75
  72.3 3.4 %negate_multiply_fusion = (f32[1024,8]{0,1:T(8,128)S(1)}, f32[1024,8]{0,1:T(8,128)S(1)}) fusion(f32[8]{0:T(128)} %param.26, f32[8]{0:T(128)} %param.25, bf16[1024,2048]{1,0:T(8,128)(2,1)} %all-gather.4.cloned.1.call-done, bf16[2048,8]{0,1:T(8,128)(2,1)} %param.20), kind=kOutput, calls=%fused_computation.86 | convolution fusion | flops 33628160 | bytes 4292672 | tf_op jit(solution)/shard_map/dot_general | solution.py:78
  75.7 2.3 reduce-window.6
  78.3 0.2 slice_reduce_fusion
  78.5 3.6 %convolution_convert_fusion.2 = bf16[1024,256]{1,0:T(8,128)(2,1)S(1)} fusion(bf16[1024,2048]{1,0:T(8,128)(2,1)} %all-gather.4.cloned.1.call-done, bf16[2048,256]{1,0:T(8,128)(2,1)S(1)} %copy-done.12), kind=kOutput, calls=%fused_computation.35 | convolution fusion | flops 1074003968 | bytes 5767168 | tf_op jit(solution)/shard_map/dot_general | solution.py:78
  82.1 7.4 %collective-permute-start.1 = (bf16[3,256]{1,0:T(4,128)(2,1)S(1)}, bf16[3,256]{1,0:T(4,128)(2,1)S(1)}, u32[]{:S(2)}, u32[]{:S(2)}) collective-permute-start(bf16[3,256]{1,0:T(4,128)(2,1)S(1)} %slice.191), channel_id=1, source_target_pairs={{0,8},{8,16},{16,24},{24,32},{32,40},{40,48},{48,56},{56,64},{64,7... | collective-permute-start | bytes 4616 | tf_op jit(solution)/shard_map/ppermute | solution.py:17
  89.7 2.3 convolution_convert_fusion.1
  92.0 1.9 collective-permute-start
  94.1 1.3 multiply_convert_fusion.3
  95.5 0.7 fusion.62
  96.2 0.3 maximum_convert_fusion
  96.6 3.2 %fusion.38 = f32[1024,512]{1,0:T(8,128)} fusion(f32[512]{0:T(512)S(1)} %copy-done.8, f32[512]{0:T(512)S(1)} %bitcast.134, f32[1027,512]{1,0:T(8,128)S(1)} %maximum_convert_fusion, pred[1024]{0:T(1024)(128)(4,1)S(1)} %get-tuple-element.20, f32[512]{0:T(512)S(1)} %bitcast.135, pred[1024]{0:T(1024)(128)(4,1)S(1)} %get-tuple-element.21, f32[512]{0:T(512)S(1)} %bitcast.133, ...), kind=kLoop, calls=%fused_computation.63 | loop fusion | flops 8912896 | bytes 10499072 | tf_op jit(solution)/shard_map/convert_element_type | solution.py:100
  99.7 2.9 %copy.86 = f32[1024,512]{0,1:T(8,128)} copy(f32[1024,512]{1,0:T(8,128)} %fusion.38) | data formatting | bytes 4194304 | tf_op jit(solution)/shard_map/convert_element_type | solution.py:100
  102.6 3.2 %reshape.206 = f32[4,256,8,64]{1,0,3,2:T(4,128)} reshape(f32[1024,512]{0,1:T(8,128)} %copy.86) | data formatting | bytes 4194304 | tf_op jit(solution)/shard_map/reshape | solution.py:100
  105.8 3.8 %broadcast_multiply_fusion = (f32[4,256,8,64]{1,0,3,2:T(4,128)S(1)}, f32[4,256,8,64]{1,0,3,2:T(4,128)}) fusion(f32[4,256,8]{1,0,2:T(4,128)S(1)} %copy.91, f32[4,256,8,64]{1,0,3,2:T(4,128)} %reshape.206, f32[4,256,8]{1,0,2:T(4,128)S(1)} %copy.87), kind=kLoop, calls=%fused_computation.59 | loop fusion | flops 1048576 | bytes 6356992 | tf_op jit(solution)/shard_map/mul | solution.py:122
  109.6 1.3 fusion.20
  110.9 0.1 fusion.42
  111.1 0.8 copy.93
  111.9 0.2 reduce-scatter.2.cloned.1.call-start
  112.4 0.2 compare_and_fusion
  112.8 1.4 fusion.67
  114.2 1.0 multiply_add_fusion
  115.3 10.9 %fusion.2 = f32[4,8,64,256]{3,2,1,0:T(8,128)} fusion(f32[4,256,256]{2,1,0:T(8,128)S(1)} %fusion.67, f32[4,8,256]{2,1,0:T(8,128)S(1)} %add_bitcast_fusion.2, pred[4,256,256]{2,1,0:T(8,128)(4,1)S(1)} %compare_and_fusion, f32[4,256,8,64]{1,0,3,2:T(4,128)S(1)} %copy-done.3), kind=kOutput, calls=%fused_computation.2 | convolution fusion | flops 1619001344 | bytes 5537792 | tf_op jit(solution)/shard_map/chts,cshp->cthp/dot_general | solution.py:116
  126.1 48.6 %all-gather.6.cloned.1.call-done = f32[256,65,128]{2,0,1:T(8,128)} async-done(((f32[8,65,128]{2,0,1:T(8,128)}), f32[256,65,128]{2,0,1:T(8,128)}) %all-gather.6.cloned.1.call-update) | async-done | bytes 8519696 | tf_op jit(solution)/shard_map/all_gather | solution.py:138
  174.8 7.6 %slice.206 = f32[32,8,64,128]{3,1,0,2:T(8,128)} slice(f32[32,8,65,128]{3,1,0,2:T(8,128)} %bitcast.119), slice={[0:32], [0:8], [0:64], [0:128]} | slice | bytes 16777216 | tf_op jit(solution)/shard_map/slice | solution.py:139
  182.4 0.9 slice.205
  183.4 0.6 select_reduce_fusion
  184.2 8.9 %fusion = f32[8,1,64,128]{3,1,2,0:T(1,128)S(1)} fusion(f32[32,8,1,1]{0,2,3,1:T(1,128)S(1)} %copy.100, f32[32,8,64,128]{3,1,0,2:T(8,128)} %slice.206), kind=kOutput, calls=%fused_computation | convolution fusion | flops 25165824 | bytes 8651776 | tf_op jit(solution)/shard_map/ih,ihpn->hpn/dot_general | solution.py:145
  193.2 2.5 bitcast_add_fusion
  195.7 3.8 %copy.105 = f32[4,256,8,64]{3,2,1,0:T(8,128)} copy(f32[4,256,8,64]{1,3,2,0:T(8,128)} %bitcast_add_fusion) | data formatting | bytes 4194304 | tf_op jit(solution)/shard_map/reshape | solution.py:153
  199.5 4.8 %reshape.219 = f32[1024,512]{1,0:T(8,128)} reshape(f32[4,256,8,64]{3,2,1,0:T(8,128)} %copy.105) | data formatting | bytes 4194304 | tf_op jit(solution)/shard_map/reshape | solution.py:153
  204.3 8.1 %multiply_reduce_fusion = (bf16[1024]{0:T(1024)(128)(2,1)S(1)}, f32[1024,512]{1,0:T(8,128)}) fusion(f32[1024,512]{1,0:T(8,128)} %reshape.219, f32[1024,512]{1,0:T(8,128)} %fusion.38, f32[512]{0:T(512)S(1)} %mul.336, bf16[1024,2048]{1,0:T(8,128)(2,1)} %all-gather.4.cloned.1.call-done, bf16[2048,512]{1,0:T(8,128)(2,1)} %param.17), kind=kOutput, calls=%fused_computation.30 | convolution fusion | flops 2152201216 | bytes 12587008 | tf_op jit(solution)/shard_map/dot_general | solution.py:78
  212.5 3.9 %convolution_convert_fusion = bf16[1024,2048]{1,0:T(8,128)(2,1)S(1)} fusion(bf16[512,2048]{1,0:T(8,128)(2,1)S(1)} %copy-done, f32[1024,512]{1,0:T(8,128)} %get-tuple-element.3, f32[512]{0:T(512)S(1)} %copy-done.13), kind=kOutput, calls=%fused_computation.14 | convolution fusion | flops 2150629376 | bytes 8390656 | tf_op jit(solution)/shard_map/dot_general | solution.py:159
  216.4 2.3 pad_maximum_fusion
  218.7 0.9 add_bitcast_fusion
  219.6 54.5 %reduce-scatter.2.cloned.1.call-done = bf16[1028,256]{1,0:T(8,128)(2,1)} async-done(((bf16[1028,2048]{1,0:T(8,128)(2,1)}), bf16[1028,256]{1,0:T(8,128)(2,1)}) %reduce-scatter.2.cloned.1.call-update) | async-done | bytes 526352 | tf_op jit(solution)/shard_map/reduce_scatter | solution.py:163
  274.1 1.1 convert_element_type.41
  275.2 1.0 fusion.23
  (71 shorter events, 1.7 us)
Async XLA Ops:
  7.2 205.3 %copy-start = (bf16[512,2048]{1,0:T(8,128)(2,1)S(1)}, bf16[512,2048]{1,0:T(8,128)(2,1)}, u32[]{:S(2)}) copy-start(bf16[512,2048]{1,0:T(8,128)(2,1)} %param.29) | copy-start | bytes 6291460
  7.2 65.1 %all-gather.4.cloned.1.call-start = ((), (), s32[]{:S(2)}) async-start(), calls=%async_computation.1 | async-start | bytes 4718592 | tf_op jit(solution)/shard_map/all_gather | solution.py:75
  7.9 166.9 %all-gather.6.cloned.1.call-start = ((), (), s32[]{:S(2)}) async-start(), calls=%async_computation.3 | async-start | bytes 8785920 | tf_op jit(solution)/shard_map/all_gather | solution.py:138
  13.8 64.7 %copy-start.12 = (bf16[2048,256]{1,0:T(8,128)(2,1)S(1)}, bf16[2048,256]{1,0:T(8,128)(2,1)}, u32[]{:S(2)}) copy-start(bf16[2048,256]{1,0:T(8,128)(2,1)} %param.19) | copy-start | bytes 3145732
  78.5 11.2 %copy-start.1 = (bf16[1024,2048]{1,0:T(8,128)(2,1)S(1)}, bf16[1024,2048]{1,0:T(8,128)(2,1)}, u32[]{:S(2)}) copy-start(bf16[1024,2048]{1,0:T(8,128)(2,1)} %all-gather.4.cloned.1.call-done) | copy-start | bytes 12582916
  78.5 11.2 %copy-start.11 = (bf16[2048,512]{1,0:T(8,128)(2,1)S(1)}, bf16[2048,512]{1,0:T(8,128)(2,1)}, u32[]{:S(2)}) copy-start(bf16[2048,512]{1,0:T(8,128)(2,1)} %param.18) | copy-start | bytes 6291460
  82.1 11.9 %collective-permute-start.1 = (bf16[3,256]{1,0:T(4,128)(2,1)S(1)}, bf16[3,256]{1,0:T(4,128)(2,1)S(1)}, u32[]{:S(2)}, u32[]{:S(2)}) collective-permute-start(bf16[3,256]{1,0:T(4,128)(2,1)S(1)} %slice.191), channel_id=1, source_target_pairs={{0,8},{8,16},{16,24},{24,32},{32,40},{40,48},{48,56},{56,64},{64,7... | collective-permute-start | bytes 4616 | tf_op jit(solution)/shard_map/ppermute | solution.py:17
  89.6 4.5 %copy-start.9 = (f32[256]{0:T(256)S(1)}, f32[256]{0:T(256)}, u32[]{:S(2)}) copy-start(f32[256]{0:T(256)} %param.24) | copy-start | bytes 3076
  92.0 4.2 %collective-permute-start = (bf16[3,512]{1,0:T(4,128)(2,1)S(1)}, bf16[3,512]{1,0:T(4,128)(2,1)S(1)}, u32[]{:S(2)}, u32[]{:S(2)}) collective-permute-start(bf16[3,512]{1,0:T(4,128)(2,1)S(1)} %slice.180), channel_id=1, source_target_pairs={{0,8},{8,16},{16,24},{24,32},{32,40},{40,48},{48,56},{56,64},{64,7... | collective-permute-start | bytes 9224 | tf_op jit(solution)/shard_map/ppermute | solution.py:17
  95.5 1.1 copy-start.8
  110.9 1.3 copy-start.10
  111.9 162.2 %reduce-scatter.2.cloned.1.call-start = ((), (), s32[]{:S(2)}) async-start(), calls=%async_computation.2 | async-start | bytes 4755456 | tf_op jit(solution)/shard_map/reduce_scatter | solution.py:163
  112.3 2.9 %copy-start.3 = (f32[4,256,8,64]{1,0,3,2:T(4,128)S(1)}, f32[4,256,8,64]{1,0,3,2:T(4,128)}, u32[]{:S(2)}) copy-start(f32[4,256,8,64]{1,0,3,2:T(4,128)} %get-tuple-element.12) | copy-start | bytes 6291460
  184.2 8.9 %copy-start.2 = (bf16[1024,128]{1,0:T(8,128)(2,1)S(1)}, bf16[1024,128]{1,0:T(8,128)(2,1)}, u32[]{:S(2)}) copy-start(bf16[1024,128]{1,0:T(8,128)(2,1)} %get-tuple-element.14) | copy-start | bytes 786436
  184.2 8.9 %copy-start.4 = (f32[4,8,64,256]{3,2,1,0:T(8,128)S(1)}, f32[4,8,64,256]{3,2,1,0:T(8,128)}, u32[]{:S(2)}) copy-start(f32[4,8,64,256]{3,2,1,0:T(8,128)} %fusion.2) | copy-start | bytes 6291460
  184.2 8.9 %copy-start.5 = (f32[1,8,64,128]{3,2,1,0:T(8,128)S(1)}, f32[1,8,64,128]{3,2,1,0:T(8,128)}, u32[]{:S(2)}) copy-start(f32[1,8,64,128]{3,2,1,0:T(8,128)} %get-tuple-element.8) | copy-start | bytes 786436
  184.2 9.0 %copy-start.6 = (f32[1,8,64,128]{3,2,1,0:T(8,128)S(1)}, f32[1,8,64,128]{3,2,1,0:T(8,128)}, u32[]{:S(2)}) copy-start(f32[1,8,64,128]{3,2,1,0:T(8,128)} %get-tuple-element.9) | copy-start | bytes 786436
  184.2 9.0 %copy-start.7 = (f32[1,8,64,128]{3,2,1,0:T(8,128)S(1)}, f32[1,8,64,128]{3,2,1,0:T(8,128)}, u32[]{:S(2)}) copy-start(f32[1,8,64,128]{3,2,1,0:T(8,128)} %get-tuple-element.10) | copy-start | bytes 786436
  204.3 8.2 %copy-start.13 = (f32[512]{0:T(512)S(1)}, f32[512]{0:T(512)}, u32[]{:S(2)}) copy-start(f32[512]{0:T(512)} %param.28) | copy-start | bytes 6148
Sparse Core Ops, SparseCore 0:
  9.7 62.5 all-gather.3
  112.0 62.6 all-gather.5
  218.8 55.2 reduce-scatter.1

commit v2 on v1

--- a/solution.py
+++ b/solution.py
@@ -134,15 +134,23 @@
         running_gain = passing[group_no] * running_gain
     blocks_n = lax.axis_size("seq")
     gain_row = jnp.broadcast_to(running_gain[:, None, None], (heads_here, 1, state_width))
-    packed = jnp.concatenate([running_state, gain_row], 1)[None]
-    gathered = lax.all_gather(packed, "seq", tiled=True)
-    all_states = gathered[:, :, :head_width]
-    all_gains = gathered[:, :, head_width, 0]
-    order = jnp.arange(blocks_n)
-    between = (order[:, None] < order[None, :]) & (order[None, :] < device)
-    factors = jnp.where(between[:, :, None], all_gains[None, :, :], 1.0)
-    weights = jnp.where((order < device)[:, None], jnp.prod(factors, axis=1), 0.0)
-    incoming = jnp.einsum("ih,ihpn->hpn", weights, all_states, precision=HIGH)
+    packed = jnp.concatenate([running_state, gain_row], 1)
+    prefix = shifted(packed, "seq", 1)
+    prefix = jnp.where(device > 0, prefix, jnp.concatenate([0.0 * running_state, 1.0 + 0.0 * gain_row], 1))
+    reach = 1
+    while reach < blocks_n:
+        earlier_part = shifted(prefix, "seq", reach)
+        later_gain = prefix[:, head_width:, :]
+        joined_part = jnp.concatenate(
+            [
+                later_gain * earlier_part[:, :head_width, :] + prefix[:, :head_width, :],
+                later_gain * earlier_part[:, head_width:, :],
+            ],
+            1,
+        )
+        prefix = jnp.where(device >= reach, joined_part, prefix)
+        reach *= 2
+    incoming = prefix[:, :head_width, :]
     entering = jnp.stack(gain_list, 0)[:, :, None, None] * incoming[None] + jnp.stack(local_list, 0)
     enter_weight = jnp.where((group_ids == prior_ids[:, None])[:, :, None], jnp.exp(cumul), 0.0)
     carried = (

time: 283 us -> 273 us (0.965)
  starting transfers between devices: 9.6 us -> 37 us
  waiting for transfers between devices: 162 us -> 137 us
  matrix products: 46.3 us -> 36.5 us
  local copies, waits for them, and re-layouts: 29 us -> 20.5 us
  other arithmetic: 21.4 us -> 26.9 us
    all_gather x1 -> x0, waiting for transfers between devices: 48.6 us -> none  [shards(): gathered = lax.all_gather(packed, 'seq', tiled=True)]
    ppermute x2 -> x8, starting transfers between devices: 9.3 us -> 36.9 us  [shifted(): return lax.ppermute(x, axis, pairs)]
    ppermute x2 -> x8, waiting for transfers between devices: 0.01 us -> 18.2 us  [shifted(): return lax.ppermute(x, axis, pairs)]
    dot_general x1 -> x0, matrix products: 8.89 us -> none  [shards(): incoming = jnp.einsum('ih,ihpn->hpn', weights, all_states, precision=HIGH)]
    slice x5 -> x2, local copies, waits for them, and re-layouts: 8.84 us -> 0.19 us  [the longest x1 7.61 us: shards(): all_states = gathered[:, :, :head_width]]
    reduce_scatter x1, waiting for transfers between devices: 54.5 us -> 59.3 us  [shards(): lax.psum_scatter(joined.astype(jnp.bfloat16), 'head', scatter_dimension=1...]
    add x0 -> x6, other arithmetic: none -> 3.03 us  [the longest x5 3.02 us: shards(): later_gain * earlier_part[:, :head_width, :] + prefix[:, :head_width, :]]
  transfers between devices with their start and end apart: 5 -> 10, of which waited for: 3 -> 7; matrix products, arithmetic and copies ran while one was open for 9% -> 9% of each run, Pallas kernels for 0% -> 0%
where the time goes in v2:
time: 273 us; the launch traced here: 272 us
  waiting for transfers between devices  137 us (50%)
  starting transfers between devices  37 us (14%)
  matrix products  36.5 us (13%)
  other arithmetic  26.9 us (10%)
  local copies, waits for them, and re-layouts  20.5 us (8%)
  between operations  14.5 us (5%)
    reduce_scatter x1, waiting for transfers between devices, shards(): lax.psum_scatter(joined.astype(jnp.bfloat16), 'head', scatter_dimension=1...  59.3 us
    all_gather x1, waiting for transfers between devices, shards(): piece = lax.all_gather(tokens, 'head', axis=1, tiled=True)  58.5 us
    ppermute x8, starting transfers between devices, shifted(): return lax.ppermute(x, axis, pairs)  36.9 us
    ppermute x8, waiting for transfers between devices, shifted(): return lax.ppermute(x, axis, pairs)  18.2 us
    dot_general x4, matrix products, partial_product(): return jnp.dot(piece, matrix, preferred_element_type=jnp.float32)  17.5 us
    dot_general x1, matrix products, shards(): jnp.einsum('chts,cshp->cthp', decays * scores[:, None, :, :], group_x, pr...  10.1 us
    reshape x2, local copies, waits for them, and re-layouts, shards(): (within + carried).reshape(rows_here, heads_here, head_width)  8.68 us
  transfers between devices with their start and end apart: 10, of which 7 were waited for; matrix products, arithmetic and copies ran while one was open for 9% of the time, Pallas kernels for 0%

profile of v2, /device:TPU:1, one launch (start us, length us, event | category | flops | bytes accessed | tf_op | source)
XLA Modules:
  0.0 272.1 jit_solution(13746437039814068808)
XLA Ops:
  8.7 0.8 broadcast_select_fusion
  11.1 0.8 fusion.56
  12.1 0.8 fusion.72
  12.9 0.9 fusion.70
  13.8 58.5 %all-gather.2.cloned.1.call-done = bf16[1024,2048]{1,0:T(8,128)(2,1)} async-done(((bf16[1024,256]{1,0:T(8,128)(2,1)}), bf16[1024,2048]{1,0:T(8,128)(2,1)}) %all-gather.2.cloned.1.call-update) | async-done | bytes 4194320 | tf_op jit(solution)/shard_map/all_gather | solution.py:75
  72.3 3.4 %negate_multiply_fusion = (f32[1024,8]{0,1:T(8,128)S(1)}, f32[1024,8]{0,1:T(8,128)S(1)}) fusion(f32[8]{0:T(128)} %param.26, f32[8]{0:T(128)} %param.25, bf16[1024,2048]{1,0:T(8,128)(2,1)} %all-gather.2.cloned.1.call-done, bf16[2048,8]{0,1:T(8,128)(2,1)} %param.20), kind=kOutput, calls=%fused_computation.101 | convolution fusion | flops 33628160 | bytes 4292672 | tf_op jit(solution)/shard_map/dot_general | solution.py:78
  75.7 2.3 reduce-window.6
  78.5 3.6 %convolution_convert_fusion.2 = bf16[1024,256]{1,0:T(8,128)(2,1)S(1)} fusion(bf16[1024,2048]{1,0:T(8,128)(2,1)} %all-gather.2.cloned.1.call-done, bf16[2048,256]{1,0:T(8,128)(2,1)S(1)} %copy-done.14), kind=kOutput, calls=%fused_computation.33 | convolution fusion | flops 1074003968 | bytes 5767168 | tf_op jit(solution)/shard_map/dot_general | solution.py:78
  82.1 7.4 %collective-permute-start.1 = (bf16[3,256]{1,0:T(4,128)(2,1)S(1)}, bf16[3,256]{1,0:T(4,128)(2,1)S(1)}, u32[]{:S(2)}, u32[]{:S(2)}) collective-permute-start(bf16[3,256]{1,0:T(4,128)(2,1)S(1)} %slice.267), channel_id=1, source_target_pairs={{0,8},{8,16},{16,24},{24,32},{32,40},{40,48},{48,56},{56,64},{64,7... | collective-permute-start | bytes 4616 | tf_op jit(solution)/shard_map/ppermute | solution.py:17
  89.7 2.3 convolution_convert_fusion.1
  92.0 1.9 collective-permute-start
  94.1 1.3 multiply_convert_fusion.3
  96.6 3.2 %fusion.36 = f32[1024,512]{1,0:T(8,128)} fusion(f32[512]{0:T(512)S(1)} %copy-done.10, f32[512]{0:T(512)S(1)} %bitcast.132, f32[1027,512]{1,0:T(8,128)S(1)} %maximum_convert_fusion, pred[1024]{0:T(1024)(128)(4,1)S(1)} %get-tuple-element.36, f32[512]{0:T(512)S(1)} %bitcast.133, pred[1024]{0:T(1024)(128)(4,1)S(1)} %get-tuple-element.37, f32[512]{0:T(512)S(1)} %bitcast.131, ...), kind=kLoop, calls=%fused_computation.61 | loop fusion | flops 8912896 | bytes 10499072 | tf_op jit(solution)/shard_map/convert_element_type | solution.py:100
  99.8 2.9 %copy.64 = f32[1024,512]{0,1:T(8,128)} copy(f32[1024,512]{1,0:T(8,128)} %fusion.36) | data formatting | bytes 4194304 | tf_op jit(solution)/shard_map/convert_element_type | solution.py:100
  102.7 3.3 %reshape.204 = f32[4,256,8,64]{1,0,3,2:T(4,128)} reshape(f32[1024,512]{0,1:T(8,128)} %copy.64) | data formatting | bytes 4194304 | tf_op jit(solution)/shard_map/reshape | solution.py:100
  106.0 3.8 %broadcast_multiply_fusion = (f32[4,256,8,64]{1,0,3,2:T(4,128)S(1)}, f32[4,256,8,64]{1,0,3,2:T(4,128)}) fusion(f32[4,256,8]{1,0,2:T(4,128)S(1)} %copy.69, f32[4,256,8,64]{1,0,3,2:T(4,128)} %reshape.204, f32[4,256,8]{1,0,2:T(4,128)S(1)} %copy.65), kind=kLoop, calls=%fused_computation.57 | loop fusion | flops 1048576 | bytes 6356992 | tf_op jit(solution)/shard_map/mul | solution.py:122
  109.8 1.3 fusion.18
  111.3 3.5 %collective-permute-start.2 = (f32[8,65,128]{2,1,0:T(8,128)S(1)}, f32[8,65,128]{2,1,0:T(8,128)S(1)}, u32[]{:S(2)}, u32[]{:S(2)}) collective-permute-start(f32[8,65,128]{2,1,0:T(8,128)S(1)} %pad_maximum_fusion.1), channel_id=1, source_target_pairs={{0,8},{8,16},{16,24},{24,32},{32,40},{40,48},{48,56},{56,64},{64,7... | collective-permute-start | bytes 798728 | tf_op jit(solution)/shard_map/ppermute | solution.py:17
  114.8 3.6 %collective-permute-done.2 = f32[8,65,128]{2,1,0:T(8,128)S(1)} collective-permute-done((f32[8,65,128]{2,1,0:T(8,128)S(1)}, f32[8,65,128]{2,1,0:T(8,128)S(1)}, u32[]{:S(2)}, u32[]{:S(2)}) %collective-permute-start.2) | collective-permute-done | bytes 266272 | tf_op jit(solution)/shard_map/ppermute | solution.py:17
  118.6 4.4 %collective-permute-start.3 = (f32[8,65,128]{2,1,0:T(8,128)S(1)}, f32[8,65,128]{2,1,0:T(8,128)}, u32[]{:S(2)}, u32[]{:S(2)}) collective-permute-start(f32[8,65,128]{2,1,0:T(8,128)S(1)} %maximum_select_fusion), channel_id=1, source_target_pairs={{0,8},{8,16},{16,24},{24,32},{32,40},{40,48},{48,56},{56,64},{64,7... | collective-permute-start | bytes 798728 | tf_op jit(solution)/shard_map/ppermute | solution.py:17
  123.0 3.6 %collective-permute-done.3 = f32[8,65,128]{2,1,0:T(8,128)} collective-permute-done((f32[8,65,128]{2,1,0:T(8,128)S(1)}, f32[8,65,128]{2,1,0:T(8,128)}, u32[]{:S(2)}, u32[]{:S(2)}) %collective-permute-start.3) | collective-permute-done | bytes 266272 | tf_op jit(solution)/shard_map/ppermute | solution.py:17
  126.7 0.8 fusion.69
  127.4 1.0 slice_add_fusion.3
  128.5 3.5 %collective-permute-start.4 = (f32[8,65,128]{2,1,0:T(8,128)S(1)}, f32[8,65,128]{2,1,0:T(8,128)}, u32[]{:S(2)}, u32[]{:S(2)}) collective-permute-start(f32[8,65,128]{2,1,0:T(8,128)S(1)} %maximum_select_fusion.1), channel_id=1, source_target_pairs={{0,16},{8,24},{16,32},{24,40},{32,48},{40,56},{48,64},{56,72},{64,... | collective-permute-start | bytes 798728 | tf_op jit(solution)/shard_map/ppermute | solution.py:17
  132.1 3.8 %collective-permute-done.4 = f32[8,65,128]{2,1,0:T(8,128)} collective-permute-done((f32[8,65,128]{2,1,0:T(8,128)S(1)}, f32[8,65,128]{2,1,0:T(8,128)}, u32[]{:S(2)}, u32[]{:S(2)}) %collective-permute-start.4) | collective-permute-done | bytes 266272 | tf_op jit(solution)/shard_map/ppermute | solution.py:17
  135.9 0.8 fusion.68
  136.6 1.0 slice_add_fusion.2
  137.6 1.0 maximum_select_fusion.2
  138.6 8.5 %collective-permute-start.5 = (f32[8,65,128]{2,1,0:T(8,128)S(1)}, f32[8,65,128]{2,1,0:T(8,128)}, u32[]{:S(2)}, u32[]{:S(2)}) collective-permute-start(f32[8,65,128]{2,1,0:T(8,128)S(1)} %maximum_select_fusion.2), channel_id=1, source_target_pairs={{0,32},{8,40},{16,48},{24,56},{32,64},{40,72},{48,80},{56,88},{64,... | collective-permute-start | bytes 798728 | tf_op jit(solution)/shard_map/ppermute | solution.py:17
  147.2 0.9 compare_and_fusion
  148.3 4.9 %collective-permute-done.5 = f32[8,65,128]{2,1,0:T(8,128)} collective-permute-done((f32[8,65,128]{2,1,0:T(8,128)S(1)}, f32[8,65,128]{2,1,0:T(8,128)}, u32[]{:S(2)}, u32[]{:S(2)}) %collective-permute-start.5) | collective-permute-done | bytes 266272 | tf_op jit(solution)/shard_map/ppermute | solution.py:17
  153.3 0.8 fusion.67
  154.0 1.0 slice_add_fusion.1
  155.1 2.1 collective-permute-start.6
  157.3 1.3 fusion.74
  158.6 2.2 collective-permute-done.6
  161.0 5.5 %collective-permute-start.7 = (f32[8,65,128]{2,1,0:T(8,128)S(1)}, f32[8,65,128]{2,1,0:T(8,128)S(1)}, u32[]{:S(2)}, u32[]{:S(2)}) collective-permute-start(f32[8,65,128]{2,1,0:T(8,128)S(1)} %maximum_select_fusion.4), channel_id=1, source_target_pairs={{0,128},{8,136},{16,144},{24,152},{32,160},{40,168},{48,176},{56,1... | collective-permute-start | bytes 798728 | tf_op jit(solution)/shard_map/ppermute | solution.py:17
  166.5 10.1 %fusion = f32[4,8,64,256]{3,2,1,0:T(8,128)S(1)} fusion(f32[4,256,256]{2,1,0:T(8,128)S(1)} %fusion.74, f32[4,8,256]{2,1,0:T(8,128)S(1)} %add_bitcast_fusion.2, pred[4,256,256]{2,1,0:T(8,128)(4,1)S(1)} %copy-done.9, f32[4,256,8,64]{1,0,3,2:T(4,128)S(1)} %copy-done.8), kind=kOutput, calls=%fused_computation | convolution fusion | flops 1619001344 | bytes 5537792 | tf_op jit(solution)/shard_map/chts,cshp->cthp/dot_general | solution.py:116
  177.5 0.8 add_bitcast_fusion
  178.3 2.4 bitcast_add_fusion
  180.7 3.9 %copy.78 = f32[4,256,8,64]{3,2,1,0:T(8,128)} copy(f32[4,256,8,64]{1,3,2,0:T(8,128)} %bitcast_add_fusion) | data formatting | bytes 4194304 | tf_op jit(solution)/shard_map/reshape | solution.py:161
  184.6 4.8 %reshape.214 = f32[1024,512]{1,0:T(8,128)} reshape(f32[4,256,8,64]{3,2,1,0:T(8,128)} %copy.78) | data formatting | bytes 4194304 | tf_op jit(solution)/shard_map/reshape | solution.py:161
  189.4 8.1 %multiply_reduce_fusion = (bf16[1024]{0:T(1024)(128)(2,1)S(1)}, f32[1024,512]{1,0:T(8,128)}) fusion(f32[1024,512]{1,0:T(8,128)} %reshape.214, f32[1024,512]{1,0:T(8,128)} %fusion.36, f32[512]{0:T(512)S(1)} %mul.454, bf16[1024,2048]{1,0:T(8,128)(2,1)} %all-gather.2.cloned.1.call-done, bf16[2048,512]{1,0:T(8,128)(2,1)} %param.17), kind=kOutput, calls=%fused_computation.28 | convolution fusion | flops 2152201216 | bytes 12587008 | tf_op jit(solution)/shard_map/dot_general | solution.py:78
  197.6 3.9 %convolution_convert_fusion = bf16[1024,2048]{1,0:T(8,128)(2,1)S(1)} fusion(bf16[512,2048]{1,0:T(8,128)(2,1)S(1)} %copy-done, f32[1024,512]{1,0:T(8,128)} %get-tuple-element.5, f32[512]{0:T(512)S(1)} %copy-done.15), kind=kOutput, calls=%fused_computation.12 | convolution fusion | flops 2150629376 | bytes 8390656 | tf_op jit(solution)/shard_map/dot_general | solution.py:167
  201.5 2.3 pad_maximum_fusion
  203.8 59.3 %reduce-scatter.2.cloned.1.call-done = bf16[1028,256]{1,0:T(8,128)(2,1)} async-done(((bf16[1028,2048]{1,0:T(8,128)(2,1)}), bf16[1028,256]{1,0:T(8,128)(2,1)}) %reduce-scatter.2.cloned.1.call-update) | async-done | bytes 526352 | tf_op jit(solution)/shard_map/reduce_scatter | solution.py:171
  263.1 1.1 convert_element_type.41
  264.3 1.0 fusion.21
  (90 shorter events, 7.0 us)
Async XLA Ops:
  7.2 190.4 %copy-start = (bf16[512,2048]{1,0:T(8,128)(2,1)S(1)}, bf16[512,2048]{1,0:T(8,128)(2,1)}, u32[]{:S(2)}) copy-start(bf16[512,2048]{1,0:T(8,128)(2,1)} %param.29) | copy-start | bytes 6291460
  7.2 65.1 %all-gather.2.cloned.1.call-start = ((), (), s32[]{:S(2)}) async-start(), calls=%async_computation.1 | async-start | bytes 4718592 | tf_op jit(solution)/shard_map/all_gather | solution.py:75
  7.9 255.2 %reduce-scatter.2.cloned.1.call-start = ((), (), s32[]{:S(2)}) async-start(), calls=%async_computation.2 | async-start | bytes 4755456 | tf_op jit(solution)/shard_map/reduce_scatter | solution.py:171
  13.8 64.7 %copy-start.14 = (bf16[2048,256]{1,0:T(8,128)(2,1)S(1)}, bf16[2048,256]{1,0:T(8,128)(2,1)}, u32[]{:S(2)}) copy-start(bf16[2048,256]{1,0:T(8,128)(2,1)} %param.19) | copy-start | bytes 3145732
  78.5 11.2 %copy-start.1 = (bf16[1024,2048]{1,0:T(8,128)(2,1)S(1)}, bf16[1024,2048]{1,0:T(8,128)(2,1)}, u32[]{:S(2)}) copy-start(bf16[1024,2048]{1,0:T(8,128)(2,1)} %all-gather.2.cloned.1.call-done) | copy-start | bytes 12582916
  78.5 11.2 %copy-start.13 = (bf16[2048,512]{1,0:T(8,128)(2,1)S(1)}, bf16[2048,512]{1,0:T(8,128)(2,1)}, u32[]{:S(2)}) copy-start(bf16[2048,512]{1,0:T(8,128)(2,1)} %param.18) | copy-start | bytes 6291460
  82.1 11.9 %collective-permute-start.1 = (bf16[3,256]{1,0:T(4,128)(2,1)S(1)}, bf16[3,256]{1,0:T(4,128)(2,1)S(1)}, u32[]{:S(2)}, u32[]{:S(2)}) collective-permute-start(bf16[3,256]{1,0:T(4,128)(2,1)S(1)} %slice.267), channel_id=1, source_target_pairs={{0,8},{8,16},{16,24},{24,32},{32,40},{40,48},{48,56},{56,64},{64,7... | collective-permute-start | bytes 4616 | tf_op jit(solution)/shard_map/ppermute | solution.py:17
  89.6 4.5 %copy-start.11 = (f32[256]{0:T(256)S(1)}, f32[256]{0:T(256)}, u32[]{:S(2)}) copy-start(f32[256]{0:T(256)} %param.24) | copy-start | bytes 3076
  92.0 4.2 %collective-permute-start = (bf16[3,512]{1,0:T(4,128)(2,1)S(1)}, bf16[3,512]{1,0:T(4,128)(2,1)S(1)}, u32[]{:S(2)}, u32[]{:S(2)}) collective-permute-start(bf16[3,512]{1,0:T(4,128)(2,1)S(1)} %slice.256), channel_id=1, source_target_pairs={{0,8},{8,16},{16,24},{24,32},{32,40},{40,48},{48,56},{56,64},{64,7... | collective-permute-start | bytes 9224 | tf_op jit(solution)/shard_map/ppermute | solution.py:17
  95.5 1.1 copy-start.10
  96.2 13.6 %copy-start.6 = (bf16[1024,128]{1,0:T(8,128)(2,1)}, bf16[1024,128]{1,0:T(8,128)(2,1)S(1)}, u32[]{:S(2)}) copy-start(bf16[1024,128]{1,0:T(8,128)(2,1)S(1)} %get-tuple-element.19) | copy-start | bytes 786436
  111.2 7.3 %copy-start.4 = (f32[8,64,128]{2,1,0:T(8,128)}, f32[8,64,128]{2,1,0:T(8,128)S(1)}, u32[]{:S(2)}) copy-start(f32[8,64,128]{2,1,0:T(8,128)S(1)} %get-tuple-element.9) | copy-start | bytes 786436
  111.3 7.1 %collective-permute-start.2 = (f32[8,65,128]{2,1,0:T(8,128)S(1)}, f32[8,65,128]{2,1,0:T(8,128)S(1)}, u32[]{:S(2)}, u32[]{:S(2)}) collective-permute-start(f32[8,65,128]{2,1,0:T(8,128)S(1)} %pad_maximum_fusion.1), channel_id=1, source_target_pairs={{0,8},{8,16},{16,24},{24,32},{32,40},{40,48},{48,56},{56,64},{64,7... | collective-permute-start | bytes 798728 | tf_op jit(solution)/shard_map/ppermute | solution.py:17
  118.6 29.6 %copy-start.12 = (f32[8]{0:T(128)S(1)}, f32[8]{0:T(128)}, u32[]{:S(2)}) copy-start(f32[8]{0:T(128)} %param.27) | copy-start | bytes 100
  118.6 9.8 %copy-start.3 = (f32[8,65,128]{2,1,0:T(8,128)}, f32[8,65,128]{2,1,0:T(8,128)S(1)}, u32[]{:S(2)}) copy-start(f32[8,65,128]{2,1,0:T(8,128)S(1)} %maximum_select_fusion) | copy-start | bytes 798724
  118.6 8.0 %collective-permute-start.3 = (f32[8,65,128]{2,1,0:T(8,128)S(1)}, f32[8,65,128]{2,1,0:T(8,128)}, u32[]{:S(2)}, u32[]{:S(2)}) collective-permute-start(f32[8,65,128]{2,1,0:T(8,128)S(1)} %maximum_select_fusion), channel_id=1, source_target_pairs={{0,8},{8,16},{16,24},{24,32},{32,40},{40,48},{48,56},{56,64},{64,7... | collective-permute-start | bytes 798728 | tf_op jit(solution)/shard_map/ppermute | solution.py:17
  128.5 9.1 %copy-start.2 = (f32[8,65,128]{2,1,0:T(8,128)}, f32[8,65,128]{2,1,0:T(8,128)S(1)}, u32[]{:S(2)}) copy-start(f32[8,65,128]{2,1,0:T(8,128)S(1)} %maximum_select_fusion.1) | copy-start | bytes 798724
  128.5 7.4 %collective-permute-start.4 = (f32[8,65,128]{2,1,0:T(8,128)S(1)}, f32[8,65,128]{2,1,0:T(8,128)}, u32[]{:S(2)}, u32[]{:S(2)}) collective-permute-start(f32[8,65,128]{2,1,0:T(8,128)S(1)} %maximum_select_fusion.1), channel_id=1, source_target_pairs={{0,16},{8,24},{16,32},{24,40},{32,48},{40,56},{48,64},{56,72},{64,... | collective-permute-start | bytes 798728 | tf_op jit(solution)/shard_map/ppermute | solution.py:17
  138.6 14.6 %collective-permute-start.5 = (f32[8,65,128]{2,1,0:T(8,128)S(1)}, f32[8,65,128]{2,1,0:T(8,128)}, u32[]{:S(2)}, u32[]{:S(2)}) collective-permute-start(f32[8,65,128]{2,1,0:T(8,128)S(1)} %maximum_select_fusion.2), channel_id=1, source_target_pairs={{0,32},{8,40},{16,48},{24,56},{32,64},{40,72},{48,80},{56,88},{64,... | collective-permute-start | bytes 798728 | tf_op jit(solution)/shard_map/ppermute | solution.py:17
  155.0 11.5 %copy-start.8 = (f32[4,256,8,64]{1,0,3,2:T(4,128)S(1)}, f32[4,256,8,64]{1,0,3,2:T(4,128)}, u32[]{:S(2)}) copy-start(f32[4,256,8,64]{1,0,3,2:T(4,128)} %get-tuple-element.18) | copy-start | bytes 6291460
  155.0 11.5 %copy-start.9 = (pred[4,256,256]{2,1,0:T(8,128)(4,1)S(1)}, pred[4,256,256]{2,1,0:T(8,128)(4,1)}, u32[]{:S(2)}) copy-start(pred[4,256,256]{2,1,0:T(8,128)(4,1)} %compare_and_fusion) | copy-start | bytes 786436
  155.1 5.8 %collective-permute-start.6 = (f32[8,65,128]{2,1,0:T(8,128)S(1)}, f32[8,65,128]{2,1,0:T(8,128)S(1)}, u32[]{:S(2)}, u32[]{:S(2)}) collective-permute-start(f32[8,65,128]{2,1,0:T(8,128)S(1)} %maximum_select_fusion.3), channel_id=1, source_target_pairs={{0,64},{8,72},{16,80},{24,88},{32,96},{40,104},{48,112},{56,120},{... | collective-permute-start | bytes 798728 | tf_op jit(solution)/shard_map/ppermute | solution.py:17
  161.0 15.7 %collective-permute-start.7 = (f32[8,65,128]{2,1,0:T(8,128)S(1)}, f32[8,65,128]{2,1,0:T(8,128)S(1)}, u32[]{:S(2)}, u32[]{:S(2)}) collective-permute-start(f32[8,65,128]{2,1,0:T(8,128)S(1)} %maximum_select_fusion.4), channel_id=1, source_target_pairs={{0,128},{8,136},{16,144},{24,152},{32,160},{40,168},{48,176},{56,1... | collective-permute-start | bytes 798728 | tf_op jit(solution)/shard_map/ppermute | solution.py:17
  176.5 1.0 copy-start.5
  176.6 1.7 copy-start.7
  189.4 8.2 %copy-start.15 = (f32[512]{0:T(512)S(1)}, f32[512]{0:T(512)}, u32[]{:S(2)}) copy-start(f32[512]{0:T(512)} %param.28) | copy-start | bytes 6148
Sparse Core Ops, SparseCore 0:
  9.7 62.5 all-gather.1
  204.0 59.1 reduce-scatter.1

commit v3 on v2

--- a/solution.py
+++ b/solution.py
@@ -5,6 +5,7 @@
 
 GROUP = 256
 INNER = 4096
+LONG = 16384
 
 
 EPSILON = 1e-05
@@ -138,7 +139,7 @@
     prefix = shifted(packed, "seq", 1)
     prefix = jnp.where(device > 0, prefix, jnp.concatenate([0.0 * running_state, 1.0 + 0.0 * gain_row], 1))
     reach = 1
-    while reach < blocks_n:
+    while reach < min(blocks_n, LONG // rows_here):
         earlier_part = shifted(prefix, "seq", reach)
         later_gain = prefix[:, head_width:, :]
         joined_part = jnp.concatenate(
@@ -161,18 +162,24 @@
     ssd_out = (within + carried).reshape(rows_here, heads_here, head_width) + skip_gain[
         None, :, None
     ] * x_float
-    gated = ssd_out.reshape(rows_here, inner_here) * jax.nn.silu(gate_full)
     heads_n = lax.axis_size("head")
-    scaled = (gated * norm_gain).astype(jnp.bfloat16)
-    partial_out = jnp.dot(scaled, w_out, preferred_element_type=jnp.float32)
-    cols = partial_out.shape[1] // heads_n
-    square_rows = jnp.sum(gated * gated, axis=1).reshape(-1, cols)
-    joined = jnp.concatenate([partial_out, jnp.tile(square_rows, (1, heads_n))], 0)
-    summed = lax.psum_scatter(
-        joined.astype(jnp.bfloat16), "head", scatter_dimension=1, tiled=True
-    ).astype(jnp.float32)
-    mean_square = (summed[rows_here:].reshape(rows_here) / INNER)[:, None]
-    mixed = (summed[:rows_here] * lax.rsqrt(mean_square + EPSILON)).astype(jnp.bfloat16)
+    halves = 2
+    span = rows_here // halves
+    mixed_parts = []
+    for half in range(halves):
+        rows = slice(half * span, (half + 1) * span)
+        gated = ssd_out.reshape(rows_here, inner_here)[rows] * jax.nn.silu(gate_full[rows])
+        scaled = (gated * norm_gain).astype(jnp.bfloat16)
+        partial_out = jnp.dot(scaled, w_out, preferred_element_type=jnp.float32)
+        cols = partial_out.shape[1] // heads_n
+        square_rows = jnp.sum(gated * gated, axis=1).reshape(-1, cols)
+        joined = jnp.concatenate([partial_out, jnp.tile(square_rows, (1, heads_n))], 0)
+        summed = lax.psum_scatter(
+            joined.astype(jnp.bfloat16), "head", scatter_dimension=1, tiled=True
+        ).astype(jnp.float32)
+        mean_square = (summed[span:].reshape(span) / INNER)[:, None]
+        mixed_parts.append((summed[:span] * lax.rsqrt(mean_square + EPSILON)).astype(jnp.bfloat16))
+    mixed = jnp.concatenate(mixed_parts, 0)
     return (mixed, end_state)
 
 

time: 273 us -> 277 us (1.015); the launches traced: 272 us -> 272 us
  waiting for transfers between devices: 137 us -> 155 us
  local copies, waits for them, and re-layouts: 20.5 us -> 13.5 us
  starting transfers between devices: 37 us -> 30.4 us
  matrix products: 36.5 us -> 31.3 us
    reduce_scatter x1 -> x2, waiting for transfers between devices: 59.3 us -> 82.9 us  [shards(): lax.psum_scatter(joined.astype(jnp.bfloat16), 'head', scatter_dimension=1...]
    reshape x2 -> x1, local copies, waits for them, and re-layouts: 8.68 us -> 0.24 us  [shards(): (within + carried).reshape(rows_here, heads_here, head_width)]
    ppermute x8 -> x7, starting transfers between devices: 36.9 us -> 30.3 us  [shifted(): return lax.ppermute(x, axis, pairs)]
    ppermute x8 -> x7, waiting for transfers between devices: 18.2 us -> 13.1 us  [shifted(): return lax.ppermute(x, axis, pairs)]
    dot_general x4, matrix products: 17.5 us -> 14.6 us  [partial_product(): return jnp.dot(piece, matrix, preferred_element_type=jnp.float32)]
  transfers between devices with their start and end apart: 10 -> 10, of which waited for: 7 -> 6; matrix products, arithmetic and copies ran while one was open for 9% -> 11% of each run, Pallas kernels for 0% -> 0%
where the time goes in v3:
time: 277 us; the launch traced here: 272 us
  waiting for transfers between devices  155 us (56%)
  matrix products  31.3 us (11%)
  starting transfers between devices  30.4 us (11%)
  other arithmetic  27.6 us (10%)
  between operations  14.4 us (5%)
  local copies, waits for them, and re-layouts  13.5 us (5%)
    reduce_scatter x2, waiting for transfers between devices, shards(): lax.psum_scatter(joined.astype(jnp.bfloat16), 'head', scatter_dimension=1...  82.9 us
    all_gather x1, waiting for transfers between devices, shards(): piece = lax.all_gather(tokens, 'head', axis=1, tiled=True)  58.5 us
    ppermute x7, starting transfers between devices, shifted(): return lax.ppermute(x, axis, pairs)  30.3 us
    dot_general x4, matrix products, partial_product(): return jnp.dot(piece, matrix, preferred_element_type=jnp.float32)  14.6 us
    ppermute x7, waiting for transfers between devices, shifted(): return lax.ppermute(x, axis, pairs)  13.1 us
    dot_general x1, matrix products, shards(): jnp.einsum('chts,cshp->cthp', decays * scores[:, None, :, :], group_x, pr...  10.1 us
  transfers between devices with their start and end apart: 10, of which 6 were waited for; matrix products, arithmetic and copies ran while one was open for 11% of the time, Pallas kernels for 0%

profile of v3, /device:TPU:1, one launch (start us, length us, event | category | flops | bytes accessed | tf_op | source)
XLA Modules:
  0.0 272.5 jit_solution(2404785764330367417)
XLA Ops:
  8.0 0.8 broadcast_select_fusion
  9.3 0.7 dynamic_slice.7
  10.2 0.7 pad_add_fusion.1
  11.1 0.8 fusion.62
  12.1 0.8 fusion.78
  13.0 0.9 fusion.76
  13.8 58.5 %all-gather.2.cloned.1.call-done = bf16[1024,2048]{1,0:T(8,128)(2,1)} async-done(((bf16[1024,256]{1,0:T(8,128)(2,1)}), bf16[1024,2048]{1,0:T(8,128)(2,1)}) %all-gather.2.cloned.1.call-update) | async-done | bytes 4194320 | tf_op jit(solution)/shard_map/all_gather | solution.py:76
  72.3 3.4 %negate_multiply_fusion = (f32[1024,8]{0,1:T(8,128)S(1)}, f32[1024,8]{0,1:T(8,128)S(1)}) fusion(f32[8]{0:T(128)} %param.26, f32[8]{0:T(128)} %param.25, bf16[1024,2048]{1,0:T(8,128)(2,1)} %all-gather.2.cloned.1.call-done, bf16[2048,8]{0,1:T(8,128)(2,1)} %param.20), kind=kOutput, calls=%fused_computation.109 | convolution fusion | flops 33628160 | bytes 4292672 | tf_op jit(solution)/shard_map/dot_general | solution.py:79
  75.7 2.3 reduce-window.6
  78.2 0.7 exponential_select_fusion
  79.8 3.6 %convolution_convert_fusion.3 = bf16[1024,256]{1,0:T(8,128)(2,1)S(1)} fusion(bf16[1024,2048]{1,0:T(8,128)(2,1)} %all-gather.2.cloned.1.call-done, bf16[2048,256]{1,0:T(8,128)(2,1)S(1)} %copy-done.23), kind=kOutput, calls=%fused_computation.34 | convolution fusion | flops 1074003968 | bytes 5767168 | tf_op jit(solution)/shard_map/dot_general | solution.py:79
  83.4 7.4 %collective-permute-start.1 = (bf16[3,256]{1,0:T(4,128)(2,1)S(1)}, bf16[3,256]{1,0:T(4,128)(2,1)S(1)}, u32[]{:S(2)}, u32[]{:S(2)}) collective-permute-start(bf16[3,256]{1,0:T(4,128)(2,1)S(1)} %slice.283), channel_id=1, source_target_pairs={{0,8},{8,16},{16,24},{24,32},{32,40},{40,48},{48,56},{56,64},{64,7... | collective-permute-start | bytes 4616 | tf_op jit(solution)/shard_map/ppermute | solution.py:18
  90.8 2.3 convolution_convert_fusion.2
  93.8 1.9 collective-permute-start
  95.9 1.3 multiply_convert_fusion.3
  97.2 0.7 fusion.71
  98.3 3.2 %fusion.35 = f32[1024,512]{1,0:T(8,128)} fusion(f32[512]{0:T(512)S(1)} %copy-done.14, f32[512]{0:T(512)S(1)} %bitcast.151, f32[1027,512]{1,0:T(8,128)S(1)} %maximum_convert_fusion, pred[1024]{0:T(1024)(128)(4,1)S(1)} %get-tuple-element.40, f32[512]{0:T(512)S(1)} %bitcast.152, pred[1024]{0:T(1024)(128)(4,1)S(1)} %get-tuple-element.41, f32[512]{0:T(512)S(1)} %bitcast.150, ...), kind=kLoop, calls=%fused_computation.65 | loop fusion | flops 8912896 | bytes 10499072 | tf_op jit(solution)/shard_map/convert_element_type | solution.py:101
  101.5 2.9 %copy.57 = f32[1024,512]{0,1:T(8,128)} copy(f32[1024,512]{1,0:T(8,128)} %fusion.35) | data formatting | bytes 4194304 | tf_op jit(solution)/shard_map/convert_element_type | solution.py:101
  104.4 3.3 %reshape.226 = f32[4,256,8,64]{1,0,3,2:T(4,128)} reshape(f32[1024,512]{0,1:T(8,128)} %copy.57) | data formatting | bytes 4194304 | tf_op jit(solution)/shard_map/reshape | solution.py:101
  107.7 3.8 %broadcast_multiply_fusion = (f32[4,256,8,64]{1,0,3,2:T(4,128)S(1)}, f32[4,256,8,64]{1,0,3,2:T(4,128)}) fusion(f32[4,256,8]{1,0,2:T(4,128)S(1)} %copy.62, f32[4,256,8,64]{1,0,3,2:T(4,128)} %reshape.226, f32[4,256,8]{1,0,2:T(4,128)S(1)} %copy.58), kind=kLoop, calls=%fused_computation.61 | loop fusion | flops 1048576 | bytes 6356992 | tf_op jit(solution)/shard_map/mul | solution.py:123
  111.5 1.3 fusion.19
  113.1 3.5 %collective-permute-start.2 = (f32[8,65,128]{2,1,0:T(8,128)S(1)}, f32[8,65,128]{2,1,0:T(8,128)S(1)}, u32[]{:S(2)}, u32[]{:S(2)}) collective-permute-start(f32[8,65,128]{2,1,0:T(8,128)S(1)} %pad_maximum_fusion.3), channel_id=1, source_target_pairs={{0,8},{8,16},{16,24},{24,32},{32,40},{40,48},{48,56},{56,64},{64,7... | collective-permute-start | bytes 798728 | tf_op jit(solution)/shard_map/ppermute | solution.py:18
  116.6 3.6 %collective-permute-done.2 = f32[8,65,128]{2,1,0:T(8,128)S(1)} collective-permute-done((f32[8,65,128]{2,1,0:T(8,128)S(1)}, f32[8,65,128]{2,1,0:T(8,128)S(1)}, u32[]{:S(2)}, u32[]{:S(2)}) %collective-permute-start.2) | collective-permute-done | bytes 266272 | tf_op jit(solution)/shard_map/ppermute | solution.py:18
  120.3 4.4 %collective-permute-start.3 = (f32[8,65,128]{2,1,0:T(8,128)S(1)}, f32[8,65,128]{2,1,0:T(8,128)}, u32[]{:S(2)}, u32[]{:S(2)}) collective-permute-start(f32[8,65,128]{2,1,0:T(8,128)S(1)} %maximum_select_fusion), channel_id=1, source_target_pairs={{0,8},{8,16},{16,24},{24,32},{32,40},{40,48},{48,56},{56,64},{64,7... | collective-permute-start | bytes 798728 | tf_op jit(solution)/shard_map/ppermute | solution.py:18
  125.1 3.3 %collective-permute-done.3 = f32[8,65,128]{2,1,0:T(8,128)} collective-permute-done((f32[8,65,128]{2,1,0:T(8,128)S(1)}, f32[8,65,128]{2,1,0:T(8,128)}, u32[]{:S(2)}, u32[]{:S(2)}) %collective-permute-start.3) | collective-permute-done | bytes 266272 | tf_op jit(solution)/shard_map/ppermute | solution.py:18
  128.4 0.8 fusion.75
  129.2 1.0 slice_add_fusion.2
  130.2 3.1 %collective-permute-start.4 = (f32[8,65,128]{2,1,0:T(8,128)S(1)}, f32[8,65,128]{2,1,0:T(8,128)S(1)}, u32[]{:S(2)}, u32[]{:S(2)}) collective-permute-start(f32[8,65,128]{2,1,0:T(8,128)S(1)} %maximum_select_fusion.1), channel_id=1, source_target_pairs={{0,16},{8,24},{16,32},{24,40},{32,48},{40,56},{48,64},{56,72},{64,... | collective-permute-start | bytes 798728 | tf_op jit(solution)/shard_map/ppermute | solution.py:18
  133.4 5.2 %fusion.81 = f32[1024,512]{0,1:T(8,128)S(1)} fusion(bf16[1024,2048]{1,0:T(8,128)(2,1)} %all-gather.2.cloned.1.call-done, bf16[2048,512]{1,0:T(8,128)(2,1)} %param.17), kind=kOutput, calls=%fused_computation.172 | convolution fusion | flops 2147483648 | bytes 8388608 | tf_op jit(solution)/shard_map/dot_general | solution.py:79
  138.8 8.1 %collective-permute-start.5 = (f32[8,65,128]{2,1,0:T(8,128)S(1)}, f32[8,65,128]{2,1,0:T(8,128)S(1)}, u32[]{:S(2)}, u32[]{:S(2)}) collective-permute-start(f32[8,65,128]{2,1,0:T(8,128)S(1)} %maximum_select_fusion.2), channel_id=1, source_target_pairs={{0,32},{8,40},{16,48},{24,56},{32,64},{40,72},{48,80},{56,88},{64,... | collective-permute-start | bytes 798728 | tf_op jit(solution)/shard_map/ppermute | solution.py:18
  147.3 6.1 %collective-permute-done.5 = f32[8,65,128]{2,1,0:T(8,128)S(1)} collective-permute-done((f32[8,65,128]{2,1,0:T(8,128)S(1)}, f32[8,65,128]{2,1,0:T(8,128)S(1)}, u32[]{:S(2)}, u32[]{:S(2)}) %collective-permute-start.5) | collective-permute-done | bytes 266272 | tf_op jit(solution)/shard_map/ppermute | solution.py:18
  153.6 1.9 collective-permute-start.6
  155.5 10.1 %fusion = f32[4,8,64,256]{3,2,1,0:T(8,128)S(1)} fusion(f32[4,256,256]{2,1,0:T(8,128)S(1)} %fusion.80, f32[4,8,256]{2,1,0:T(8,128)S(1)} %add_bitcast_fusion.2, pred[4,256,256]{2,1,0:T(8,128)(4,1)S(1)} %compare_and_fusion, f32[4,256,8,64]{1,0,3,2:T(4,128)S(1)} %copy-done.8), kind=kOutput, calls=%fused_computation | convolution fusion | flops 1619001344 | bytes 5537792 | tf_op jit(solution)/shard_map/chts,cshp->cthp/dot_general | solution.py:117
  165.8 0.7 copy-done.4
  166.5 0.8 add_bitcast_fusion
  167.3 1.1 fusion.18
  168.7 1.3 copy-done.1
  170.1 0.7 multiply_add_fusion
  171.0 1.7 multiply_reduce_fusion.1
  172.7 2.6 convolution_convert_fusion.1
  175.3 1.5 pad_maximum_fusion
  177.0 1.4 convolution_convert_fusion
  178.3 1.5 pad_maximum_fusion.1
  179.9 39.8 %reduce-scatter.3.cloned.1.call-done = bf16[514,256]{1,0:T(8,128)(2,1)} async-done(((bf16[514,2048]{1,0:T(8,128)(2,1)}), bf16[514,256]{1,0:T(8,128)(2,1)}) %reduce-scatter.3.cloned.1.call-update) | async-done | bytes 263184 | tf_op jit(solution)/shard_map/reduce_scatter | solution.py:177
  219.6 1.0 convert_element_type.51
  220.8 43.2 %reduce-scatter.5.cloned.1.call-done = bf16[514,256]{1,0:T(8,128)(2,1)} async-done(((bf16[514,2048]{1,0:T(8,128)(2,1)}), bf16[514,256]{1,0:T(8,128)(2,1)}) %reduce-scatter.5.cloned.1.call-update) | async-done | bytes 263184 | tf_op jit(solution)/shard_map/reduce_scatter | solution.py:177
  264.0 1.0 convert_element_type.54
  265.1 0.8 pad_maximum_fusion.2
  (116 shorter events, 6.5 us)
Async XLA Ops:
  7.2 165.6 %copy-start = (bf16[512,2048]{1,0:T(8,128)(2,1)S(1)}, bf16[512,2048]{1,0:T(8,128)(2,1)}, u32[]{:S(2)}) copy-start(bf16[512,2048]{1,0:T(8,128)(2,1)} %param.29) | copy-start | bytes 6291460
  7.2 65.1 %all-gather.2.cloned.1.call-start = ((), (), s32[]{:S(2)}) async-start(), calls=%async_computation.2 | async-start | bytes 4718592 | tf_op jit(solution)/shard_map/all_gather | solution.py:76
  7.9 211.7 %reduce-scatter.3.cloned.1.call-start = ((), (), s32[]{:S(2)}) async-start(), calls=%async_computation.3 | async-start | bytes 2396160 | tf_op jit(solution)/shard_map/reduce_scatter | solution.py:177
  13.8 66.0 %copy-start.23 = (bf16[2048,256]{1,0:T(8,128)(2,1)S(1)}, bf16[2048,256]{1,0:T(8,128)(2,1)}, u32[]{:S(2)}) copy-start(bf16[2048,256]{1,0:T(8,128)(2,1)} %param.19) | copy-start | bytes 3145732
  79.8 33.2 %copy-start.12 = (f32[8]{0:T(128)}, f32[8]{0:T(128)S(1)}, u32[]{:S(2)}) copy-start(f32[8]{0:T(128)S(1)} %get-tuple-element.13) | copy-start | bytes 100
  79.8 11.0 %copy-start.2 = (bf16[1024,2048]{1,0:T(8,128)(2,1)S(1)}, bf16[1024,2048]{1,0:T(8,128)(2,1)}, u32[]{:S(2)}) copy-start(bf16[1024,2048]{1,0:T(8,128)(2,1)} %all-gather.2.cloned.1.call-done) | copy-start | bytes 12582916
  79.8 11.0 %copy-start.22 = (bf16[2048,512]{1,0:T(8,128)(2,1)S(1)}, bf16[2048,512]{1,0:T(8,128)(2,1)}, u32[]{:S(2)}) copy-start(bf16[2048,512]{1,0:T(8,128)(2,1)} %param.18) | copy-start | bytes 6291460
  83.4 12.5 %copy-start.20 = (f32[256]{0:T(256)S(1)}, f32[256]{0:T(256)}, u32[]{:S(2)}) copy-start(f32[256]{0:T(256)} %param.24) | copy-start | bytes 3076
  83.4 12.3 %collective-permute-start.1 = (bf16[3,256]{1,0:T(4,128)(2,1)S(1)}, bf16[3,256]{1,0:T(4,128)(2,1)S(1)}, u32[]{:S(2)}, u32[]{:S(2)}) collective-permute-start(bf16[3,256]{1,0:T(4,128)(2,1)S(1)} %slice.283), channel_id=1, source_target_pairs={{0,8},{8,16},{16,24},{24,32},{32,40},{40,48},{48,56},{56,64},{64,7... | collective-permute-start | bytes 4616 | tf_op jit(solution)/shard_map/ppermute | solution.py:18
  93.8 19.0 %copy-start.10 = (f32[8]{0:T(128)}, f32[8]{0:T(128)S(1)}, u32[]{:S(2)}) copy-start(f32[8]{0:T(128)S(1)} %get-tuple-element.52) | copy-start | bytes 100
  93.8 4.2 %collective-permute-start = (bf16[3,512]{1,0:T(4,128)(2,1)S(1)}, bf16[3,512]{1,0:T(4,128)(2,1)S(1)}, u32[]{:S(2)}, u32[]{:S(2)}) collective-permute-start(bf16[3,512]{1,0:T(4,128)(2,1)S(1)} %slice.272), channel_id=1, source_target_pairs={{0,8},{8,16},{16,24},{24,32},{32,40},{40,48},{48,56},{56,64},{64,7... | collective-permute-start | bytes 9224 | tf_op jit(solution)/shard_map/ppermute | solution.py:18
  97.2 1.1 copy-start.14
  98.0 13.5 %copy-start.5 = (bf16[1024,128]{1,0:T(8,128)(2,1)}, bf16[1024,128]{1,0:T(8,128)(2,1)S(1)}, u32[]{:S(2)}) copy-start(bf16[1024,128]{1,0:T(8,128)(2,1)S(1)} %get-tuple-element.25) | copy-start | bytes 786436
  111.5 1.3 copy-start.15
  111.5 8.7 %copy-start.16 = (f32[8]{0:T(128)S(1)}, f32[8]{0:T(128)}, u32[]{:S(2)}) copy-start(f32[8]{0:T(128)} %get-tuple-element.12) | copy-start | bytes 100
  113.0 7.3 %copy-start.3 = (f32[8,64,128]{2,1,0:T(8,128)}, f32[8,64,128]{2,1,0:T(8,128)S(1)}, u32[]{:S(2)}) copy-start(f32[8,64,128]{2,1,0:T(8,128)S(1)} %get-tuple-element.11) | copy-start | bytes 786436
  113.1 7.1 %collective-permute-start.2 = (f32[8,65,128]{2,1,0:T(8,128)S(1)}, f32[8,65,128]{2,1,0:T(8,128)S(1)}, u32[]{:S(2)}, u32[]{:S(2)}) collective-permute-start(f32[8,65,128]{2,1,0:T(8,128)S(1)} %pad_maximum_fusion.3), channel_id=1, source_target_pairs={{0,8},{8,16},{16,24},{24,32},{32,40},{40,48},{48,56},{56,64},{64,7... | collective-permute-start | bytes 798728 | tf_op jit(solution)/shard_map/ppermute | solution.py:18
  120.3 8.0 %collective-permute-start.3 = (f32[8,65,128]{2,1,0:T(8,128)S(1)}, f32[8,65,128]{2,1,0:T(8,128)}, u32[]{:S(2)}, u32[]{:S(2)}) collective-permute-start(f32[8,65,128]{2,1,0:T(8,128)S(1)} %maximum_select_fusion), channel_id=1, source_target_pairs={{0,8},{8,16},{16,24},{24,32},{32,40},{40,48},{48,56},{56,64},{64,7... | collective-permute-start | bytes 798728 | tf_op jit(solution)/shard_map/ppermute | solution.py:18
  130.2 16.7 %copy-start.17 = (f32[1,8]{1,0:T(1,128)S(1)}, f32[1,8]{1,0:T(1,128)}, u32[]{:S(2)}) copy-start(f32[1,8]{1,0:T(1,128)} %get-tuple-element.50) | copy-start | bytes 100
  130.2 16.7 %copy-start.18 = (f32[1,8]{1,0:T(1,128)S(1)}, f32[1,8]{1,0:T(1,128)}, u32[]{:S(2)}) copy-start(f32[1,8]{1,0:T(1,128)} %get-tuple-element.54) | copy-start | bytes 100
  130.2 16.7 %copy-start.19 = (f32[1,8]{1,0:T(1,128)S(1)}, f32[1,8]{1,0:T(1,128)}, u32[]{:S(2)}) copy-start(f32[1,8]{1,0:T(1,128)} %get-tuple-element.55) | copy-start | bytes 100
  130.2 16.8 %copy-start.6 = (bf16[1024,128]{1,0:T(8,128)(2,1)S(1)}, bf16[1024,128]{1,0:T(8,128)(2,1)}, u32[]{:S(2)}) copy-start(bf16[1024,128]{1,0:T(8,128)(2,1)} %copy-done.5) | copy-start | bytes 786436
  130.2 16.8 %copy-start.7 = (bf16[1024,128]{1,0:T(8,128)(2,1)S(1)}, bf16[1024,128]{1,0:T(8,128)(2,1)}, u32[]{:S(2)}) copy-start(bf16[1024,128]{1,0:T(8,128)(2,1)} %get-tuple-element.26) | copy-start | bytes 786436
  130.2 8.5 %collective-permute-start.4 = (f32[8,65,128]{2,1,0:T(8,128)S(1)}, f32[8,65,128]{2,1,0:T(8,128)S(1)}, u32[]{:S(2)}, u32[]{:S(2)}) collective-permute-start(f32[8,65,128]{2,1,0:T(8,128)S(1)} %maximum_select_fusion.1), channel_id=1, source_target_pairs={{0,16},{8,24},{16,32},{24,40},{32,48},{40,56},{48,64},{56,72},{64,... | collective-permute-start | bytes 798728 | tf_op jit(solution)/shard_map/ppermute | solution.py:18
  138.8 16.7 %copy-start.8 = (f32[4,256,8,64]{1,0,3,2:T(4,128)S(1)}, f32[4,256,8,64]{1,0,3,2:T(4,128)}, u32[]{:S(2)}) copy-start(f32[4,256,8,64]{1,0,3,2:T(4,128)} %get-tuple-element.20) | copy-start | bytes 6291460
  138.8 14.6 %collective-permute-start.5 = (f32[8,65,128]{2,1,0:T(8,128)S(1)}, f32[8,65,128]{2,1,0:T(8,128)S(1)}, u32[]{:S(2)}, u32[]{:S(2)}) collective-permute-start(f32[8,65,128]{2,1,0:T(8,128)S(1)} %maximum_select_fusion.2), channel_id=1, source_target_pairs={{0,32},{8,40},{16,48},{24,56},{32,64},{40,72},{48,80},{56,88},{64,... | collective-permute-start | bytes 798728 | tf_op jit(solution)/shard_map/ppermute | solution.py:18
  153.6 12.2 %collective-permute-start.6 = (f32[8,65,128]{2,1,0:T(8,128)S(1)}, f32[8,65,128]{2,1,0:T(8,128)S(1)}, u32[]{:S(2)}, u32[]{:S(2)}) collective-permute-start(f32[8,65,128]{2,1,0:T(8,128)S(1)} %maximum_select_fusion.3), channel_id=1, source_target_pairs={{0,64},{8,72},{16,80},{24,88},{32,96},{40,104},{48,112},{56,120},{... | collective-permute-start | bytes 798728 | tf_op jit(solution)/shard_map/ppermute | solution.py:18
  155.5 10.1 %copy-start.11 = (f32[8]{0:T(128)S(1)}, f32[8]{0:T(128)}, u32[]{:S(2)}) copy-start(f32[8]{0:T(128)} %copy-done.10) | copy-start | bytes 100
  165.6 1.0 copy-start.4
  165.6 0.9 copy-start.13
  165.6 1.7 copy-start.9
  168.5 1.6 copy-start.1
  168.5 1.6 copy-start.21
  171.0 1.7 copy-start.24
  176.9 87.1 %reduce-scatter.5.cloned.1.call-start = ((), (), s32[]{:S(2)}) async-start(), calls=%async_computation.4 | async-start | bytes 2396160 | tf_op jit(solution)/shard_map/reduce_scatter | solution.py:177
Sparse Core Ops, SparseCore 0:
  9.7 62.5 all-gather.1
  177.0 42.6 reduce-scatter.2
  222.2 41.7 reduce-scatter.4

commit v4 on v2

--- a/solution.py
+++ b/solution.py
@@ -5,6 +5,7 @@
 
 GROUP = 256
 INNER = 4096
+LONG = 16384
 
 
 EPSILON = 1e-05
@@ -135,21 +136,33 @@
     blocks_n = lax.axis_size("seq")
     gain_row = jnp.broadcast_to(running_gain[:, None, None], (heads_here, 1, state_width))
     packed = jnp.concatenate([running_state, gain_row], 1)
-    prefix = shifted(packed, "seq", 1)
-    prefix = jnp.where(device > 0, prefix, jnp.concatenate([0.0 * running_state, 1.0 + 0.0 * gain_row], 1))
-    reach = 1
-    while reach < blocks_n:
-        earlier_part = shifted(prefix, "seq", reach)
-        later_gain = prefix[:, head_width:, :]
-        joined_part = jnp.concatenate(
+    identity = jnp.concatenate([0.0 * running_state, 1.0 + 0.0 * gain_row], 1)
+
+    def joined_of(earlier_part, later_part):
+        later_gain = later_part[:, head_width:, :]
+        return jnp.concatenate(
             [
-                later_gain * earlier_part[:, :head_width, :] + prefix[:, :head_width, :],
+                later_gain * earlier_part[:, :head_width, :] + later_part[:, :head_width, :],
                 later_gain * earlier_part[:, head_width:, :],
             ],
             1,
         )
-        prefix = jnp.where(device >= reach, joined_part, prefix)
-        reach *= 2
+
+    def fetched(part, by):
+        return jnp.where(device >= by, shifted(part, "seq", by), identity)
+
+    depth = min(blocks_n, LONG // rows_here)
+    span = 1
+    while span * span < depth:
+        span += 1
+    recent = identity
+    for by in range(span, 0, -1):
+        if by < blocks_n:
+            recent = joined_of(recent, fetched(packed, by))
+    prefix = recent
+    for hop in range(1, (depth + span - 1) // span):
+        if hop * span < blocks_n:
+            prefix = joined_of(fetched(recent, hop * span), prefix)
     incoming = prefix[:, :head_width, :]
     entering = jnp.stack(gain_list, 0)[:, :, None, None] * incoming[None] + jnp.stack(local_list, 0)
     enter_weight = jnp.where((group_ids == prior_ids[:, None])[:, :, None], jnp.exp(cumul), 0.0)
@@ -161,8 +174,8 @@
     ssd_out = (within + carried).reshape(rows_here, heads_here, head_width) + skip_gain[
         None, :, None
     ] * x_float
+    heads_n = lax.axis_size("head")
     gated = ssd_out.reshape(rows_here, inner_here) * jax.nn.silu(gate_full)
-    heads_n = lax.axis_size("head")
     scaled = (gated * norm_gain).astype(jnp.bfloat16)
     partial_out = jnp.dot(scaled, w_out, preferred_element_type=jnp.float32)
     cols = partial_out.shape[1] // heads_n

time: 273 us -> 262 us (0.960)
  matrix products: 36.5 us -> 31.3 us
  waiting for transfers between devices: 137 us -> 132 us
    reduce_sum x0 -> x1, other arithmetic: none -> 8.66 us  [shards(): square_rows = jnp.sum(gated * gated, axis=1).reshape(-1, cols)]
    dot_general x4, matrix products: 17.5 us -> 13.3 us  [partial_product(): return jnp.dot(piece, matrix, preferred_element_type=jnp.float32)]
    add x6 -> x2, other arithmetic: 3.03 us -> 0.1 us  [the longest x1 0.09 us: joined_of(): later_gain * earlier_part[:, :head_width, :] + later_part[:, :head_width, :]]
    ppermute x8 -> x9, waiting for transfers between devices: 18.2 us -> 16 us  [shifted(): return lax.ppermute(x, axis, pairs)]
    ppermute x8 -> x9, starting transfers between devices: 36.9 us -> 35.1 us  [shifted(): return lax.ppermute(x, axis, pairs)]
  transfers between devices with their start and end apart: 10 -> 11, of which waited for: 7 -> 6; matrix products, arithmetic and copies ran while one was open for 9% -> 10% of each run, Pallas kernels for 0% -> 0%
where the time goes in v4:
time: 262 us
  waiting for transfers between devices  132 us (50%)
  starting transfers between devices  35.2 us (13%)
  matrix products  31.3 us (12%)
  other arithmetic  27.2 us (10%)
  local copies, waits for them, and re-layouts  20.9 us (8%)
  between operations  14.5 us (6%)
    reduce_scatter x1, waiting for transfers between devices, shards(): lax.psum_scatter(joined.astype(jnp.bfloat16), 'head', scatter_dimension=1...  58.3 us
    all_gather x1, waiting for transfers between devices, shards(): piece = lax.all_gather(tokens, 'head', axis=1, tiled=True)  57.4 us
    ppermute x9, starting transfers between devices, shifted(): return lax.ppermute(x, axis, pairs)  35.1 us
    ppermute x9, waiting for transfers between devices, shifted(): return lax.ppermute(x, axis, pairs)  16 us
    dot_general x4, matrix products, partial_product(): return jnp.dot(piece, matrix, preferred_element_type=jnp.float32)  13.3 us
    dot_general x1, matrix products, shards(): jnp.einsum('chts,cshp->cthp', decays * scores[:, None, :, :], group_x, pr...  10.1 us
    reduce_sum x1, other arithmetic, shards(): square_rows = jnp.sum(gated * gated, axis=1).reshape(-1, cols)  8.66 us
    reshape x2, local copies, waits for them, and re-layouts, shards(): (within + carried).reshape(rows_here, heads_here, head_width)  8.61 us
  transfers between devices with their start and end apart: 11, of which 6 were waited for; matrix products, arithmetic and copies ran while one was open for 10% of the time, Pallas kernels for 0%

profile of v4, /device:TPU:1, one launch (start us, length us, event | category | flops | bytes accessed | tf_op | source)
XLA Modules:
  0.0 261.6 jit_solution(2966265363044667161)
XLA Ops:
  7.2 0.7 all-gather.2.cloned.1.call-update
  8.0 0.8 broadcast_select_fusion.6
  8.8 0.6 slice.196
  9.4 0.7 dynamic_slice.7
  10.1 0.7 mul.484
  11.0 0.7 pad_add_fusion.1
  11.9 0.8 fusion.63
  13.0 0.8 fusion.74
  13.8 0.9 fusion.72
  14.9 57.4 %all-gather.2.cloned.1.call-done = bf16[1024,2048]{1,0:T(8,128)(2,1)} async-done(((bf16[1024,256]{1,0:T(8,128)(2,1)}), bf16[1024,2048]{1,0:T(8,128)(2,1)}) %all-gather.2.cloned.1.call-update) | async-done | bytes 4194320 | tf_op jit(solution)/shard_map/all_gather | solution.py:76
  72.3 3.4 %negate_multiply_fusion = (f32[1024,8]{0,1:T(8,128)S(1)}, f32[1024,8]{0,1:T(8,128)S(1)}) fusion(f32[8]{0:T(128)} %param.26, f32[8]{0:T(128)} %param.25, bf16[1024,2048]{1,0:T(8,128)(2,1)} %all-gather.2.cloned.1.call-done, bf16[2048,8]{0,1:T(8,128)(2,1)} %param.20), kind=kOutput, calls=%fused_computation.109 | convolution fusion | flops 33628160 | bytes 4292672 | tf_op jit(solution)/shard_map/dot_general | solution.py:79
  75.7 2.3 reduce-window.6
  78.7 3.9 %convolution_convert_fusion.2 = bf16[1024,256]{1,0:T(8,128)(2,1)S(1)} fusion(bf16[1024,2048]{1,0:T(8,128)(2,1)} %all-gather.2.cloned.1.call-done, bf16[2048,256]{1,0:T(8,128)(2,1)} %param.19), kind=kOutput, calls=%fused_computation.33 | convolution fusion | flops 1074003968 | bytes 5767168 | tf_op jit(solution)/shard_map/dot_general | solution.py:79
  82.6 7.5 %collective-permute-start.1 = (bf16[3,256]{1,0:T(4,128)(2,1)S(1)}, bf16[3,256]{1,0:T(4,128)(2,1)S(1)}, u32[]{:S(2)}, u32[]{:S(2)}) collective-permute-start(bf16[3,256]{1,0:T(4,128)(2,1)S(1)} %slice.235), channel_id=1, source_target_pairs={{0,8},{8,16},{16,24},{24,32},{32,40},{40,48},{48,56},{56,64},{64,7... | collective-permute-start | bytes 4616 | tf_op jit(solution)/shard_map/ppermute | solution.py:18
  90.2 2.3 convolution_convert_fusion.1
  92.5 3.7 %fusion.77 = f32[1024,512]{1,0:T(8,128)} fusion(bf16[1024,2048]{1,0:T(8,128)(2,1)S(1)} %copy-done.2, bf16[2048,512]{1,0:T(8,128)(2,1)S(1)} %copy-done.6), kind=kOutput, calls=%fused_computation.162 | convolution fusion | flops 2147483648 | bytes 8388608 | tf_op jit(solution)/shard_map/dot_general | solution.py:79
  96.3 1.9 collective-permute-start
  98.3 1.3 multiply_convert_fusion.3
  99.8 0.3 maximum_convert_fusion
  100.1 1.4 copy-done.1
  101.4 3.1 %fusion.36 = f32[1024,512]{1,0:T(8,128)} fusion(f32[512]{0:T(512)S(1)} %copy-done.3, f32[512]{0:T(512)S(1)} %bitcast.131, f32[1027,512]{1,0:T(8,128)S(1)} %maximum_convert_fusion, pred[1024]{0:T(1024)(128)(4,1)S(1)} %get-tuple-element.39, f32[512]{0:T(512)S(1)} %bitcast.133, pred[1024]{0:T(1024)(128)(4,1)S(1)} %get-tuple-element.40, f32[512]{0:T(512)S(1)} %bitcast.129, ...), kind=kLoop, calls=%fused_computation.61 | loop fusion | flops 8912896 | bytes 10499072 | tf_op jit(solution)/shard_map/convert_element_type | solution.py:101
  104.5 2.9 %copy.64 = f32[1024,512]{0,1:T(8,128)} copy(f32[1024,512]{1,0:T(8,128)} %fusion.36) | data formatting | bytes 4194304 | tf_op jit(solution)/shard_map/convert_element_type | solution.py:101
  107.4 3.2 %reshape.200 = f32[4,256,8,64]{1,0,3,2:T(4,128)} reshape(f32[1024,512]{0,1:T(8,128)} %copy.64) | data formatting | bytes 4194304 | tf_op jit(solution)/shard_map/reshape | solution.py:101
  110.6 2.4 broadcast_multiply_fusion
  113.0 1.3 fusion.18
  114.6 4.4 %collective-permute-start.5 = (f32[8,65,128]{2,1,0:T(8,128)S(1)}, f32[8,65,128]{2,1,0:T(8,128)S(1)}, u32[]{:S(2)}, u32[]{:S(2)}) collective-permute-start(f32[8,65,128]{2,1,0:T(8,128)S(1)} %pad_maximum_fusion.2), channel_id=1, source_target_pairs={{0,32},{8,40},{16,48},{24,56},{32,64},{40,72},{48,80},{56,88},{64,... | collective-permute-start | bytes 798728 | tf_op jit(solution)/shard_map/ppermute | solution.py:18
  118.9 6.0 %collective-permute-start.4 = (f32[8,65,128]{2,1,0:T(8,128)S(1)}, f32[8,65,128]{2,1,0:T(8,128)S(1)}, u32[]{:S(2)}, u32[]{:S(2)}) collective-permute-start(f32[8,65,128]{2,1,0:T(8,128)S(1)} %pad_maximum_fusion.2), channel_id=1, source_target_pairs={{0,24},{8,32},{16,40},{24,48},{32,56},{40,64},{48,72},{56,80},{64,... | collective-permute-start | bytes 798728 | tf_op jit(solution)/shard_map/ppermute | solution.py:18
  124.9 1.3 collective-permute-start.3
  126.2 2.5 collective-permute-start.2
  128.8 0.3 fusion.76
  129.1 2.6 collective-permute-done.4
  131.7 6.3 %collective-permute-done.3 = f32[8,65,128]{2,1,0:T(8,128)S(1)} collective-permute-done((f32[8,65,128]{2,1,0:T(8,128)S(1)}, f32[8,65,128]{2,1,0:T(8,128)S(1)}, u32[]{:S(2)}, u32[]{:S(2)}) %collective-permute-start.3) | collective-permute-done | bytes 266272 | tf_op jit(solution)/shard_map/ppermute | solution.py:18
  138.0 3.5 %collective-permute-done.2 = f32[8,65,128]{2,1,0:T(8,128)S(1)} collective-permute-done((f32[8,65,128]{2,1,0:T(8,128)S(1)}, f32[8,65,128]{2,1,0:T(8,128)S(1)}, u32[]{:S(2)}, u32[]{:S(2)}) %collective-permute-start.2) | collective-permute-done | bytes 266272 | tf_op jit(solution)/shard_map/ppermute | solution.py:18
  142.0 3.1 %collective-permute-start.7 = (f32[8,65,128]{2,1,0:T(8,128)S(1)}, f32[8,65,128]{2,1,0:T(8,128)S(1)}, u32[]{:S(2)}, u32[]{:S(2)}) collective-permute-start(f32[8,65,128]{2,1,0:T(8,128)S(1)} %pad_maximum_fusion.3), channel_id=1, source_target_pairs={{0,64},{8,72},{16,80},{24,88},{32,96},{40,104},{48,112},{56,120},{... | collective-permute-start | bytes 798728 | tf_op jit(solution)/shard_map/ppermute | solution.py:18
  145.1 3.6 %collective-permute-start.6 = (f32[8,65,128]{2,1,0:T(8,128)S(1)}, f32[8,65,128]{2,1,0:T(8,128)S(1)}, u32[]{:S(2)}, u32[]{:S(2)}) collective-permute-start(f32[8,65,128]{2,1,0:T(8,128)S(1)} %pad_maximum_fusion.3), channel_id=1, source_target_pairs={{0,32},{8,40},{16,48},{24,56},{32,64},{40,72},{48,80},{56,88},{64,... | collective-permute-start | bytes 798728 | tf_op jit(solution)/shard_map/ppermute | solution.py:18
  148.7 10.1 %fusion = f32[4,8,64,256]{3,2,1,0:T(8,128)S(1)} fusion(f32[4,256,256]{2,1,0:T(8,128)S(1)} %fusion.76, f32[4,8,256]{2,1,0:T(8,128)S(1)} %add_bitcast_fusion.2, pred[4,256,256]{2,1,0:T(8,128)(4,1)S(1)} %compare_and_fusion, f32[4,256,8,64]{1,0,3,2:T(4,128)S(1)} %get-tuple-element.20), kind=kOutput, calls=%fused_computation | convolution fusion | flops 1619001344 | bytes 5537792 | tf_op jit(solution)/shard_map/chts,cshp->cthp/dot_general | solution.py:117
  158.9 4.9 %collective-permute-start.8 = (f32[8,65,128]{2,1,0:T(8,128)S(1)}, f32[8,65,128]{2,1,0:T(8,128)S(1)}, u32[]{:S(2)}, u32[]{:S(2)}) collective-permute-start(f32[8,65,128]{2,1,0:T(8,128)S(1)} %pad_maximum_fusion.3), channel_id=1, source_target_pairs={{0,96},{8,104},{16,112},{24,120},{32,128},{40,136},{48,144},{56,15... | collective-permute-start | bytes 798728 | tf_op jit(solution)/shard_map/ppermute | solution.py:18
  163.9 3.5 %collective-permute-done.8 = f32[8,65,128]{2,1,0:T(8,128)S(1)} collective-permute-done((f32[8,65,128]{2,1,0:T(8,128)S(1)}, f32[8,65,128]{2,1,0:T(8,128)S(1)}, u32[]{:S(2)}, u32[]{:S(2)}) %collective-permute-start.8) | collective-permute-done | bytes 266272 | tf_op jit(solution)/shard_map/ppermute | solution.py:18
  167.4 0.8 add_bitcast_fusion
  168.2 2.5 bitcast_add_fusion
  170.7 3.8 %copy.78 = f32[4,256,8,64]{3,2,1,0:T(8,128)} copy(f32[4,256,8,64]{1,3,2,0:T(8,128)} %bitcast_add_fusion) | data formatting | bytes 4194304 | tf_op jit(solution)/shard_map/reshape | solution.py:174
  174.5 4.8 %reshape.210 = f32[1024,512]{1,0:T(8,128)} reshape(f32[4,256,8,64]{3,2,1,0:T(8,128)} %copy.78) | data formatting | bytes 4194304 | tf_op jit(solution)/shard_map/reshape | solution.py:174
  179.3 8.7 %multiply_reduce_fusion = (bf16[1024]{0:T(1024)(128)(2,1)S(1)}, f32[1024,512]{1,0:T(8,128)}) fusion(f32[1024,512]{1,0:T(8,128)} %fusion.77, f32[1024,512]{1,0:T(8,128)} %reshape.210, f32[512]{0:T(512)S(1)} %mul.485, f32[512]{0:T(512)S(1)} %copy-done.3, f32[512]{0:T(512)S(1)} %bitcast.132, f32[1027,512]{1,0:T(8,128)} %copy-done.1, ...), kind=kLoop, calls=%fused_computation.28 | loop fusion | flops 13630464 | bytes 14697472 | tf_op jit(solution)/shard_map/reduce_sum | solution.py:182
  188.0 3.9 %convolution_convert_fusion = bf16[1024,2048]{1,0:T(8,128)(2,1)S(1)} fusion(bf16[512,2048]{1,0:T(8,128)(2,1)S(1)} %copy-done, f32[1024,512]{1,0:T(8,128)} %get-tuple-element.5, f32[512]{0:T(512)S(1)} %copy-done.7), kind=kOutput, calls=%fused_computation.12 | convolution fusion | flops 2150629376 | bytes 8390656 | tf_op jit(solution)/shard_map/dot_general | solution.py:180
  191.9 2.3 pad_maximum_fusion
  194.3 58.3 %reduce-scatter.2.cloned.1.call-done = bf16[1028,256]{1,0:T(8,128)(2,1)} async-done(((bf16[1028,2048]{1,0:T(8,128)(2,1)}), bf16[1028,256]{1,0:T(8,128)(2,1)}) %reduce-scatter.2.cloned.1.call-update) | async-done | bytes 526352 | tf_op jit(solution)/shard_map/reduce_scatter | solution.py:184
  252.6 1.1 convert_element_type.41
  253.7 1.0 fusion.21
  (68 shorter events, 2.8 us)
Async XLA Ops:
  7.2 180.8 %copy-start = (bf16[512,2048]{1,0:T(8,128)(2,1)S(1)}, bf16[512,2048]{1,0:T(8,128)(2,1)}, u32[]{:S(2)}) copy-start(bf16[512,2048]{1,0:T(8,128)(2,1)} %param.29) | copy-start | bytes 6291460
  7.2 65.1 %all-gather.2.cloned.1.call-start = ((), (), s32[]{:S(2)}) async-start(), calls=%async_computation.1 | async-start | bytes 4718592 | tf_op jit(solution)/shard_map/all_gather | solution.py:76
  7.9 244.7 %reduce-scatter.2.cloned.1.call-start = ((), (), s32[]{:S(2)}) async-start(), calls=%async_computation.2 | async-start | bytes 4755456 | tf_op jit(solution)/shard_map/reduce_scatter | solution.py:184
  78.7 11.5 %copy-start.2 = (bf16[1024,2048]{1,0:T(8,128)(2,1)S(1)}, bf16[1024,2048]{1,0:T(8,128)(2,1)}, u32[]{:S(2)}) copy-start(bf16[1024,2048]{1,0:T(8,128)(2,1)} %all-gather.2.cloned.1.call-done) | copy-start | bytes 12582916
  78.7 11.5 %copy-start.5 = (bf16[2048,512]{1,0:T(8,128)(2,1)S(1)}, bf16[2048,512]{1,0:T(8,128)(2,1)}, u32[]{:S(2)}) copy-start(bf16[2048,512]{1,0:T(8,128)(2,1)} %param.18) | copy-start | bytes 6291460
  82.6 9.9 %copy-start.6 = (bf16[2048,512]{1,0:T(8,128)(2,1)S(1)}, bf16[2048,512]{1,0:T(8,128)(2,1)}, u32[]{:S(2)}) copy-start(bf16[2048,512]{1,0:T(8,128)(2,1)} %param.17) | copy-start | bytes 6291460
  82.6 15.6 %collective-permute-start.1 = (bf16[3,256]{1,0:T(4,128)(2,1)S(1)}, bf16[3,256]{1,0:T(4,128)(2,1)S(1)}, u32[]{:S(2)}, u32[]{:S(2)}) collective-permute-start(bf16[3,256]{1,0:T(4,128)(2,1)S(1)} %slice.235), channel_id=1, source_target_pairs={{0,8},{8,16},{16,24},{24,32},{32,40},{40,48},{48,56},{56,64},{64,7... | collective-permute-start | bytes 4616 | tf_op jit(solution)/shard_map/ppermute | solution.py:18
  92.5 5.8 %copy-start.4 = (f32[256]{0:T(256)S(1)}, f32[256]{0:T(256)}, u32[]{:S(2)}) copy-start(f32[256]{0:T(256)} %param.24) | copy-start | bytes 3076
  96.3 3.5 %collective-permute-start = (bf16[3,512]{1,0:T(4,128)(2,1)S(1)}, bf16[3,512]{1,0:T(4,128)(2,1)S(1)}, u32[]{:S(2)}, u32[]{:S(2)}) collective-permute-start(bf16[3,512]{1,0:T(4,128)(2,1)S(1)} %slice.224), channel_id=1, source_target_pairs={{0,8},{8,16},{16,24},{24,32},{32,40},{40,48},{48,56},{56,64},{64,7... | collective-permute-start | bytes 9224 | tf_op jit(solution)/shard_map/ppermute | solution.py:18
  99.7 1.8 copy-start.3
  100.1 1.4 copy-start.1
  114.6 14.5 %collective-permute-start.5 = (f32[8,65,128]{2,1,0:T(8,128)S(1)}, f32[8,65,128]{2,1,0:T(8,128)S(1)}, u32[]{:S(2)}, u32[]{:S(2)}) collective-permute-start(f32[8,65,128]{2,1,0:T(8,128)S(1)} %pad_maximum_fusion.2), channel_id=1, source_target_pairs={{0,32},{8,40},{16,48},{24,56},{32,64},{40,72},{48,80},{56,88},{64,... | collective-permute-start | bytes 798728 | tf_op jit(solution)/shard_map/ppermute | solution.py:18
  118.9 12.8 %collective-permute-start.4 = (f32[8,65,128]{2,1,0:T(8,128)S(1)}, f32[8,65,128]{2,1,0:T(8,128)S(1)}, u32[]{:S(2)}, u32[]{:S(2)}) collective-permute-start(f32[8,65,128]{2,1,0:T(8,128)S(1)} %pad_maximum_fusion.2), channel_id=1, source_target_pairs={{0,24},{8,32},{16,40},{24,48},{32,56},{40,64},{48,72},{56,80},{64,... | collective-permute-start | bytes 798728 | tf_op jit(solution)/shard_map/ppermute | solution.py:18
  124.9 13.1 %collective-permute-start.3 = (f32[8,65,128]{2,1,0:T(8,128)S(1)}, f32[8,65,128]{2,1,0:T(8,128)S(1)}, u32[]{:S(2)}, u32[]{:S(2)}) collective-permute-start(f32[8,65,128]{2,1,0:T(8,128)S(1)} %pad_maximum_fusion.2), channel_id=1, source_target_pairs={{0,16},{8,24},{16,32},{24,40},{32,48},{40,56},{48,64},{56,72},{64,... | collective-permute-start | bytes 798728 | tf_op jit(solution)/shard_map/ppermute | solution.py:18
  126.2 15.3 %collective-permute-start.2 = (f32[8,65,128]{2,1,0:T(8,128)S(1)}, f32[8,65,128]{2,1,0:T(8,128)S(1)}, u32[]{:S(2)}, u32[]{:S(2)}) collective-permute-start(f32[8,65,128]{2,1,0:T(8,128)S(1)} %pad_maximum_fusion.2), channel_id=1, source_target_pairs={{0,8},{8,16},{16,24},{24,32},{32,40},{40,48},{48,56},{56,64},{64,7... | collective-permute-start | bytes 798728 | tf_op jit(solution)/shard_map/ppermute | solution.py:18
  142.0 21.8 %collective-permute-start.7 = (f32[8,65,128]{2,1,0:T(8,128)S(1)}, f32[8,65,128]{2,1,0:T(8,128)S(1)}, u32[]{:S(2)}, u32[]{:S(2)}) collective-permute-start(f32[8,65,128]{2,1,0:T(8,128)S(1)} %pad_maximum_fusion.3), channel_id=1, source_target_pairs={{0,64},{8,72},{16,80},{24,88},{32,96},{40,104},{48,112},{56,120},{... | collective-permute-start | bytes 798728 | tf_op jit(solution)/shard_map/ppermute | solution.py:18
  145.1 18.7 %collective-permute-start.6 = (f32[8,65,128]{2,1,0:T(8,128)S(1)}, f32[8,65,128]{2,1,0:T(8,128)S(1)}, u32[]{:S(2)}, u32[]{:S(2)}) collective-permute-start(f32[8,65,128]{2,1,0:T(8,128)S(1)} %pad_maximum_fusion.3), channel_id=1, source_target_pairs={{0,32},{8,40},{16,48},{24,56},{32,64},{40,72},{48,80},{56,88},{64,... | collective-permute-start | bytes 798728 | tf_op jit(solution)/shard_map/ppermute | solution.py:18
  158.9 8.5 %collective-permute-start.8 = (f32[8,65,128]{2,1,0:T(8,128)S(1)}, f32[8,65,128]{2,1,0:T(8,128)S(1)}, u32[]{:S(2)}, u32[]{:S(2)}) collective-permute-start(f32[8,65,128]{2,1,0:T(8,128)S(1)} %pad_maximum_fusion.3), channel_id=1, source_target_pairs={{0,96},{8,104},{16,112},{24,120},{32,128},{40,136},{48,144},{56,15... | collective-permute-start | bytes 798728 | tf_op jit(solution)/shard_map/ppermute | solution.py:18
  179.3 8.7 %copy-start.7 = (f32[512]{0:T(512)S(1)}, f32[512]{0:T(512)}, u32[]{:S(2)}) copy-start(f32[512]{0:T(512)} %param.28) | copy-start | bytes 6148
Sparse Core Ops, SparseCore 0:
  9.7 62.5 all-gather.1
  194.4 58.1 reduce-scatter.1

commit v5 on v4

--- a/solution.py
+++ b/solution.py
@@ -171,15 +171,20 @@
         * enter_weight[:, :, :, None]
     )
     end_state = (running_gain[:, None, None] * incoming + running_state)[None]
-    ssd_out = (within + carried).reshape(rows_here, heads_here, head_width) + skip_gain[
-        None, :, None
-    ] * x_float
     heads_n = lax.axis_size("head")
-    gated = ssd_out.reshape(rows_here, inner_here) * jax.nn.silu(gate_full)
-    scaled = (gated * norm_gain).astype(jnp.bfloat16)
-    partial_out = jnp.dot(scaled, w_out, preferred_element_type=jnp.float32)
+    group_shape = (count, GROUP, heads_here, head_width)
+    gate_act = jax.nn.silu(gate_full).reshape(group_shape)
+    direct = skip_gain[:, None] * x_float.reshape(group_shape)
+    gated = (within + carried + direct) * gate_act
+    scaled = (gated * norm_gain.reshape(heads_here, head_width)).astype(jnp.bfloat16)
+    partial_out = jnp.einsum(
+        "cthp,hpo->cto",
+        scaled,
+        w_out.reshape(heads_here, head_width, w_out.shape[1]),
+        preferred_element_type=jnp.float32,
+    ).reshape(rows_here, w_out.shape[1])
     cols = partial_out.shape[1] // heads_n
-    square_rows = jnp.sum(gated * gated, axis=1).reshape(-1, cols)
+    square_rows = jnp.sum(gated * gated, axis=(2, 3)).reshape(-1, cols)
     joined = jnp.concatenate([partial_out, jnp.tile(square_rows, (1, heads_n))], 0)
     summed = lax.psum_scatter(
         joined.astype(jnp.bfloat16), "head", scatter_dimension=1, tiled=True

time: 262 us -> 248 us (0.947)
  waiting for transfers between devices: 132 us -> 123 us
  other arithmetic: 27.2 us -> 22.6 us
    ppermute x9, waiting for transfers between devices: 16 us -> 6.79 us  [shifted(): return lax.ppermute(x, axis, pairs)]
    reduce_sum x1 -> x0, other arithmetic: 8.66 us -> none  [shards(): square_rows = jnp.sum(gated * gated, axis=1).reshape(-1, cols)]
    reshape x0 -> x1, other arithmetic: none -> 3.11 us  [shards(): x_conv.astype(jnp.float32).reshape(rows_here, heads_here, head_width)]
    convert_element_type x1 -> x0, other arithmetic: 3.08 us -> none  [shards(): x_conv.astype(jnp.float32).reshape(rows_here, heads_here, head_width)]
    convert_element_type x1 -> x0, local copies, waits for them, and re-layouts: 2.91 us -> none  [shards(): x_conv.astype(jnp.float32).reshape(rows_here, heads_here, head_width)]
    reshape x1 -> x2, local copies, waits for them, and re-layouts: 3.18 us -> 6.07 us  [shards(): x_conv.astype(jnp.float32).reshape(rows_here, heads_here, head_width)]
  transfers between devices with their start and end apart: 11 -> 11, of which waited for: 6 -> 4; matrix products, arithmetic and copies ran while one was open for 10% -> 14% of each run, Pallas kernels for 0% -> 0%
where the time goes in v5:
time: 248 us; the launch traced here: 247 us
  waiting for transfers between devices  123 us (50%)
  starting transfers between devices  35.7 us (14%)
  matrix products  30.9 us (12%)
  other arithmetic  22.6 us (9%)
  local copies, waits for them, and re-layouts  20.6 us (8%)
  between operations  14.5 us (6%)
    reduce_scatter x1, waiting for transfers between devices, shards(): lax.psum_scatter(joined.astype(jnp.bfloat16), 'head', scatter_dimension=1...  58.3 us
    all_gather x1, waiting for transfers between devices, shards(): piece = lax.all_gather(tokens, 'head', axis=1, tiled=True)  56.7 us
    ppermute x9, starting transfers between devices, shifted(): return lax.ppermute(x, axis, pairs)  35.7 us
    dot_general x4, matrix products, partial_product(): return jnp.dot(piece, matrix, preferred_element_type=jnp.float32)  14 us
    dot_general x1, matrix products, shards(): jnp.einsum('chts,cshp->cthp', decays * scores[:, None, :, :], group_x, pr...  10.1 us
    reshape x2, local copies, waits for them, and re-layouts, shards(): gate_act = jax.nn.silu(gate_full).reshape(group_shape)  8.26 us
    ppermute x9, waiting for transfers between devices, shifted(): return lax.ppermute(x, axis, pairs)  6.79 us
    reshape x2, local copies, waits for them, and re-layouts, shards(): x_conv.astype(jnp.float32).reshape(rows_here, heads_here, head_width)  6.07 us
  transfers between devices with their start and end apart: 11, of which 4 were waited for; matrix products, arithmetic and copies ran while one was open for 14% of the time, Pallas kernels for 0%

profile of v5, /device:TPU:1, one launch (start us, length us, event | category | flops | bytes accessed | tf_op | source)
XLA Modules:
  0.0 246.9 jit_solution(11101362550842569108)
XLA Ops:
  7.2 0.7 all-gather.2.cloned.1.call-update
  8.0 0.8 mul.485
  8.7 0.7 dynamic_slice.7
  9.4 0.8 broadcast_select_fusion.6
  10.2 0.6 slice.196
  11.0 0.7 pad_add_fusion.1
  11.9 0.8 fusion.65
  12.9 0.8 fusion.76
  13.7 0.9 fusion.74
  14.6 1.0 compare_and_fusion
  15.5 56.7 %all-gather.2.cloned.1.call-done = bf16[1024,2048]{1,0:T(8,128)(2,1)} async-done(((bf16[1024,256]{1,0:T(8,128)(2,1)}), bf16[1024,2048]{1,0:T(8,128)(2,1)}) %all-gather.2.cloned.1.call-update) | async-done | bytes 4194320 | tf_op jit(solution)/shard_map/all_gather | solution.py:76
  72.3 3.4 %negate_multiply_fusion = (f32[1024,8]{0,1:T(8,128)S(1)}, f32[1024,8]{0,1:T(8,128)S(1)}) fusion(f32[8]{0:T(128)} %param.26, f32[8]{0:T(128)} %param.25, bf16[1024,2048]{1,0:T(8,128)(2,1)} %all-gather.2.cloned.1.call-done, bf16[2048,8]{0,1:T(8,128)(2,1)} %param.20), kind=kOutput, calls=%fused_computation.112 | convolution fusion | flops 33628160 | bytes 4292672 | tf_op jit(solution)/shard_map/dot_general | solution.py:79
  75.7 2.3 reduce-window.6
  78.6 5.3 %convolution_convert_fusion = bf16[1024,512]{1,0:T(8,128)(2,1)S(1)} fusion(bf16[1024,2048]{1,0:T(8,128)(2,1)} %all-gather.2.cloned.1.call-done, bf16[2048,512]{1,0:T(8,128)(2,1)} %param.18), kind=kOutput, calls=%fused_computation.35 | convolution fusion | flops 2148007936 | bytes 7340032 | tf_op jit(solution)/shard_map/dot_general | solution.py:79
  84.0 7.5 %collective-permute-start = (bf16[3,512]{1,0:T(4,128)(2,1)S(1)}, bf16[3,512]{1,0:T(4,128)(2,1)S(1)}, u32[]{:S(2)}, u32[]{:S(2)}) collective-permute-start(bf16[3,512]{1,0:T(4,128)(2,1)S(1)} %slice.224), channel_id=1, source_target_pairs={{0,8},{8,16},{16,24},{24,32},{32,40},{40,48},{48,56},{56,64},{64,7... | collective-permute-start | bytes 9224 | tf_op jit(solution)/shard_map/ppermute | solution.py:18
  91.5 1.2 convolution_convert_fusion.1
  92.8 1.9 collective-permute-start.1
  94.7 4.0 %divide_multiply_fusion = f32[1024,512]{1,0:T(8,128)} fusion(bf16[1024,2048]{1,0:T(8,128)(2,1)S(1)} %copy-done.3, bf16[2048,512]{1,0:T(8,128)(2,1)S(1)} %copy-done.13), kind=kOutput, calls=%fused_computation.33 | convolution fusion | flops 2149580800 | bytes 8388608 | tf_op jit(solution)/shard_map/dot_general | solution.py:79
  99.0 1.3 multiply_convert_fusion.2
  100.4 0.7 fusion.73
  101.4 3.1 %fusion.38 = f32[1024,512]{1,0:T(8,128)} fusion(f32[512]{0:T(512)S(1)} %copy-done.10, f32[512]{0:T(512)S(1)} %bitcast.149, f32[1027,512]{1,0:T(8,128)S(1)} %maximum_convert_fusion, pred[1024]{0:T(1024)(128)(4,1)S(1)} %get-tuple-element.39, f32[512]{0:T(512)S(1)} %bitcast.150, pred[1024]{0:T(1024)(128)(4,1)S(1)} %get-tuple-element.40, f32[512]{0:T(512)S(1)} %bitcast.148, ...), kind=kLoop, calls=%fused_computation.64 | loop fusion | flops 8912896 | bytes 10499072 | tf_op jit(solution)/shard_map/reshape | solution.py:101
  104.5 2.9 %copy.63 = f32[1024,512]{0,1:T(8,128)} copy(f32[1024,512]{1,0:T(8,128)} %fusion.38) | data formatting | bytes 4194304 | tf_op jit(solution)/shard_map/reshape | solution.py:101
  107.4 3.2 %reshape.215 = f32[4,256,8,64]{1,0,3,2:T(4,128)} reshape(f32[1024,512]{0,1:T(8,128)} %copy.63) | data formatting | bytes 4194304 | tf_op jit(solution)/shard_map/reshape | solution.py:101
  110.6 3.8 %broadcast_multiply_fusion = (f32[4,256,8,64]{1,0,3,2:T(4,128)S(1)}, f32[4,256,8,64]{1,0,3,2:T(4,128)}) fusion(f32[4,256,8]{1,0,2:T(4,128)S(1)} %copy.68, f32[4,256,8,64]{1,0,3,2:T(4,128)} %reshape.215, f32[4,256,8]{1,0,2:T(4,128)S(1)} %copy.64), kind=kLoop, calls=%fused_computation.60 | loop fusion | flops 1048576 | bytes 6356992 | tf_op jit(solution)/shard_map/mul | solution.py:123
  114.4 1.3 fusion.20
  116.0 0.6 copy-done.4
  116.6 0.7 pad_maximum_fusion.2
  117.3 5.1 %collective-permute-start.5 = (f32[8,65,128]{2,1,0:T(8,128)}, f32[8,65,128]{2,1,0:T(8,128)}, u32[]{:S(2)}, u32[]{:S(2)}) collective-permute-start(f32[8,65,128]{2,1,0:T(8,128)} %pad_maximum_fusion.2), channel_id=1, source_target_pairs={{0,32},{8,40},{16,48},{24,56},{32,64},{40,72},{48,80},{56,88},{64,... | collective-permute-start | bytes 798728 | tf_op jit(solution)/shard_map/ppermute | solution.py:18
  122.4 4.0 %collective-permute-start.4 = (f32[8,65,128]{2,1,0:T(8,128)}, f32[8,65,128]{2,1,0:T(8,128)}, u32[]{:S(2)}, u32[]{:S(2)}) collective-permute-start(f32[8,65,128]{2,1,0:T(8,128)} %pad_maximum_fusion.2), channel_id=1, source_target_pairs={{0,24},{8,32},{16,40},{24,48},{32,56},{40,64},{48,72},{56,80},{64,... | collective-permute-start | bytes 798728 | tf_op jit(solution)/shard_map/ppermute | solution.py:18
  126.4 3.1 %collective-permute-start.3 = (f32[8,65,128]{2,1,0:T(8,128)}, f32[8,65,128]{2,1,0:T(8,128)}, u32[]{:S(2)}, u32[]{:S(2)}) collective-permute-start(f32[8,65,128]{2,1,0:T(8,128)} %pad_maximum_fusion.2), channel_id=1, source_target_pairs={{0,16},{8,24},{16,32},{24,40},{32,48},{40,56},{48,64},{56,72},{64,... | collective-permute-start | bytes 798728 | tf_op jit(solution)/shard_map/ppermute | solution.py:18
  129.5 2.1 collective-permute-start.2
  131.7 4.4 %reshape.219 = f32[4,256,8,64]{3,2,1,0:T(8,128)} reshape(f32[1024,512]{1,0:T(8,128)} %divide_multiply_fusion) | data formatting | bytes 4194304 | tf_op jit(solution)/shard_map/reshape | solution.py:176
  136.1 3.9 %copy.72 = f32[4,256,8,64]{1,3,2,0:T(8,128)} copy(f32[4,256,8,64]{3,2,1,0:T(8,128)} %reshape.219) | data formatting | bytes 4194304 | tf_op jit(solution)/shard_map/reshape | solution.py:176
  140.0 1.4 fusion.78
  141.4 3.2 %collective-permute-done.2 = f32[8,65,128]{2,1,0:T(8,128)} collective-permute-done((f32[8,65,128]{2,1,0:T(8,128)}, f32[8,65,128]{2,1,0:T(8,128)}, u32[]{:S(2)}, u32[]{:S(2)}) %collective-permute-start.2) | collective-permute-done | bytes 266272 | tf_op jit(solution)/shard_map/ppermute | solution.py:18
  144.7 1.2 broadcast_select_fusion.2
  146.2 3.4 %collective-permute-start.7 = (f32[8,65,128]{2,1,0:T(8,128)S(1)}, f32[8,65,128]{2,1,0:T(8,128)S(1)}, u32[]{:S(2)}, u32[]{:S(2)}) collective-permute-start(f32[8,65,128]{2,1,0:T(8,128)S(1)} %pad_maximum_fusion.3), channel_id=1, source_target_pairs={{0,64},{8,72},{16,80},{24,88},{32,96},{40,104},{48,112},{56,120},{... | collective-permute-start | bytes 798728 | tf_op jit(solution)/shard_map/ppermute | solution.py:18
  149.5 3.3 %collective-permute-start.6 = (f32[8,65,128]{2,1,0:T(8,128)S(1)}, f32[8,65,128]{2,1,0:T(8,128)S(1)}, u32[]{:S(2)}, u32[]{:S(2)}) collective-permute-start(f32[8,65,128]{2,1,0:T(8,128)S(1)} %pad_maximum_fusion.3), channel_id=1, source_target_pairs={{0,32},{8,40},{16,48},{24,56},{32,64},{40,72},{48,80},{56,88},{64,... | collective-permute-start | bytes 798728 | tf_op jit(solution)/shard_map/ppermute | solution.py:18
  152.9 10.1 %fusion = f32[4,8,64,256]{3,2,1,0:T(8,128)S(1)} fusion(f32[4,256,256]{2,1,0:T(8,128)S(1)} %fusion.78, f32[4,8,256]{2,1,0:T(8,128)S(1)} %add_bitcast_fusion.2, pred[4,256,256]{2,1,0:T(8,128)(4,1)S(1)} %copy-done.9, f32[4,256,8,64]{1,0,3,2:T(4,128)S(1)} %copy-done.8), kind=kOutput, calls=%fused_computation.1 | convolution fusion | flops 1619001344 | bytes 5537792 | tf_op jit(solution)/shard_map/chts,cshp->cthp/dot_general | solution.py:117
  163.1 5.2 %collective-permute-start.8 = (f32[8,65,128]{2,1,0:T(8,128)S(1)}, f32[8,65,128]{2,1,0:T(8,128)S(1)}, u32[]{:S(2)}, u32[]{:S(2)}) collective-permute-start(f32[8,65,128]{2,1,0:T(8,128)S(1)} %pad_maximum_fusion.3), channel_id=1, source_target_pairs={{0,96},{8,104},{16,112},{24,120},{32,128},{40,136},{48,144},{56,15... | collective-permute-start | bytes 798728 | tf_op jit(solution)/shard_map/ppermute | solution.py:18
  168.5 3.5 %collective-permute-done.8 = f32[8,65,128]{2,1,0:T(8,128)S(1)} collective-permute-done((f32[8,65,128]{2,1,0:T(8,128)S(1)}, f32[8,65,128]{2,1,0:T(8,128)S(1)}, u32[]{:S(2)}, u32[]{:S(2)}) %collective-permute-start.8) | collective-permute-done | bytes 266272 | tf_op jit(solution)/shard_map/ppermute | solution.py:18
  172.0 0.8 add_bitcast_fusion
  172.8 1.8 fusion.23
  174.8 2.4 bitcast_convert_fusion
  177.3 2.3 pad_maximum_fusion
  179.6 58.3 %reduce-scatter.2.cloned.1.call-done = bf16[1028,256]{1,0:T(8,128)(2,1)} async-done(((bf16[1028,2048]{1,0:T(8,128)(2,1)}), bf16[1028,256]{1,0:T(8,128)(2,1)}) %reduce-scatter.2.cloned.1.call-update) | async-done | bytes 526352 | tf_op jit(solution)/shard_map/reduce_scatter | solution.py:189
  237.9 1.1 convert_element_type.38
  239.1 1.0 fusion.24
  (80 shorter events, 2.8 us)
Async XLA Ops:
  7.2 167.7 %copy-start = (bf16[512,2048]{1,0:T(8,128)(2,1)S(1)}, bf16[512,2048]{1,0:T(8,128)(2,1)}, u32[]{:S(2)}) copy-start(bf16[512,2048]{1,0:T(8,128)(2,1)} %param.29) | copy-start | bytes 6291460
  7.2 65.1 %all-gather.2.cloned.1.call-start = ((), (), s32[]{:S(2)}) async-start(), calls=%async_computation.1 | async-start | bytes 4718592 | tf_op jit(solution)/shard_map/all_gather | solution.py:76
  7.9 230.0 %reduce-scatter.2.cloned.1.call-start = ((), (), s32[]{:S(2)}) async-start(), calls=%async_computation.2 | async-start | bytes 4755456 | tf_op jit(solution)/shard_map/reduce_scatter | solution.py:189
  78.6 12.9 %copy-start.3 = (bf16[1024,2048]{1,0:T(8,128)(2,1)S(1)}, bf16[1024,2048]{1,0:T(8,128)(2,1)}, u32[]{:S(2)}) copy-start(bf16[1024,2048]{1,0:T(8,128)(2,1)} %all-gather.2.cloned.1.call-done) | copy-start | bytes 12582916
  78.6 12.9 %copy-start.14 = (bf16[2048,256]{1,0:T(8,128)(2,1)S(1)}, bf16[2048,256]{1,0:T(8,128)(2,1)}, u32[]{:S(2)}) copy-start(bf16[2048,256]{1,0:T(8,128)(2,1)} %param.19) | copy-start | bytes 3145732
  84.0 10.8 %copy-start.13 = (bf16[2048,512]{1,0:T(8,128)(2,1)S(1)}, bf16[2048,512]{1,0:T(8,128)(2,1)}, u32[]{:S(2)}) copy-start(bf16[2048,512]{1,0:T(8,128)(2,1)} %param.17) | copy-start | bytes 6291460
  84.0 17.1 %collective-permute-start = (bf16[3,512]{1,0:T(4,128)(2,1)S(1)}, bf16[3,512]{1,0:T(4,128)(2,1)S(1)}, u32[]{:S(2)}, u32[]{:S(2)}) collective-permute-start(bf16[3,512]{1,0:T(4,128)(2,1)S(1)} %slice.224), channel_id=1, source_target_pairs={{0,8},{8,16},{16,24},{24,32},{32,40},{40,48},{48,56},{56,64},{64,7... | collective-permute-start | bytes 9224 | tf_op jit(solution)/shard_map/ppermute | solution.py:18
  92.8 6.2 %copy-start.11 = (f32[256]{0:T(256)S(1)}, f32[256]{0:T(256)}, u32[]{:S(2)}) copy-start(f32[256]{0:T(256)} %param.24) | copy-start | bytes 3076
  92.8 6.1 %collective-permute-start.1 = (bf16[3,256]{1,0:T(4,128)(2,1)S(1)}, bf16[3,256]{1,0:T(4,128)(2,1)S(1)}, u32[]{:S(2)}, u32[]{:S(2)}) collective-permute-start(bf16[3,256]{1,0:T(4,128)(2,1)S(1)} %slice.235), channel_id=1, source_target_pairs={{0,8},{8,16},{16,24},{24,32},{32,40},{40,48},{48,56},{56,64},{64,7... | collective-permute-start | bytes 4616 | tf_op jit(solution)/shard_map/ppermute | solution.py:18
  100.4 1.1 copy-start.10
  101.1 13.3 %copy-start.6 = (bf16[1024,128]{1,0:T(8,128)(2,1)}, bf16[1024,128]{1,0:T(8,128)(2,1)S(1)}, u32[]{:S(2)}) copy-start(bf16[1024,128]{1,0:T(8,128)(2,1)S(1)} %get-tuple-element.21) | copy-start | bytes 786436
  115.9 0.7 copy-start.4
  117.3 24.0 %collective-permute-start.5 = (f32[8,65,128]{2,1,0:T(8,128)}, f32[8,65,128]{2,1,0:T(8,128)}, u32[]{:S(2)}, u32[]{:S(2)}) collective-permute-start(f32[8,65,128]{2,1,0:T(8,128)} %pad_maximum_fusion.2), channel_id=1, source_target_pairs={{0,32},{8,40},{16,48},{24,56},{32,64},{40,72},{48,80},{56,88},{64,... | collective-permute-start | bytes 798728 | tf_op jit(solution)/shard_map/ppermute | solution.py:18
  122.4 19.0 %collective-permute-start.4 = (f32[8,65,128]{2,1,0:T(8,128)}, f32[8,65,128]{2,1,0:T(8,128)}, u32[]{:S(2)}, u32[]{:S(2)}) collective-permute-start(f32[8,65,128]{2,1,0:T(8,128)} %pad_maximum_fusion.2), channel_id=1, source_target_pairs={{0,24},{8,32},{16,40},{24,48},{32,56},{40,64},{48,72},{56,80},{64,... | collective-permute-start | bytes 798728 | tf_op jit(solution)/shard_map/ppermute | solution.py:18
  126.4 15.0 %collective-permute-start.3 = (f32[8,65,128]{2,1,0:T(8,128)}, f32[8,65,128]{2,1,0:T(8,128)}, u32[]{:S(2)}, u32[]{:S(2)}) collective-permute-start(f32[8,65,128]{2,1,0:T(8,128)} %pad_maximum_fusion.2), channel_id=1, source_target_pairs={{0,16},{8,24},{16,32},{24,40},{32,48},{40,56},{48,64},{56,72},{64,... | collective-permute-start | bytes 798728 | tf_op jit(solution)/shard_map/ppermute | solution.py:18
  129.5 15.1 %collective-permute-start.2 = (f32[8,65,128]{2,1,0:T(8,128)}, f32[8,65,128]{2,1,0:T(8,128)}, u32[]{:S(2)}, u32[]{:S(2)}) collective-permute-start(f32[8,65,128]{2,1,0:T(8,128)} %pad_maximum_fusion.2), channel_id=1, source_target_pairs={{0,8},{8,16},{16,24},{24,32},{32,40},{40,48},{48,56},{56,64},{64,7... | collective-permute-start | bytes 798728 | tf_op jit(solution)/shard_map/ppermute | solution.py:18
  140.0 6.0 %copy-start.5 = (f32[8,64,128]{2,1,0:T(8,128)S(1)}, f32[8,64,128]{2,1,0:T(8,128)}, u32[]{:S(2)}) copy-start(f32[8,64,128]{2,1,0:T(8,128)} %copy-done.4) | copy-start | bytes 786436
  144.7 8.2 %copy-start.8 = (f32[4,256,8,64]{1,0,3,2:T(4,128)S(1)}, f32[4,256,8,64]{1,0,3,2:T(4,128)}, u32[]{:S(2)}) copy-start(f32[4,256,8,64]{1,0,3,2:T(4,128)} %get-tuple-element.18) | copy-start | bytes 6291460
  144.7 8.2 %copy-start.9 = (pred[4,256,256]{2,1,0:T(8,128)(4,1)S(1)}, pred[4,256,256]{2,1,0:T(8,128)(4,1)}, u32[]{:S(2)}) copy-start(pred[4,256,256]{2,1,0:T(8,128)(4,1)} %compare_and_fusion) | copy-start | bytes 786436
  146.2 22.2 %collective-permute-start.7 = (f32[8,65,128]{2,1,0:T(8,128)S(1)}, f32[8,65,128]{2,1,0:T(8,128)S(1)}, u32[]{:S(2)}, u32[]{:S(2)}) collective-permute-start(f32[8,65,128]{2,1,0:T(8,128)S(1)} %pad_maximum_fusion.3), channel_id=1, source_target_pairs={{0,64},{8,72},{16,80},{24,88},{32,96},{40,104},{48,112},{56,120},{... | collective-permute-start | bytes 798728 | tf_op jit(solution)/shard_map/ppermute | solution.py:18
  149.5 18.9 %collective-permute-start.6 = (f32[8,65,128]{2,1,0:T(8,128)S(1)}, f32[8,65,128]{2,1,0:T(8,128)S(1)}, u32[]{:S(2)}, u32[]{:S(2)}) collective-permute-start(f32[8,65,128]{2,1,0:T(8,128)S(1)} %pad_maximum_fusion.3), channel_id=1, source_target_pairs={{0,32},{8,40},{16,48},{24,56},{32,64},{40,72},{48,80},{56,88},{64,... | collective-permute-start | bytes 798728 | tf_op jit(solution)/shard_map/ppermute | solution.py:18
  163.0 9.9 %copy-start.2 = (f32[4,256,8,64]{1,3,2,0:T(8,128)S(1)}, f32[4,256,8,64]{1,3,2,0:T(8,128)}, u32[]{:S(2)}) copy-start(f32[4,256,8,64]{1,3,2,0:T(8,128)} %copy.72) | copy-start | bytes 6291460
  163.1 9.7 %copy-start.1 = (f32[4,256,8,64]{1,0,3,2:T(4,128)S(1)}, f32[4,256,8,64]{1,0,3,2:T(4,128)}, u32[]{:S(2)}) copy-start(f32[4,256,8,64]{1,0,3,2:T(4,128)} %reshape.215) | copy-start | bytes 6291460
  163.1 9.7 %copy-start.7 = (bf16[1024,128]{1,0:T(8,128)(2,1)S(1)}, bf16[1024,128]{1,0:T(8,128)(2,1)}, u32[]{:S(2)}) copy-start(bf16[1024,128]{1,0:T(8,128)(2,1)} %get-tuple-element.22) | copy-start | bytes 786436
  163.1 9.7 %copy-start.12 = (f32[8]{0:T(128)S(1)}, f32[8]{0:T(128)}, u32[]{:S(2)}) copy-start(f32[8]{0:T(128)} %param.27) | copy-start | bytes 100
  163.1 8.9 %collective-permute-start.8 = (f32[8,65,128]{2,1,0:T(8,128)S(1)}, f32[8,65,128]{2,1,0:T(8,128)S(1)}, u32[]{:S(2)}, u32[]{:S(2)}) collective-permute-start(f32[8,65,128]{2,1,0:T(8,128)S(1)} %pad_maximum_fusion.3), channel_id=1, source_target_pairs={{0,96},{8,104},{16,112},{24,120},{32,128},{40,136},{48,144},{56,15... | collective-permute-start | bytes 798728 | tf_op jit(solution)/shard_map/ppermute | solution.py:18
Sparse Core Ops, SparseCore 0:
  9.7 62.5 all-gather.1
  179.7 58.1 reduce-scatter.1

commit v6 on v5

--- a/solution.py
+++ b/solution.py
@@ -78,7 +78,6 @@
     def partial_product(matrix):
         return jnp.dot(piece, matrix, preferred_element_type=jnp.float32)
 
-    gate_full = partial_product(w_gate)
     x_sum = partial_product(w_x)
     bc_sum = partial_product(w_bc)
     dt_raw = partial_product(w_dt)
@@ -87,9 +86,12 @@
     idents = lax.dynamic_slice_in_dim(seg_ids, first_row, rows_here)
     earlier = lax.dynamic_slice_in_dim(seg_ids, jnp.maximum(first_row - lag_count, 0), lag_count)
     earlier = jnp.where(device > 0, earlier, -1)
-    edge_x, edge_bc = shifted(
-        (x_pre[rows_here - lag_count :], bc_pre[rows_here - lag_count :]), "seq", 1
-    )
+    edges = shifted(
+        jnp.concatenate([x_pre[rows_here - lag_count :], bc_pre[rows_here - lag_count :]], 1),
+        "seq",
+        1,
+    )
+    edge_x, edge_bc = edges[:, :inner_here], edges[:, inner_here:]
     x_conv = jax.nn.silu(conv_block(x_pre, edge_x, conv_x, conv_x_bias, idents, earlier)).astype(
         jnp.bfloat16
     )
@@ -137,6 +139,8 @@
     gain_row = jnp.broadcast_to(running_gain[:, None, None], (heads_here, 1, state_width))
     packed = jnp.concatenate([running_state, gain_row], 1)
     identity = jnp.concatenate([0.0 * running_state, 1.0 + 0.0 * gain_row], 1)
+    late_piece, packed = lax.optimization_barrier((piece, packed))
+    gate_full = jnp.dot(late_piece, w_gate, preferred_element_type=jnp.float32)
 
     def joined_of(earlier_part, later_part):
         later_gain = later_part[:, head_width:, :]

time: 248 us -> 250 us (level)
  waiting for transfers between devices: 123 us -> 128 us
    ppermute x9 -> x8, waiting for transfers between devices: 6.79 us -> 11.9 us  [shifted(): return lax.ppermute(x, axis, pairs)]
    dot_general x4 -> x3, matrix products: 14 us -> 9.33 us  [partial_product(): return jnp.dot(piece, matrix, preferred_element_type=jnp.float32)]
    dot_general x0 -> x1, matrix products: none -> 3.95 us  [shards(): gate_full = jnp.dot(late_piece, w_gate, preferred_element_type=jnp.float32)]
    ppermute x9 -> x8, starting transfers between devices: 35.7 us -> 34.4 us  [shifted(): return lax.ppermute(x, axis, pairs)]
  transfers between devices with their start and end apart: 11 -> 10, of which waited for: 4 -> 6; matrix products, arithmetic and copies ran while one was open for 14% -> 13% of each run, Pallas kernels for 0% -> 0%
where the time goes in v6:
time: 250 us; the launch traced here: 249 us
  waiting for transfers between devices  128 us (51%)
  starting transfers between devices  34.4 us (14%)
  matrix products  31.4 us (13%)
  local copies, waits for them, and re-layouts  21.1 us (8%)
  other arithmetic  20.3 us (8%)
  between operations  14.5 us (6%)
    reduce_scatter x1, waiting for transfers between devices, shards(): lax.psum_scatter(joined.astype(jnp.bfloat16), 'head', scatter_dimension=1...  58.2 us
    all_gather x1, waiting for transfers between devices, shards(): piece = lax.all_gather(tokens, 'head', axis=1, tiled=True)  56.7 us
    ppermute x8, starting transfers between devices, shifted(): return lax.ppermute(x, axis, pairs)  34.4 us
    ppermute x8, waiting for transfers between devices, shifted(): return lax.ppermute(x, axis, pairs)  11.9 us
    dot_general x1, matrix products, shards(): jnp.einsum('chts,cshp->cthp', decays * scores[:, None, :, :], group_x, pr...  10.8 us
    dot_general x3, matrix products, partial_product(): return jnp.dot(piece, matrix, preferred_element_type=jnp.float32)  9.33 us
    reshape x2, local copies, waits for them, and re-layouts, shards(): gate_act = jax.nn.silu(gate_full).reshape(group_shape)  8.15 us
    reshape x2, local copies, waits for them, and re-layouts, shards(): x_conv.astype(jnp.float32).reshape(rows_here, heads_here, head_width)  6.14 us
  transfers between devices with their start and end apart: 10, of which 6 were waited for; matrix products, arithmetic and copies ran while one was open for 13% of the time, Pallas kernels for 0%

profile of v6, /device:TPU:1, one launch (start us, length us, event | category | flops | bytes accessed | tf_op | source)
XLA Modules:
  0.0 249.4 jit_solution(12937112282148495123)
XLA Ops:
  7.2 0.7 all-gather.2.cloned.1.call-update
  8.0 0.8 mul.485
  8.7 0.7 dynamic_slice.7
  9.4 0.8 broadcast_select_fusion.6
  10.2 0.6 slice.204
  11.0 0.7 pad_add_fusion.1
  11.9 0.8 fusion.65
  12.9 0.8 fusion.75
  13.7 0.9 fusion.74
  14.6 1.0 compare_and_fusion
  15.6 56.7 %all-gather.2.cloned.1.call-done = bf16[1024,2048]{1,0:T(8,128)(2,1)} async-done(((bf16[1024,256]{1,0:T(8,128)(2,1)}), bf16[1024,2048]{1,0:T(8,128)(2,1)}) %all-gather.2.cloned.1.call-update) | async-done | bytes 4194320 | tf_op jit(solution)/shard_map/all_gather | solution.py:76
  72.3 3.4 %negate_multiply_fusion = (f32[1024,8]{0,1:T(8,128)S(1)}, f32[1024,8]{0,1:T(8,128)S(1)}) fusion(f32[8]{0:T(128)} %param.26, f32[8]{0:T(128)} %param.25, bf16[1024,2048]{1,0:T(8,128)(2,1)} %all-gather.2.cloned.1.call-done, bf16[2048,8]{0,1:T(8,128)(2,1)} %param.20), kind=kOutput, calls=%fused_computation.112 | convolution fusion | flops 33628160 | bytes 4292672 | tf_op jit(solution)/shard_map/dot_general | solution.py:79
  75.7 2.3 reduce-window.6
  78.6 3.6 %convolution_convert_fusion.1 = bf16[1024,256]{1,0:T(8,128)(2,1)S(1)} fusion(bf16[1024,2048]{1,0:T(8,128)(2,1)} %all-gather.2.cloned.1.call-done, bf16[2048,256]{1,0:T(8,128)(2,1)S(1)} %copy-done.19), kind=kOutput, calls=%fused_computation.36 | convolution fusion | flops 1074003968 | bytes 5767168 | tf_op jit(solution)/shard_map/dot_general | solution.py:79
  82.3 0.5 copy-done.17
  82.8 2.3 convolution_convert_fusion
  85.1 7.4 %collective-permute-start = (bf16[3,768]{1,0:T(4,128)(2,1)S(1)}, bf16[3,768]{1,0:T(4,128)(2,1)S(1)}, u32[]{:S(2)}, u32[]{:S(2)}) collective-permute-start(bf16[3,768]{1,0:T(4,128)(2,1)S(1)} %pad_maximum_fusion.4), channel_id=1, source_target_pairs={{0,8},{8,16},{16,24},{24,32},{32,40},{40,48},{48,56},{56,64},{64,7... | collective-permute-start | bytes 13832 | tf_op jit(solution)/shard_map/ppermute | solution.py:18
  92.7 0.6 collective-permute-done
  93.4 1.3 multiply_convert_fusion.2
  94.7 0.7 fusion.73
  95.8 3.1 %fusion.38 = f32[1024,512]{1,0:T(8,128)} fusion(f32[512]{0:T(512)S(1)} %copy-done.14, f32[512]{0:T(512)S(1)} %bitcast.149, f32[1027,512]{1,0:T(8,128)S(1)} %maximum_convert_fusion, pred[1024]{0:T(1024)(128)(4,1)S(1)} %get-tuple-element.43, f32[512]{0:T(512)S(1)} %bitcast.150, pred[1024]{0:T(1024)(128)(4,1)S(1)} %get-tuple-element.44, f32[512]{0:T(512)S(1)} %bitcast.148, ...), kind=kLoop, calls=%fused_computation.64 | loop fusion | flops 8912896 | bytes 10499072 | tf_op jit(solution)/shard_map/reshape | solution.py:103
  99.0 3.0 %copy.63 = f32[1024,512]{0,1:T(8,128)} copy(f32[1024,512]{1,0:T(8,128)} %fusion.38) | data formatting | bytes 4194304 | tf_op jit(solution)/shard_map/reshape | solution.py:103
  101.9 3.2 %reshape.215 = f32[4,256,8,64]{1,0,3,2:T(4,128)} reshape(f32[1024,512]{0,1:T(8,128)} %copy.63) | data formatting | bytes 4194304 | tf_op jit(solution)/shard_map/reshape | solution.py:103
  105.1 2.6 %broadcast_multiply_fusion = (f32[4,256,8,64]{1,0,3,2:T(4,128)S(1)}, f32[4,256,8,64]{1,0,3,2:T(4,128)S(1)}) fusion(f32[4,256,8]{1,0,2:T(4,128)S(1)} %copy.68, f32[4,256,8,64]{1,0,3,2:T(4,128)} %reshape.215, f32[4,256,8]{1,0,2:T(4,128)S(1)} %copy.64), kind=kLoop, calls=%fused_computation.60 | loop fusion | flops 1048576 | bytes 6356992 | tf_op jit(solution)/shard_map/mul | solution.py:125
  107.7 1.3 fusion.20
  109.3 4.5 %collective-permute-start.4 = (f32[8,65,128]{2,1,0:T(8,128)S(1)}, f32[8,65,128]{2,1,0:T(8,128)S(1)}, u32[]{:S(2)}, u32[]{:S(2)}) collective-permute-start(f32[8,65,128]{2,1,0:T(8,128)S(1)} %pad_maximum_fusion.2), channel_id=1, source_target_pairs={{0,32},{8,40},{16,48},{24,56},{32,64},{40,72},{48,80},{56,88},{64,... | collective-permute-start | bytes 798728 | tf_op jit(solution)/shard_map/ppermute | solution.py:18
  113.8 6.8 %collective-permute-start.3 = (f32[8,65,128]{2,1,0:T(8,128)S(1)}, f32[8,65,128]{2,1,0:T(8,128)S(1)}, u32[]{:S(2)}, u32[]{:S(2)}) collective-permute-start(f32[8,65,128]{2,1,0:T(8,128)S(1)} %pad_maximum_fusion.2), channel_id=1, source_target_pairs={{0,24},{8,32},{16,40},{24,48},{32,56},{40,64},{48,72},{56,80},{64,... | collective-permute-start | bytes 798728 | tf_op jit(solution)/shard_map/ppermute | solution.py:18
  120.6 1.3 collective-permute-start.2
  121.9 2.6 %collective-permute-start.1 = (f32[8,65,128]{2,1,0:T(8,128)S(1)}, f32[8,65,128]{2,1,0:T(8,128)S(1)}, u32[]{:S(2)}, u32[]{:S(2)}) collective-permute-start(f32[8,65,128]{2,1,0:T(8,128)S(1)} %pad_maximum_fusion.2), channel_id=1, source_target_pairs={{0,8},{8,16},{16,24},{24,32},{32,40},{40,48},{48,56},{56,64},{64,7... | collective-permute-start | bytes 798728 | tf_op jit(solution)/shard_map/ppermute | solution.py:18
  124.6 3.9 %divide_multiply_fusion = f32[1024,512]{1,0:T(8,128)} fusion(bf16[1024,2048]{1,0:T(8,128)(2,1)S(1)} %copy-done.4, bf16[2048,512]{1,0:T(8,128)(2,1)S(1)} %copy-done.18), kind=kOutput, calls=%fused_computation.33 | convolution fusion | flops 2149580800 | bytes 8388608 | tf_op jit(solution)/shard_map/dot_general | solution.py:143
  128.8 4.4 %collective-permute-done.2 = f32[8,65,128]{2,1,0:T(8,128)S(1)} collective-permute-done((f32[8,65,128]{2,1,0:T(8,128)S(1)}, f32[8,65,128]{2,1,0:T(8,128)S(1)}, u32[]{:S(2)}, u32[]{:S(2)}) %collective-permute-start.2) | collective-permute-done | bytes 266272 | tf_op jit(solution)/shard_map/ppermute | solution.py:18
  133.2 3.2 %collective-permute-done.1 = f32[8,65,128]{2,1,0:T(8,128)S(1)} collective-permute-done((f32[8,65,128]{2,1,0:T(8,128)S(1)}, f32[8,65,128]{2,1,0:T(8,128)S(1)}, u32[]{:S(2)}, u32[]{:S(2)}) %collective-permute-start.1) | collective-permute-done | bytes 266272 | tf_op jit(solution)/shard_map/ppermute | solution.py:18
  136.8 0.7 copy-done.7
  137.5 0.7 pad_maximum_fusion.3
  138.2 3.8 %collective-permute-start.6 = (f32[8,65,128]{2,1,0:T(8,128)}, f32[8,65,128]{2,1,0:T(8,128)}, u32[]{:S(2)}, u32[]{:S(2)}) collective-permute-start(f32[8,65,128]{2,1,0:T(8,128)} %pad_maximum_fusion.3), channel_id=1, source_target_pairs={{0,64},{8,72},{16,80},{24,88},{32,96},{40,104},{48,112},{56,120},{... | collective-permute-start | bytes 798728 | tf_op jit(solution)/shard_map/ppermute | solution.py:18
  142.0 4.7 %collective-permute-start.5 = (f32[8,65,128]{2,1,0:T(8,128)}, f32[8,65,128]{2,1,0:T(8,128)}, u32[]{:S(2)}, u32[]{:S(2)}) collective-permute-start(f32[8,65,128]{2,1,0:T(8,128)} %pad_maximum_fusion.3), channel_id=1, source_target_pairs={{0,32},{8,40},{16,48},{24,56},{32,64},{40,72},{48,80},{56,88},{64,... | collective-permute-start | bytes 798728 | tf_op jit(solution)/shard_map/ppermute | solution.py:18
  146.8 10.8 %fusion = f32[4,8,64,256]{3,2,1,0:T(8,128)} fusion(f32[4,256,256]{2,1,0:T(8,128)S(1)} %fusion.78, f32[4,8,256]{2,1,0:T(8,128)S(1)} %add_bitcast_fusion.2, pred[4,256,256]{2,1,0:T(8,128)(4,1)S(1)} %copy-done.13, f32[4,256,8,64]{1,0,3,2:T(4,128)S(1)} %get-tuple-element.22), kind=kOutput, calls=%fused_computation.1 | convolution fusion | flops 1619001344 | bytes 5537792 | tf_op jit(solution)/shard_map/chts,cshp->cthp/dot_general | solution.py:119
  157.6 4.4 %reshape.219 = f32[4,256,8,64]{3,2,1,0:T(8,128)} reshape(f32[1024,512]{1,0:T(8,128)} %divide_multiply_fusion) | data formatting | bytes 4194304 | tf_op jit(solution)/shard_map/reshape | solution.py:180
  162.0 3.8 %copy.72 = f32[4,256,8,64]{1,3,2,0:T(8,128)} copy(f32[4,256,8,64]{3,2,1,0:T(8,128)} %reshape.219) | data formatting | bytes 4194304 | tf_op jit(solution)/shard_map/reshape | solution.py:180
  165.9 3.2 %collective-permute-start.7 = (f32[8,65,128]{2,1,0:T(8,128)}, f32[8,65,128]{2,1,0:T(8,128)S(1)}, u32[]{:S(2)}, u32[]{:S(2)}) collective-permute-start(f32[8,65,128]{2,1,0:T(8,128)} %pad_maximum_fusion.3), channel_id=1, source_target_pairs={{0,96},{8,104},{16,112},{24,120},{32,128},{40,136},{48,144},{56,15... | collective-permute-start | bytes 798728 | tf_op jit(solution)/shard_map/ppermute | solution.py:18
  169.2 3.8 %collective-permute-done.7 = f32[8,65,128]{2,1,0:T(8,128)S(1)} collective-permute-done((f32[8,65,128]{2,1,0:T(8,128)}, f32[8,65,128]{2,1,0:T(8,128)S(1)}, u32[]{:S(2)}, u32[]{:S(2)}) %collective-permute-start.7) | collective-permute-done | bytes 266272 | tf_op jit(solution)/shard_map/ppermute | solution.py:18
  173.0 0.8 add_bitcast_fusion
  173.9 3.3 %fusion.23 = (bf16[4,8,8,8,256]{4,3,2,1,0:T(8,128)(2,1)S(1)}, bf16[4,256]{1,0:T(4,128)(2,1)S(1)}) fusion(f32[8,64]{1,0:T(8,128)S(1)} %mul.485, f32[4,256,8,64]{1,3,2,0:T(8,128)S(1)} %copy-done.2, f32[4,256,8,64]{1,0,3,2:T(4,128)S(1)} %copy-done.1, f32[8]{0:T(128)S(1)} %copy-done.16, f32[4,256,8]{1,2,0:T(8,128)S(1)} %get-tuple-element.16, ...), kind=kOutput, calls=%fused_computation.39 | convolution fusion | flops 811334656 | bytes 8687792 | tf_op jit(solution)/shard_map/ctn,chpn->cthp/dot_general | solution.py:174
  177.4 2.4 bitcast_convert_fusion
  179.8 2.3 pad_maximum_fusion
  182.2 58.2 %reduce-scatter.2.cloned.1.call-done = bf16[1028,256]{1,0:T(8,128)(2,1)} async-done(((bf16[1028,2048]{1,0:T(8,128)(2,1)}), bf16[1028,256]{1,0:T(8,128)(2,1)}) %reduce-scatter.2.cloned.1.call-update) | async-done | bytes 526352 | tf_op jit(solution)/shard_map/reduce_scatter | solution.py:193
  240.4 1.1 convert_element_type.38
  241.5 1.0 fusion.24
  (91 shorter events, 3.3 us)
Async XLA Ops:
  7.2 170.3 %copy-start = (bf16[512,2048]{1,0:T(8,128)(2,1)S(1)}, bf16[512,2048]{1,0:T(8,128)(2,1)}, u32[]{:S(2)}) copy-start(bf16[512,2048]{1,0:T(8,128)(2,1)} %param.29) | copy-start | bytes 6291460
  7.2 65.1 %all-gather.2.cloned.1.call-start = ((), (), s32[]{:S(2)}) async-start(), calls=%async_computation.1 | async-start | bytes 4718592 | tf_op jit(solution)/shard_map/all_gather | solution.py:76
  7.9 232.5 %reduce-scatter.2.cloned.1.call-start = ((), (), s32[]{:S(2)}) async-start(), calls=%async_computation.2 | async-start | bytes 4755456 | tf_op jit(solution)/shard_map/reduce_scatter | solution.py:193
  15.5 63.1 %copy-start.19 = (bf16[2048,256]{1,0:T(8,128)(2,1)S(1)}, bf16[2048,256]{1,0:T(8,128)(2,1)}, u32[]{:S(2)}) copy-start(bf16[2048,256]{1,0:T(8,128)(2,1)} %param.19) | copy-start | bytes 3145732
  78.6 3.6 %copy-start.3 = (bf16[1024,2048]{1,0:T(8,128)(2,1)S(1)}, bf16[1024,2048]{1,0:T(8,128)(2,1)}, u32[]{:S(2)}) copy-start(bf16[1024,2048]{1,0:T(8,128)(2,1)} %all-gather.2.cloned.1.call-done) | copy-start | bytes 12582916
  78.6 4.1 %copy-start.17 = (bf16[2048,512]{1,0:T(8,128)(2,1)S(1)}, bf16[2048,512]{1,0:T(8,128)(2,1)}, u32[]{:S(2)}) copy-start(bf16[2048,512]{1,0:T(8,128)(2,1)} %param.18) | copy-start | bytes 6291460
  82.8 10.6 %copy-start.15 = (f32[256]{0:T(256)S(1)}, f32[256]{0:T(256)}, u32[]{:S(2)}) copy-start(f32[256]{0:T(256)} %param.24) | copy-start | bytes 3076
  85.1 8.1 %collective-permute-start = (bf16[3,768]{1,0:T(4,128)(2,1)S(1)}, bf16[3,768]{1,0:T(4,128)(2,1)S(1)}, u32[]{:S(2)}, u32[]{:S(2)}) collective-permute-start(bf16[3,768]{1,0:T(4,128)(2,1)S(1)} %pad_maximum_fusion.4), channel_id=1, source_target_pairs={{0,8},{8,16},{16,24},{24,32},{32,40},{40,48},{48,56},{56,64},{64,7... | collective-permute-start | bytes 13832 | tf_op jit(solution)/shard_map/ppermute | solution.py:18
  94.7 1.1 copy-start.14
  95.5 12.2 %copy-start.9 = (bf16[1024,128]{1,0:T(8,128)(2,1)}, bf16[1024,128]{1,0:T(8,128)(2,1)S(1)}, u32[]{:S(2)}) copy-start(bf16[1024,128]{1,0:T(8,128)(2,1)S(1)} %get-tuple-element.26) | copy-start | bytes 786436
  105.1 19.5 %copy-start.18 = (bf16[2048,512]{1,0:T(8,128)(2,1)S(1)}, bf16[2048,512]{1,0:T(8,128)(2,1)}, u32[]{:S(2)}) copy-start(bf16[2048,512]{1,0:T(8,128)(2,1)} %param.17) | copy-start | bytes 6291460
  107.7 16.9 %copy-start.4 = (bf16[1024,2048]{1,0:T(8,128)(2,1)S(1)}, bf16[1024,2048]{1,0:T(8,128)(2,1)}, u32[]{:S(2)}) copy-start(bf16[1024,2048]{1,0:T(8,128)(2,1)} %all-gather.2.cloned.1.call-done) | copy-start | bytes 12582916
  109.1 27.5 %copy-start.5 = (f32[8,64,128]{2,1,0:T(8,128)}, f32[8,64,128]{2,1,0:T(8,128)S(1)}, u32[]{:S(2)}) copy-start(f32[8,64,128]{2,1,0:T(8,128)S(1)} %get-tuple-element.15) | copy-start | bytes 786436
  109.2 19.3 %copy-start.10 = (bf16[1024,128]{1,0:T(8,128)(2,1)S(1)}, bf16[1024,128]{1,0:T(8,128)(2,1)}, u32[]{:S(2)}) copy-start(bf16[1024,128]{1,0:T(8,128)(2,1)} %copy-done.9) | copy-start | bytes 786436
  109.2 19.3 %copy-start.11 = (bf16[1024,128]{1,0:T(8,128)(2,1)S(1)}, bf16[1024,128]{1,0:T(8,128)(2,1)}, u32[]{:S(2)}) copy-start(bf16[1024,128]{1,0:T(8,128)(2,1)} %get-tuple-element.25) | copy-start | bytes 786436
  109.3 19.6 %collective-permute-start.4 = (f32[8,65,128]{2,1,0:T(8,128)S(1)}, f32[8,65,128]{2,1,0:T(8,128)S(1)}, u32[]{:S(2)}, u32[]{:S(2)}) collective-permute-start(f32[8,65,128]{2,1,0:T(8,128)S(1)} %pad_maximum_fusion.2), channel_id=1, source_target_pairs={{0,32},{8,40},{16,48},{24,56},{32,64},{40,72},{48,80},{56,88},{64,... | collective-permute-start | bytes 798728 | tf_op jit(solution)/shard_map/ppermute | solution.py:18
  113.8 15.1 %collective-permute-start.3 = (f32[8,65,128]{2,1,0:T(8,128)S(1)}, f32[8,65,128]{2,1,0:T(8,128)S(1)}, u32[]{:S(2)}, u32[]{:S(2)}) collective-permute-start(f32[8,65,128]{2,1,0:T(8,128)S(1)} %pad_maximum_fusion.2), channel_id=1, source_target_pairs={{0,24},{8,32},{16,40},{24,48},{32,56},{40,64},{48,72},{56,80},{64,... | collective-permute-start | bytes 798728 | tf_op jit(solution)/shard_map/ppermute | solution.py:18
  120.6 12.7 %collective-permute-start.2 = (f32[8,65,128]{2,1,0:T(8,128)S(1)}, f32[8,65,128]{2,1,0:T(8,128)S(1)}, u32[]{:S(2)}, u32[]{:S(2)}) collective-permute-start(f32[8,65,128]{2,1,0:T(8,128)S(1)} %pad_maximum_fusion.2), channel_id=1, source_target_pairs={{0,16},{8,24},{16,32},{24,40},{32,48},{40,56},{48,64},{56,72},{64,... | collective-permute-start | bytes 798728 | tf_op jit(solution)/shard_map/ppermute | solution.py:18
  121.9 14.5 %collective-permute-start.1 = (f32[8,65,128]{2,1,0:T(8,128)S(1)}, f32[8,65,128]{2,1,0:T(8,128)S(1)}, u32[]{:S(2)}, u32[]{:S(2)}) collective-permute-start(f32[8,65,128]{2,1,0:T(8,128)S(1)} %pad_maximum_fusion.2), channel_id=1, source_target_pairs={{0,8},{8,16},{16,24},{24,32},{32,40},{40,48},{48,56},{56,64},{64,7... | collective-permute-start | bytes 798728 | tf_op jit(solution)/shard_map/ppermute | solution.py:18
  136.5 10.3 %copy-start.13 = (pred[4,256,256]{2,1,0:T(8,128)(4,1)S(1)}, pred[4,256,256]{2,1,0:T(8,128)(4,1)}, u32[]{:S(2)}) copy-start(pred[4,256,256]{2,1,0:T(8,128)(4,1)} %compare_and_fusion) | copy-start | bytes 786436
  136.8 0.7 copy-start.7
  138.2 30.9 %collective-permute-start.6 = (f32[8,65,128]{2,1,0:T(8,128)}, f32[8,65,128]{2,1,0:T(8,128)}, u32[]{:S(2)}, u32[]{:S(2)}) collective-permute-start(f32[8,65,128]{2,1,0:T(8,128)} %pad_maximum_fusion.3), channel_id=1, source_target_pairs={{0,64},{8,72},{16,80},{24,88},{32,96},{40,104},{48,112},{56,120},{... | collective-permute-start | bytes 798728 | tf_op jit(solution)/shard_map/ppermute | solution.py:18
  142.0 27.1 %collective-permute-start.5 = (f32[8,65,128]{2,1,0:T(8,128)}, f32[8,65,128]{2,1,0:T(8,128)}, u32[]{:S(2)}, u32[]{:S(2)}) collective-permute-start(f32[8,65,128]{2,1,0:T(8,128)} %pad_maximum_fusion.3), channel_id=1, source_target_pairs={{0,32},{8,40},{16,48},{24,56},{32,64},{40,72},{48,80},{56,88},{64,... | collective-permute-start | bytes 798728 | tf_op jit(solution)/shard_map/ppermute | solution.py:18
  165.7 7.3 %copy-start.6 = (f32[8,64,128]{2,1,0:T(8,128)S(1)}, f32[8,64,128]{2,1,0:T(8,128)}, u32[]{:S(2)}) copy-start(f32[8,64,128]{2,1,0:T(8,128)} %copy-done.5) | copy-start | bytes 786436
  165.7 7.3 %copy-start.8 = (f32[8,64,128]{2,1,0:T(8,128)S(1)}, f32[8,64,128]{2,1,0:T(8,128)}, u32[]{:S(2)}) copy-start(f32[8,64,128]{2,1,0:T(8,128)} %copy-done.7) | copy-start | bytes 786436
  165.7 8.2 %copy-start.2 = (f32[4,256,8,64]{1,3,2,0:T(8,128)S(1)}, f32[4,256,8,64]{1,3,2,0:T(8,128)}, u32[]{:S(2)}) copy-start(f32[4,256,8,64]{1,3,2,0:T(8,128)} %copy.72) | copy-start | bytes 6291460
  165.9 8.0 %copy-start.1 = (f32[4,256,8,64]{1,0,3,2:T(4,128)S(1)}, f32[4,256,8,64]{1,0,3,2:T(4,128)}, u32[]{:S(2)}) copy-start(f32[4,256,8,64]{1,0,3,2:T(4,128)} %reshape.215) | copy-start | bytes 6291460
  165.9 8.0 %copy-start.12 = (bf16[1024,128]{1,0:T(8,128)(2,1)S(1)}, bf16[1024,128]{1,0:T(8,128)(2,1)}, u32[]{:S(2)}) copy-start(bf16[1024,128]{1,0:T(8,128)(2,1)} %get-tuple-element.25) | copy-start | bytes 786436
  165.9 8.0 %copy-start.16 = (f32[8]{0:T(128)S(1)}, f32[8]{0:T(128)}, u32[]{:S(2)}) copy-start(f32[8]{0:T(128)} %param.27) | copy-start | bytes 100
  165.9 7.1 %collective-permute-start.7 = (f32[8,65,128]{2,1,0:T(8,128)}, f32[8,65,128]{2,1,0:T(8,128)S(1)}, u32[]{:S(2)}, u32[]{:S(2)}) collective-permute-start(f32[8,65,128]{2,1,0:T(8,128)} %pad_maximum_fusion.3), channel_id=1, source_target_pairs={{0,96},{8,104},{16,112},{24,120},{32,128},{40,136},{48,144},{56,15... | collective-permute-start | bytes 798728 | tf_op jit(solution)/shard_map/ppermute | solution.py:18
Sparse Core Ops, SparseCore 0:
  9.7 62.5 all-gather.1
  182.3 58.0 reduce-scatter.1

commit v7 on v6

--- a/solution.py
+++ b/solution.py
@@ -140,7 +140,12 @@
     packed = jnp.concatenate([running_state, gain_row], 1)
     identity = jnp.concatenate([0.0 * running_state, 1.0 + 0.0 * gain_row], 1)
     late_piece, packed = lax.optimization_barrier((piece, packed))
-    gate_full = jnp.dot(late_piece, w_gate, preferred_element_type=jnp.float32)
+    gate_turned = jnp.einsum(
+        "ctd,dk->ckt",
+        late_piece.reshape(rows_here // GROUP, GROUP, late_piece.shape[1]),
+        w_gate,
+        preferred_element_type=jnp.float32,
+    )
 
     def joined_of(earlier_part, later_part):
         later_gain = later_part[:, head_width:, :]
@@ -177,7 +182,9 @@
     end_state = (running_gain[:, None, None] * incoming + running_state)[None]
     heads_n = lax.axis_size("head")
     group_shape = (count, GROUP, heads_here, head_width)
-    gate_act = jax.nn.silu(gate_full).reshape(group_shape)
+    gate_act = jnp.transpose(
+        jax.nn.silu(gate_turned).reshape(count, heads_here, head_width, GROUP), (0, 3, 1, 2)
+    )
     direct = skip_gain[:, None] * x_float.reshape(group_shape)
     gated = (within + carried + direct) * gate_act
     scaled = (gated * norm_gain.reshape(heads_here, head_width)).astype(jnp.bfloat16)

time: 250 us -> 245 us (0.980)
  local copies, waits for them, and re-layouts: 21.1 us -> 15.9 us
    reshape x2 -> x0, local copies, waits for them, and re-layouts: 8.15 us -> none  [shards(): gate_act = jax.nn.silu(gate_full).reshape(group_shape)]
    mul x0 -> x1, local copies, waits for them, and re-layouts: none -> 2.96 us  [shards(): jax.nn.silu(gate_turned).reshape(count, heads_here, head_width, GROUP)]
  transfers between devices with their start and end apart: 10 -> 10, of which waited for: 6 -> 6; matrix products, arithmetic and copies ran while one was open for 13% -> 11% of each run, Pallas kernels for 0% -> 0%
where the time goes in v7:
time: 245 us; the launch traced here: 244 us
  waiting for transfers between devices  128 us (52%)
  starting transfers between devices  34.3 us (14%)
  matrix products  31.4 us (13%)
  other arithmetic  20.3 us (8%)
  local copies, waits for them, and re-layouts  15.9 us (6%)
  between operations  14.5 us (6%)
    reduce_scatter x1, waiting for transfers between devices, shards(): lax.psum_scatter(joined.astype(jnp.bfloat16), 'head', scatter_dimension=1...  58.2 us
    all_gather x1, waiting for transfers between devices, shards(): piece = lax.all_gather(tokens, 'head', axis=1, tiled=True)  56.7 us
    ppermute x8, starting transfers between devices, shifted(): return lax.ppermute(x, axis, pairs)  34.2 us
    ppermute x8, waiting for transfers between devices, shifted(): return lax.ppermute(x, axis, pairs)  11.9 us
    dot_general x1, matrix products, shards(): jnp.einsum('chts,cshp->cthp', decays * scores[:, None, :, :], group_x, pr...  10.8 us
    dot_general x3, matrix products, partial_product(): return jnp.dot(piece, matrix, preferred_element_type=jnp.float32)  9.33 us
    reshape x2, local copies, waits for them, and re-layouts, shards(): x_conv.astype(jnp.float32).reshape(rows_here, heads_here, head_width)  6.14 us
  transfers between devices with their start and end apart: 10, of which 6 were waited for; matrix products, arithmetic and copies ran while one was open for 11% of the time, Pallas kernels for 0%

profile of v7, /device:TPU:1, one launch (start us, length us, event | category | flops | bytes accessed | tf_op | source)
XLA Modules:
  0.0 244.0 jit_solution(16046483623244254136)
XLA Ops:
  7.2 0.7 all-gather.2.cloned.1.call-update
  8.0 0.8 mul.486
  8.7 0.7 dynamic_slice.7
  9.4 0.8 broadcast_select_fusion.6
  10.2 0.6 slice.204
  11.0 0.7 pad_add_fusion.1
  11.9 0.8 fusion.72
  12.9 0.8 fusion.82
  13.7 0.9 fusion.81
  14.6 1.0 compare_and_fusion
  15.6 56.7 %all-gather.2.cloned.1.call-done = bf16[1024,2048]{1,0:T(8,128)(2,1)} async-done(((bf16[1024,256]{1,0:T(8,128)(2,1)}), bf16[1024,2048]{1,0:T(8,128)(2,1)}) %all-gather.2.cloned.1.call-update) | async-done | bytes 4194320 | tf_op jit(solution)/shard_map/all_gather | solution.py:76
  72.3 3.4 %negate_multiply_fusion = (f32[1024,8]{0,1:T(8,128)S(1)}, f32[1024,8]{0,1:T(8,128)S(1)}) fusion(f32[8]{0:T(128)} %param.26, f32[8]{0:T(128)} %param.25, bf16[1024,2048]{1,0:T(8,128)(2,1)} %all-gather.2.cloned.1.call-done, bf16[2048,8]{0,1:T(8,128)(2,1)} %param.20), kind=kOutput, calls=%fused_computation.118 | convolution fusion | flops 33628160 | bytes 4292672 | tf_op jit(solution)/shard_map/dot_general | solution.py:79
  75.7 2.3 reduce-window.6
  78.6 3.6 %convolution_convert_fusion.1 = bf16[1024,256]{1,0:T(8,128)(2,1)S(1)} fusion(bf16[1024,2048]{1,0:T(8,128)(2,1)} %all-gather.2.cloned.1.call-done, bf16[2048,256]{1,0:T(8,128)(2,1)S(1)} %copy-done.19), kind=kOutput, calls=%fused_computation.42 | convolution fusion | flops 1074003968 | bytes 5767168 | tf_op jit(solution)/shard_map/dot_general | solution.py:79
  82.3 0.5 copy-done.17
  82.8 2.3 convolution_convert_fusion
  85.1 7.4 %collective-permute-start = (bf16[3,768]{1,0:T(4,128)(2,1)S(1)}, bf16[3,768]{1,0:T(4,128)(2,1)S(1)}, u32[]{:S(2)}, u32[]{:S(2)}) collective-permute-start(bf16[3,768]{1,0:T(4,128)(2,1)S(1)} %pad_maximum_fusion.4), channel_id=1, source_target_pairs={{0,8},{8,16},{16,24},{24,32},{32,40},{40,48},{48,56},{56,64},{64,7... | collective-permute-start | bytes 13832 | tf_op jit(solution)/shard_map/ppermute | solution.py:18
  92.7 0.6 collective-permute-done
  93.4 1.3 multiply_convert_fusion.2
  94.7 0.7 fusion.80
  95.5 0.3 maximum_convert_fusion
  95.8 3.1 %fusion.45 = f32[1024,512]{1,0:T(8,128)} fusion(f32[512]{0:T(512)S(1)} %copy-done.14, f32[512]{0:T(512)S(1)} %bitcast.170, f32[1027,512]{1,0:T(8,128)S(1)} %maximum_convert_fusion, pred[1024]{0:T(1024)(128)(4,1)S(1)} %get-tuple-element.43, f32[512]{0:T(512)S(1)} %bitcast.171, pred[1024]{0:T(1024)(128)(4,1)S(1)} %get-tuple-element.44, f32[512]{0:T(512)S(1)} %bitcast.169, ...), kind=kLoop, calls=%fused_computation.70 | loop fusion | flops 8912896 | bytes 10499072 | tf_op jit(solution)/shard_map/reshape | solution.py:103
  99.0 3.0 %copy.60 = f32[1024,512]{0,1:T(8,128)} copy(f32[1024,512]{1,0:T(8,128)} %fusion.45) | data formatting | bytes 4194304 | tf_op jit(solution)/shard_map/reshape | solution.py:103
  101.9 3.2 %reshape.219 = f32[4,256,8,64]{1,0,3,2:T(4,128)} reshape(f32[1024,512]{0,1:T(8,128)} %copy.60) | data formatting | bytes 4194304 | tf_op jit(solution)/shard_map/reshape | solution.py:103
  105.1 2.6 %broadcast_multiply_fusion = (f32[4,256,8,64]{1,0,3,2:T(4,128)S(1)}, f32[4,256,8,64]{1,0,3,2:T(4,128)S(1)}) fusion(f32[4,256,8]{1,0,2:T(4,128)S(1)} %copy.65, f32[4,256,8,64]{1,0,3,2:T(4,128)} %reshape.219, f32[4,256,8]{1,0,2:T(4,128)S(1)} %copy.61), kind=kLoop, calls=%fused_computation.66 | loop fusion | flops 1048576 | bytes 6356992 | tf_op jit(solution)/shard_map/mul | solution.py:125
  107.7 1.3 fusion.25
  109.2 4.4 %collective-permute-start.4 = (f32[8,65,128]{2,1,0:T(8,128)S(1)}, f32[8,65,128]{2,1,0:T(8,128)S(1)}, u32[]{:S(2)}, u32[]{:S(2)}) collective-permute-start(f32[8,65,128]{2,1,0:T(8,128)S(1)} %pad_maximum_fusion.2), channel_id=1, source_target_pairs={{0,32},{8,40},{16,48},{24,56},{32,64},{40,72},{48,80},{56,88},{64,... | collective-permute-start | bytes 798728 | tf_op jit(solution)/shard_map/ppermute | solution.py:18
  113.6 6.8 %collective-permute-start.3 = (f32[8,65,128]{2,1,0:T(8,128)S(1)}, f32[8,65,128]{2,1,0:T(8,128)S(1)}, u32[]{:S(2)}, u32[]{:S(2)}) collective-permute-start(f32[8,65,128]{2,1,0:T(8,128)S(1)} %pad_maximum_fusion.2), channel_id=1, source_target_pairs={{0,24},{8,32},{16,40},{24,48},{32,56},{40,64},{48,72},{56,80},{64,... | collective-permute-start | bytes 798728 | tf_op jit(solution)/shard_map/ppermute | solution.py:18
  120.4 1.3 collective-permute-start.2
  121.7 2.6 %collective-permute-start.1 = (f32[8,65,128]{2,1,0:T(8,128)S(1)}, f32[8,65,128]{2,1,0:T(8,128)S(1)}, u32[]{:S(2)}, u32[]{:S(2)}) collective-permute-start(f32[8,65,128]{2,1,0:T(8,128)S(1)} %pad_maximum_fusion.2), channel_id=1, source_target_pairs={{0,8},{8,16},{16,24},{24,32},{32,40},{40,48},{48,56},{56,64},{64,7... | collective-permute-start | bytes 798728 | tf_op jit(solution)/shard_map/ppermute | solution.py:18
  124.4 4.0 %bitcast_multiply_fusion = f32[4,512,256]{1,2,0:T(8,128)} fusion(bf16[4,256,2048]{2,1,0:T(8,128)(2,1)S(1)} %bitcast.151, bf16[2048,512]{1,0:T(8,128)(2,1)S(1)} %copy-done.18), kind=kOutput, calls=%fused_computation.24 | convolution fusion | flops 2149580800 | bytes 8388608 | tf_op jit(solution)/shard_map/ctd,dk->ckt/dot_general | solution.py:143
  128.7 4.3 %collective-permute-done.2 = f32[8,65,128]{2,1,0:T(8,128)S(1)} collective-permute-done((f32[8,65,128]{2,1,0:T(8,128)S(1)}, f32[8,65,128]{2,1,0:T(8,128)S(1)}, u32[]{:S(2)}, u32[]{:S(2)}) %collective-permute-start.2) | collective-permute-done | bytes 266272 | tf_op jit(solution)/shard_map/ppermute | solution.py:18
  133.1 3.2 %collective-permute-done.1 = f32[8,65,128]{2,1,0:T(8,128)S(1)} collective-permute-done((f32[8,65,128]{2,1,0:T(8,128)S(1)}, f32[8,65,128]{2,1,0:T(8,128)S(1)}, u32[]{:S(2)}, u32[]{:S(2)}) %collective-permute-start.1) | collective-permute-done | bytes 266272 | tf_op jit(solution)/shard_map/ppermute | solution.py:18
  136.6 0.7 copy-done.7
  137.3 0.7 pad_maximum_fusion.3
  138.1 3.8 %collective-permute-start.6 = (f32[8,65,128]{2,1,0:T(8,128)}, f32[8,65,128]{2,1,0:T(8,128)}, u32[]{:S(2)}, u32[]{:S(2)}) collective-permute-start(f32[8,65,128]{2,1,0:T(8,128)} %pad_maximum_fusion.3), channel_id=1, source_target_pairs={{0,64},{8,72},{16,80},{24,88},{32,96},{40,104},{48,112},{56,120},{... | collective-permute-start | bytes 798728 | tf_op jit(solution)/shard_map/ppermute | solution.py:18
  141.9 4.7 %collective-permute-start.5 = (f32[8,65,128]{2,1,0:T(8,128)}, f32[8,65,128]{2,1,0:T(8,128)}, u32[]{:S(2)}, u32[]{:S(2)}) collective-permute-start(f32[8,65,128]{2,1,0:T(8,128)} %pad_maximum_fusion.3), channel_id=1, source_target_pairs={{0,32},{8,40},{16,48},{24,56},{32,64},{40,72},{48,80},{56,88},{64,... | collective-permute-start | bytes 798728 | tf_op jit(solution)/shard_map/ppermute | solution.py:18
  146.6 10.8 %fusion = f32[4,8,64,256]{3,2,1,0:T(8,128)} fusion(f32[4,256,256]{2,1,0:T(8,128)S(1)} %fusion.85, f32[4,8,256]{2,1,0:T(8,128)S(1)} %add_bitcast_fusion.2, pred[4,256,256]{2,1,0:T(8,128)(4,1)S(1)} %copy-done.13, f32[4,256,8,64]{1,0,3,2:T(4,128)S(1)} %get-tuple-element.22), kind=kOutput, calls=%fused_computation.1 | convolution fusion | flops 1619001344 | bytes 5537792 | tf_op jit(solution)/shard_map/chts,cshp->cthp/dot_general | solution.py:119
  157.4 3.0 %copy.68 = f32[4,512,256]{2,1,0:T(8,128)} copy(f32[4,512,256]{1,2,0:T(8,128)} %bitcast_multiply_fusion) | data formatting | bytes 4194304 | tf_op jit(solution)/shard_map/jit(silu)/mul | solution.py:186
  160.5 3.2 %collective-permute-start.7 = (f32[8,65,128]{2,1,0:T(8,128)}, f32[8,65,128]{2,1,0:T(8,128)S(1)}, u32[]{:S(2)}, u32[]{:S(2)}) collective-permute-start(f32[8,65,128]{2,1,0:T(8,128)} %pad_maximum_fusion.3), channel_id=1, source_target_pairs={{0,96},{8,104},{16,112},{24,120},{32,128},{40,136},{48,144},{56,15... | collective-permute-start | bytes 798728 | tf_op jit(solution)/shard_map/ppermute | solution.py:18
  163.9 3.8 %collective-permute-done.7 = f32[8,65,128]{2,1,0:T(8,128)S(1)} collective-permute-done((f32[8,65,128]{2,1,0:T(8,128)}, f32[8,65,128]{2,1,0:T(8,128)S(1)}, u32[]{:S(2)}, u32[]{:S(2)}) %collective-permute-start.7) | collective-permute-done | bytes 266272 | tf_op jit(solution)/shard_map/ppermute | solution.py:18
  167.7 0.8 add_bitcast_fusion
  168.6 3.3 %fusion.30 = (bf16[4,8,8,8,256]{4,3,2,1,0:T(8,128)(2,1)S(1)}, bf16[4,256]{1,0:T(4,128)(2,1)S(1)}) fusion(f32[8,64]{1,0:T(8,128)S(1)} %mul.486, f32[4,256,8,64]{1,3,2,0:T(8,128)S(1)} %bitcast.150, f32[4,256,8,64]{1,0,3,2:T(4,128)S(1)} %copy-done.1, f32[8]{0:T(128)S(1)} %copy-done.16, f32[4,256,8]{1,2,0:T(8,128)S(1)} %get-tuple-element.16, ...), kind=kOutput, calls=%fused_computation.45 | convolution fusion | flops 811334656 | bytes 8687792 | tf_op jit(solution)/shard_map/ctn,chpn->cthp/dot_general | solution.py:179
  172.1 2.4 bitcast_convert_fusion
  174.5 2.3 pad_maximum_fusion
  176.8 58.2 %reduce-scatter.2.cloned.1.call-done = bf16[1028,256]{1,0:T(8,128)(2,1)} async-done(((bf16[1028,2048]{1,0:T(8,128)(2,1)}), bf16[1028,256]{1,0:T(8,128)(2,1)}) %reduce-scatter.2.cloned.1.call-update) | async-done | bytes 526352 | tf_op jit(solution)/shard_map/reduce_scatter | solution.py:200
  235.1 1.1 convert_element_type.38
  236.2 1.0 fusion.31
  (90 shorter events, 2.9 us)
Async XLA Ops:
  7.2 164.9 %copy-start = (bf16[512,2048]{1,0:T(8,128)(2,1)S(1)}, bf16[512,2048]{1,0:T(8,128)(2,1)}, u32[]{:S(2)}) copy-start(bf16[512,2048]{1,0:T(8,128)(2,1)} %param.29) | copy-start | bytes 6291460
  7.2 65.1 %all-gather.2.cloned.1.call-start = ((), (), s32[]{:S(2)}) async-start(), calls=%async_computation.1 | async-start | bytes 4718592 | tf_op jit(solution)/shard_map/all_gather | solution.py:76
  7.9 227.1 %reduce-scatter.2.cloned.1.call-start = ((), (), s32[]{:S(2)}) async-start(), calls=%async_computation.2 | async-start | bytes 4755456 | tf_op jit(solution)/shard_map/reduce_scatter | solution.py:200
  15.5 63.1 %copy-start.19 = (bf16[2048,256]{1,0:T(8,128)(2,1)S(1)}, bf16[2048,256]{1,0:T(8,128)(2,1)}, u32[]{:S(2)}) copy-start(bf16[2048,256]{1,0:T(8,128)(2,1)} %param.19) | copy-start | bytes 3145732
  78.6 3.6 %copy-start.3 = (bf16[1024,2048]{1,0:T(8,128)(2,1)S(1)}, bf16[1024,2048]{1,0:T(8,128)(2,1)}, u32[]{:S(2)}) copy-start(bf16[1024,2048]{1,0:T(8,128)(2,1)} %all-gather.2.cloned.1.call-done) | copy-start | bytes 12582916
  78.6 4.1 %copy-start.17 = (bf16[2048,512]{1,0:T(8,128)(2,1)S(1)}, bf16[2048,512]{1,0:T(8,128)(2,1)}, u32[]{:S(2)}) copy-start(bf16[2048,512]{1,0:T(8,128)(2,1)} %param.18) | copy-start | bytes 6291460
  82.8 10.6 %copy-start.15 = (f32[256]{0:T(256)S(1)}, f32[256]{0:T(256)}, u32[]{:S(2)}) copy-start(f32[256]{0:T(256)} %param.24) | copy-start | bytes 3076
  85.1 8.1 %collective-permute-start = (bf16[3,768]{1,0:T(4,128)(2,1)S(1)}, bf16[3,768]{1,0:T(4,128)(2,1)S(1)}, u32[]{:S(2)}, u32[]{:S(2)}) collective-permute-start(bf16[3,768]{1,0:T(4,128)(2,1)S(1)} %pad_maximum_fusion.4), channel_id=1, source_target_pairs={{0,8},{8,16},{16,24},{24,32},{32,40},{40,48},{48,56},{56,64},{64,7... | collective-permute-start | bytes 13832 | tf_op jit(solution)/shard_map/ppermute | solution.py:18
  94.7 1.1 copy-start.14
  95.5 12.2 %copy-start.9 = (bf16[1024,128]{1,0:T(8,128)(2,1)}, bf16[1024,128]{1,0:T(8,128)(2,1)S(1)}, u32[]{:S(2)}) copy-start(bf16[1024,128]{1,0:T(8,128)(2,1)S(1)} %get-tuple-element.26) | copy-start | bytes 786436
  105.1 19.3 %copy-start.18 = (bf16[2048,512]{1,0:T(8,128)(2,1)S(1)}, bf16[2048,512]{1,0:T(8,128)(2,1)}, u32[]{:S(2)}) copy-start(bf16[2048,512]{1,0:T(8,128)(2,1)} %param.17) | copy-start | bytes 6291460
  107.7 16.7 %copy-start.4 = (bf16[1024,2048]{1,0:T(8,128)(2,1)S(1)}, bf16[1024,2048]{1,0:T(8,128)(2,1)}, u32[]{:S(2)}) copy-start(bf16[1024,2048]{1,0:T(8,128)(2,1)} %all-gather.2.cloned.1.call-done) | copy-start | bytes 12582916
  109.1 27.4 %copy-start.5 = (f32[8,64,128]{2,1,0:T(8,128)}, f32[8,64,128]{2,1,0:T(8,128)S(1)}, u32[]{:S(2)}) copy-start(f32[8,64,128]{2,1,0:T(8,128)S(1)} %get-tuple-element.15) | copy-start | bytes 786436
  109.2 19.5 %collective-permute-start.4 = (f32[8,65,128]{2,1,0:T(8,128)S(1)}, f32[8,65,128]{2,1,0:T(8,128)S(1)}, u32[]{:S(2)}, u32[]{:S(2)}) collective-permute-start(f32[8,65,128]{2,1,0:T(8,128)S(1)} %pad_maximum_fusion.2), channel_id=1, source_target_pairs={{0,32},{8,40},{16,48},{24,56},{32,64},{40,72},{48,80},{56,88},{64,... | collective-permute-start | bytes 798728 | tf_op jit(solution)/shard_map/ppermute | solution.py:18
  113.6 15.1 %collective-permute-start.3 = (f32[8,65,128]{2,1,0:T(8,128)S(1)}, f32[8,65,128]{2,1,0:T(8,128)S(1)}, u32[]{:S(2)}, u32[]{:S(2)}) collective-permute-start(f32[8,65,128]{2,1,0:T(8,128)S(1)} %pad_maximum_fusion.2), channel_id=1, source_target_pairs={{0,24},{8,32},{16,40},{24,48},{32,56},{40,64},{48,72},{56,80},{64,... | collective-permute-start | bytes 798728 | tf_op jit(solution)/shard_map/ppermute | solution.py:18
  120.4 12.7 %collective-permute-start.2 = (f32[8,65,128]{2,1,0:T(8,128)S(1)}, f32[8,65,128]{2,1,0:T(8,128)S(1)}, u32[]{:S(2)}, u32[]{:S(2)}) collective-permute-start(f32[8,65,128]{2,1,0:T(8,128)S(1)} %pad_maximum_fusion.2), channel_id=1, source_target_pairs={{0,16},{8,24},{16,32},{24,40},{32,48},{40,56},{48,64},{56,72},{64,... | collective-permute-start | bytes 798728 | tf_op jit(solution)/shard_map/ppermute | solution.py:18
  121.7 14.5 %collective-permute-start.1 = (f32[8,65,128]{2,1,0:T(8,128)S(1)}, f32[8,65,128]{2,1,0:T(8,128)S(1)}, u32[]{:S(2)}, u32[]{:S(2)}) collective-permute-start(f32[8,65,128]{2,1,0:T(8,128)S(1)} %pad_maximum_fusion.2), channel_id=1, source_target_pairs={{0,8},{8,16},{16,24},{24,32},{32,40},{40,48},{48,56},{56,64},{64,7... | collective-permute-start | bytes 798728 | tf_op jit(solution)/shard_map/ppermute | solution.py:18
  124.4 4.0 %copy-start.10 = (bf16[1024,128]{1,0:T(8,128)(2,1)S(1)}, bf16[1024,128]{1,0:T(8,128)(2,1)}, u32[]{:S(2)}) copy-start(bf16[1024,128]{1,0:T(8,128)(2,1)} %copy-done.9) | copy-start | bytes 786436
  124.4 4.0 %copy-start.11 = (bf16[1024,128]{1,0:T(8,128)(2,1)S(1)}, bf16[1024,128]{1,0:T(8,128)(2,1)}, u32[]{:S(2)}) copy-start(bf16[1024,128]{1,0:T(8,128)(2,1)} %get-tuple-element.25) | copy-start | bytes 786436
  136.3 10.3 %copy-start.13 = (pred[4,256,256]{2,1,0:T(8,128)(4,1)S(1)}, pred[4,256,256]{2,1,0:T(8,128)(4,1)}, u32[]{:S(2)}) copy-start(pred[4,256,256]{2,1,0:T(8,128)(4,1)} %compare_and_fusion) | copy-start | bytes 786436
  136.6 0.7 copy-start.7
  138.1 25.7 %collective-permute-start.6 = (f32[8,65,128]{2,1,0:T(8,128)}, f32[8,65,128]{2,1,0:T(8,128)}, u32[]{:S(2)}, u32[]{:S(2)}) collective-permute-start(f32[8,65,128]{2,1,0:T(8,128)} %pad_maximum_fusion.3), channel_id=1, source_target_pairs={{0,64},{8,72},{16,80},{24,88},{32,96},{40,104},{48,112},{56,120},{... | collective-permute-start | bytes 798728 | tf_op jit(solution)/shard_map/ppermute | solution.py:18
  141.9 21.9 %collective-permute-start.5 = (f32[8,65,128]{2,1,0:T(8,128)}, f32[8,65,128]{2,1,0:T(8,128)}, u32[]{:S(2)}, u32[]{:S(2)}) collective-permute-start(f32[8,65,128]{2,1,0:T(8,128)} %pad_maximum_fusion.3), channel_id=1, source_target_pairs={{0,32},{8,40},{16,48},{24,56},{32,64},{40,72},{48,80},{56,88},{64,... | collective-permute-start | bytes 798728 | tf_op jit(solution)/shard_map/ppermute | solution.py:18
  160.4 7.3 %copy-start.6 = (f32[8,64,128]{2,1,0:T(8,128)S(1)}, f32[8,64,128]{2,1,0:T(8,128)}, u32[]{:S(2)}) copy-start(f32[8,64,128]{2,1,0:T(8,128)} %copy-done.5) | copy-start | bytes 786436
  160.4 7.3 %copy-start.8 = (f32[8,64,128]{2,1,0:T(8,128)S(1)}, f32[8,64,128]{2,1,0:T(8,128)}, u32[]{:S(2)}) copy-start(f32[8,64,128]{2,1,0:T(8,128)} %copy-done.7) | copy-start | bytes 786436
  160.4 8.2 %copy-start.2 = (f32[4,512,256]{2,1,0:T(8,128)S(1)}, f32[4,512,256]{2,1,0:T(8,128)}, u32[]{:S(2)}) copy-start(f32[4,512,256]{2,1,0:T(8,128)} %copy.68) | copy-start | bytes 6291460
  160.5 8.0 %copy-start.1 = (f32[4,256,8,64]{1,0,3,2:T(4,128)S(1)}, f32[4,256,8,64]{1,0,3,2:T(4,128)}, u32[]{:S(2)}) copy-start(f32[4,256,8,64]{1,0,3,2:T(4,128)} %reshape.219) | copy-start | bytes 6291460
  160.5 8.0 %copy-start.12 = (bf16[1024,128]{1,0:T(8,128)(2,1)S(1)}, bf16[1024,128]{1,0:T(8,128)(2,1)}, u32[]{:S(2)}) copy-start(bf16[1024,128]{1,0:T(8,128)(2,1)} %get-tuple-element.25) | copy-start | bytes 786436
  160.5 8.0 %copy-start.16 = (f32[8]{0:T(128)S(1)}, f32[8]{0:T(128)}, u32[]{:S(2)}) copy-start(f32[8]{0:T(128)} %param.27) | copy-start | bytes 100
  160.5 7.2 %collective-permute-start.7 = (f32[8,65,128]{2,1,0:T(8,128)}, f32[8,65,128]{2,1,0:T(8,128)S(1)}, u32[]{:S(2)}, u32[]{:S(2)}) collective-permute-start(f32[8,65,128]{2,1,0:T(8,128)} %pad_maximum_fusion.3), channel_id=1, source_target_pairs={{0,96},{8,104},{16,112},{24,120},{32,128},{40,136},{48,144},{56,15... | collective-permute-start | bytes 798728 | tf_op jit(solution)/shard_map/ppermute | solution.py:18
Sparse Core Ops, SparseCore 0:
  9.7 62.5 all-gather.1
  176.9 58.0 reduce-scatter.1

commit v8 on v7

--- a/solution.py
+++ b/solution.py
@@ -140,11 +140,16 @@
     packed = jnp.concatenate([running_state, gain_row], 1)
     identity = jnp.concatenate([0.0 * running_state, 1.0 + 0.0 * gain_row], 1)
     late_piece, packed = lax.optimization_barrier((piece, packed))
-    gate_turned = jnp.einsum(
-        "ctd,dk->ckt",
-        late_piece.reshape(rows_here // GROUP, GROUP, late_piece.shape[1]),
-        w_gate,
-        preferred_element_type=jnp.float32,
+    gate_turned = jnp.stack(
+        [
+            jnp.dot(
+                w_gate.T,
+                late_piece[group_no * GROUP : (group_no + 1) * GROUP].T,
+                preferred_element_type=jnp.float32,
+            )
+            for group_no in range(rows_here // GROUP)
+        ],
+        0,
     )
 
     def joined_of(earlier_part, later_part):

time: 245 us -> 245 us (level)
  waiting for transfers between devices: 128 us -> 120 us
  local copies, waits for them, and re-layouts: 15.9 us -> 21.8 us
    dot_general x0 -> x4, local copies, waits for them, and re-layouts: none -> 8.17 us  [shards(): jnp.dot(w_gate.T, late_piece[group_no * GROUP:(group_no + 1) * GROUP].T,...]
    ppermute x8, waiting for transfers between devices: 11.9 us -> 4.4 us  [shifted(): return lax.ppermute(x, axis, pairs)]
    mul x1 -> x0, local copies, waits for them, and re-layouts: 2.96 us -> none  [shards(): jax.nn.silu(gate_turned).reshape(count, heads_here, head_width, GROUP)]
    dot_general x1 -> x4, matrix products: 3.97 us -> 6 us  [shards(): jnp.dot(w_gate.T, late_piece[group_no * GROUP:(group_no + 1) * GROUP].T,...]
  transfers between devices with their start and end apart: 10 -> 10, of which waited for: 6 -> 4; matrix products, arithmetic and copies ran while one was open for 11% -> 12% of each run, Pallas kernels for 0% -> 0%
where the time goes in v8:
time: 245 us; the launch traced here: 244 us
  waiting for transfers between devices  120 us (49%)
  matrix products  33.7 us (14%)
  starting transfers between devices  33.4 us (14%)
  local copies, waits for them, and re-layouts  21.8 us (9%)
  other arithmetic  20.3 us (8%)
  between operations  14.6 us (6%)
    reduce_scatter x1, waiting for transfers between devices, shards(): lax.psum_scatter(joined.astype(jnp.bfloat16), 'head', scatter_dimension=1...  58.2 us
    all_gather x1, waiting for transfers between devices, shards(): piece = lax.all_gather(tokens, 'head', axis=1, tiled=True)  56.7 us
    ppermute x8, starting transfers between devices, shifted(): return lax.ppermute(x, axis, pairs)  33.3 us
    dot_general x1, matrix products, shards(): jnp.einsum('chts,cshp->cthp', decays * scores[:, None, :, :], group_x, pr...  10.9 us
    dot_general x3, matrix products, partial_product(): return jnp.dot(piece, matrix, preferred_element_type=jnp.float32)  9.33 us
    dot_general x4, local copies, waits for them, and re-layouts, shards(): jnp.dot(w_gate.T, late_piece[group_no * GROUP:(group_no + 1) * GROUP].T,...  8.17 us
    reshape x2, local copies, waits for them, and re-layouts, shards(): x_conv.astype(jnp.float32).reshape(rows_here, heads_here, head_width)  6.15 us
    dot_general x4, matrix products, shards(): jnp.dot(w_gate.T, late_piece[group_no * GROUP:(group_no + 1) * GROUP].T,...  6 us
  transfers between devices with their start and end apart: 10, of which 4 were waited for; matrix products, arithmetic and copies ran while one was open for 12% of the time, Pallas kernels for 0%

profile of v8, /device:TPU:1, one launch (start us, length us, event | category | flops | bytes accessed | tf_op | source)
XLA Modules:
  0.0 243.7 jit_solution(9496241439324483595)
XLA Ops:
  7.2 0.7 all-gather.2.cloned.1.call-update
  8.0 0.8 mul.487
  8.7 0.7 dynamic_slice.7
  9.4 0.8 broadcast_select_fusion.6
  11.0 0.7 pad_add_fusion.1
  11.9 0.8 fusion.68
  12.9 0.8 fusion.79
  13.7 0.9 fusion.77
  14.6 1.0 compare_and_fusion
  15.6 56.7 %all-gather.2.cloned.1.call-done = bf16[1024,2048]{1,0:T(8,128)(2,1)} async-done(((bf16[1024,256]{1,0:T(8,128)(2,1)}), bf16[1024,2048]{1,0:T(8,128)(2,1)}) %all-gather.2.cloned.1.call-update) | async-done | bytes 4194320 | tf_op jit(solution)/shard_map/all_gather | solution.py:76
  72.3 3.4 %negate_multiply_fusion = (f32[1024,8]{0,1:T(8,128)S(1)}, f32[1024,8]{0,1:T(8,128)S(1)}) fusion(f32[8]{0:T(128)} %param.26, f32[8]{0:T(128)} %param.25, bf16[1024,2048]{1,0:T(8,128)(2,1)} %all-gather.2.cloned.1.call-done, bf16[2048,8]{0,1:T(8,128)(2,1)} %param.20), kind=kOutput, calls=%fused_computation.120 | convolution fusion | flops 33628160 | bytes 4292672 | tf_op jit(solution)/shard_map/dot_general | solution.py:79
  75.7 2.3 reduce-window.6
  78.6 3.6 %convolution_convert_fusion.1 = bf16[1024,256]{1,0:T(8,128)(2,1)S(1)} fusion(bf16[1024,2048]{1,0:T(8,128)(2,1)} %all-gather.2.cloned.1.call-done, bf16[2048,256]{1,0:T(8,128)(2,1)S(1)} %copy-done.21), kind=kOutput, calls=%fused_computation.36 | convolution fusion | flops 1074003968 | bytes 5767168 | tf_op jit(solution)/shard_map/dot_general | solution.py:79
  82.8 2.3 convolution_convert_fusion
  85.1 7.4 %collective-permute-start = (bf16[3,768]{1,0:T(4,128)(2,1)S(1)}, bf16[3,768]{1,0:T(4,128)(2,1)S(1)}, u32[]{:S(2)}, u32[]{:S(2)}) collective-permute-start(bf16[3,768]{1,0:T(4,128)(2,1)S(1)} %pad_maximum_fusion.5), channel_id=1, source_target_pairs={{0,8},{8,16},{16,24},{24,32},{32,40},{40,48},{48,56},{56,64},{64,7... | collective-permute-start | bytes 13832 | tf_op jit(solution)/shard_map/ppermute | solution.py:18
  93.4 1.3 multiply_convert_fusion.2
  94.7 0.8 fusion.76
  95.8 3.1 %fusion.41 = f32[1024,512]{1,0:T(8,128)} fusion(f32[512]{0:T(512)S(1)} %copy-done.17, f32[512]{0:T(512)S(1)} %bitcast.171, f32[1027,512]{1,0:T(8,128)S(1)} %maximum_convert_fusion, pred[1024]{0:T(1024)(128)(4,1)S(1)} %get-tuple-element.43, f32[512]{0:T(512)S(1)} %bitcast.172, pred[1024]{0:T(1024)(128)(4,1)S(1)} %get-tuple-element.44, f32[512]{0:T(512)S(1)} %bitcast.170, ...), kind=kLoop, calls=%fused_computation.72 | loop fusion | flops 8912896 | bytes 10499072 | tf_op jit(solution)/shard_map/reshape | solution.py:103
  99.0 3.0 %copy.72 = f32[1024,512]{0,1:T(8,128)} copy(f32[1024,512]{1,0:T(8,128)} %fusion.41) | data formatting | bytes 4194304 | tf_op jit(solution)/shard_map/reshape | solution.py:103
  102.0 3.2 %reshape.220 = f32[4,256,8,64]{1,0,3,2:T(4,128)} reshape(f32[1024,512]{0,1:T(8,128)} %copy.72) | data formatting | bytes 4194304 | tf_op jit(solution)/shard_map/reshape | solution.py:103
  105.1 2.6 %broadcast_multiply_fusion = (f32[4,256,8,64]{1,0,3,2:T(4,128)S(1)}, f32[4,256,8,64]{1,0,3,2:T(4,128)S(1)}) fusion(f32[4,256,8]{1,0,2:T(4,128)S(1)} %copy.77, f32[4,256,8,64]{1,0,3,2:T(4,128)} %reshape.220, f32[4,256,8]{1,0,2:T(4,128)S(1)} %copy.73), kind=kLoop, calls=%fused_computation.68 | loop fusion | flops 1048576 | bytes 6356992 | tf_op jit(solution)/shard_map/mul | solution.py:125
  107.7 1.3 fusion.19
  109.9 1.5 convolution_bitcast_fusion
  111.4 1.5 convolution_bitcast_fusion.1
  112.9 4.3 %collective-permute-start.4 = (f32[8,65,128]{2,1,0:T(8,128)S(1)}, f32[8,65,128]{2,1,0:T(8,128)S(1)}, u32[]{:S(2)}, u32[]{:S(2)}) collective-permute-start(f32[8,65,128]{2,1,0:T(8,128)S(1)} %pad_maximum_fusion.3), channel_id=1, source_target_pairs={{0,32},{8,40},{16,48},{24,56},{32,64},{40,72},{48,80},{56,88},{64,... | collective-permute-start | bytes 798728 | tf_op jit(solution)/shard_map/ppermute | solution.py:18
  117.3 6.8 %collective-permute-start.3 = (f32[8,65,128]{2,1,0:T(8,128)S(1)}, f32[8,65,128]{2,1,0:T(8,128)S(1)}, u32[]{:S(2)}, u32[]{:S(2)}) collective-permute-start(f32[8,65,128]{2,1,0:T(8,128)S(1)} %pad_maximum_fusion.3), channel_id=1, source_target_pairs={{0,24},{8,32},{16,40},{24,48},{32,56},{40,64},{48,72},{56,80},{64,... | collective-permute-start | bytes 798728 | tf_op jit(solution)/shard_map/ppermute | solution.py:18
  124.1 1.3 collective-permute-start.2
  125.4 2.6 %collective-permute-start.1 = (f32[8,65,128]{2,1,0:T(8,128)S(1)}, f32[8,65,128]{2,1,0:T(8,128)S(1)}, u32[]{:S(2)}, u32[]{:S(2)}) collective-permute-start(f32[8,65,128]{2,1,0:T(8,128)S(1)} %pad_maximum_fusion.3), channel_id=1, source_target_pairs={{0,8},{8,16},{16,24},{24,32},{32,40},{40,48},{48,56},{56,64},{64,7... | collective-permute-start | bytes 798728 | tf_op jit(solution)/shard_map/ppermute | solution.py:18
  128.4 10.9 %fusion = f32[4,8,64,256]{3,2,1,0:T(8,128)} fusion(f32[4,256,256]{2,1,0:T(8,128)S(1)} %fusion.81, f32[4,8,256]{2,1,0:T(8,128)S(1)} %add_bitcast_fusion.2, pred[4,256,256]{2,1,0:T(8,128)(4,1)S(1)} %copy-done.16, f32[4,256,8,64]{1,0,3,2:T(4,128)S(1)} %get-tuple-element.22), kind=kOutput, calls=%fused_computation.1 | convolution fusion | flops 1619001344 | bytes 5537792 | tf_op jit(solution)/shard_map/chts,cshp->cthp/dot_general | solution.py:119
  139.2 1.5 convolution_bitcast_fusion.2
  141.1 0.7 copy-done.6
  141.8 0.8 pad_maximum_fusion.4
  142.6 3.9 %collective-permute-start.6 = (f32[8,65,128]{2,1,0:T(8,128)}, f32[8,65,128]{2,1,0:T(8,128)}, u32[]{:S(2)}, u32[]{:S(2)}) collective-permute-start(f32[8,65,128]{2,1,0:T(8,128)} %pad_maximum_fusion.4), channel_id=1, source_target_pairs={{0,64},{8,72},{16,80},{24,88},{32,96},{40,104},{48,112},{56,120},{... | collective-permute-start | bytes 798728 | tf_op jit(solution)/shard_map/ppermute | solution.py:18
  146.5 4.4 %collective-permute-start.5 = (f32[8,65,128]{2,1,0:T(8,128)}, f32[8,65,128]{2,1,0:T(8,128)}, u32[]{:S(2)}, u32[]{:S(2)}) collective-permute-start(f32[8,65,128]{2,1,0:T(8,128)} %pad_maximum_fusion.4), channel_id=1, source_target_pairs={{0,32},{8,40},{16,48},{24,56},{32,64},{40,72},{48,80},{56,88},{64,... | collective-permute-start | bytes 798728 | tf_op jit(solution)/shard_map/ppermute | solution.py:18
  150.8 1.5 convolution_bitcast_fusion.3
  152.3 2.0 copy.83
  154.4 2.0 copy.82
  156.4 2.0 copy.81
  158.5 2.1 copy.80
  160.7 2.5 %collective-permute-start.7 = (f32[8,65,128]{2,1,0:T(8,128)}, f32[8,65,128]{2,1,0:T(8,128)S(1)}, u32[]{:S(2)}, u32[]{:S(2)}) collective-permute-start(f32[8,65,128]{2,1,0:T(8,128)} %pad_maximum_fusion.4), channel_id=1, source_target_pairs={{0,96},{8,104},{16,112},{24,120},{32,128},{40,136},{48,144},{56,15... | collective-permute-start | bytes 798728 | tf_op jit(solution)/shard_map/ppermute | solution.py:18
  163.4 3.8 %collective-permute-done.7 = f32[8,65,128]{2,1,0:T(8,128)S(1)} collective-permute-done((f32[8,65,128]{2,1,0:T(8,128)}, f32[8,65,128]{2,1,0:T(8,128)S(1)}, u32[]{:S(2)}, u32[]{:S(2)}) %collective-permute-start.7) | collective-permute-done | bytes 266272 | tf_op jit(solution)/shard_map/ppermute | solution.py:18
  167.2 0.8 add_bitcast_fusion
  168.1 3.5 %fusion.22 = (bf16[4,8,8,8,256]{4,3,2,1,0:T(8,128)(2,1)S(1)}, bf16[4,256]{1,0:T(4,128)(2,1)S(1)}) fusion(f32[8,64]{1,0:T(8,128)S(1)} %mul.487, f32[1,8,64,256]{3,2,1,0:T(8,128)S(1)} %bitcast.154, f32[1,8,64,256]{3,2,1,0:T(8,128)S(1)} %bitcast.155, f32[1,8,64,256]{3,2,1,0:T(8,128)S(1)} %bitcast.156, f32[1,8,64,256]{3,2,1,0:T(8,128)S(1)} %bitcast.157, ...), kind=kOutput, calls=%fused_computation.43 | convolution fusion | flops 815004672 | bytes 8687792 | tf_op jit(solution)/shard_map/ctn,chpn->cthp/dot_general | solution.py:184
  171.8 2.4 bitcast_convert_fusion
  174.2 2.3 pad_maximum_fusion
  176.5 58.2 %reduce-scatter.2.cloned.1.call-done = bf16[1028,256]{1,0:T(8,128)(2,1)} async-done(((bf16[1028,2048]{1,0:T(8,128)(2,1)}), bf16[1028,256]{1,0:T(8,128)(2,1)}) %reduce-scatter.2.cloned.1.call-update) | async-done | bytes 526352 | tf_op jit(solution)/shard_map/reduce_scatter | solution.py:205
  234.7 1.1 convert_element_type.38
  235.9 1.0 fusion.23
  (102 shorter events, 5.5 us)
Async XLA Ops:
  7.2 164.6 %copy-start = (bf16[512,2048]{1,0:T(8,128)(2,1)S(1)}, bf16[512,2048]{1,0:T(8,128)(2,1)}, u32[]{:S(2)}) copy-start(bf16[512,2048]{1,0:T(8,128)(2,1)} %param.29) | copy-start | bytes 6291460
  7.2 65.1 %all-gather.2.cloned.1.call-start = ((), (), s32[]{:S(2)}) async-start(), calls=%async_computation.1 | async-start | bytes 4718592 | tf_op jit(solution)/shard_map/all_gather | solution.py:76
  7.9 226.8 %reduce-scatter.2.cloned.1.call-start = ((), (), s32[]{:S(2)}) async-start(), calls=%async_computation.2 | async-start | bytes 4755456 | tf_op jit(solution)/shard_map/reduce_scatter | solution.py:205
  15.6 63.1 %copy-start.21 = (bf16[2048,256]{1,0:T(8,128)(2,1)S(1)}, bf16[2048,256]{1,0:T(8,128)(2,1)}, u32[]{:S(2)}) copy-start(bf16[2048,256]{1,0:T(8,128)(2,1)} %param.19) | copy-start | bytes 3145732
  78.6 3.6 %copy-start.2 = (bf16[1024,2048]{1,0:T(8,128)(2,1)S(1)}, bf16[1024,2048]{1,0:T(8,128)(2,1)}, u32[]{:S(2)}) copy-start(bf16[1024,2048]{1,0:T(8,128)(2,1)} %all-gather.2.cloned.1.call-done) | copy-start | bytes 12582916
  78.6 4.1 %copy-start.19 = (bf16[2048,512]{1,0:T(8,128)(2,1)S(1)}, bf16[2048,512]{1,0:T(8,128)(2,1)}, u32[]{:S(2)}) copy-start(bf16[2048,512]{1,0:T(8,128)(2,1)} %param.18) | copy-start | bytes 6291460
  82.8 10.6 %copy-start.18 = (f32[256]{0:T(256)S(1)}, f32[256]{0:T(256)}, u32[]{:S(2)}) copy-start(f32[256]{0:T(256)} %param.24) | copy-start | bytes 3076
  85.1 8.1 %collective-permute-start = (bf16[3,768]{1,0:T(4,128)(2,1)S(1)}, bf16[3,768]{1,0:T(4,128)(2,1)S(1)}, u32[]{:S(2)}, u32[]{:S(2)}) collective-permute-start(bf16[3,768]{1,0:T(4,128)(2,1)S(1)} %pad_maximum_fusion.5), channel_id=1, source_target_pairs={{0,8},{8,16},{16,24},{24,32},{32,40},{40,48},{48,56},{56,64},{64,7... | collective-permute-start | bytes 13832 | tf_op jit(solution)/shard_map/ppermute | solution.py:18
  94.7 1.1 copy-start.17
  95.5 12.2 %copy-start.8 = (bf16[1024,128]{1,0:T(8,128)(2,1)}, bf16[1024,128]{1,0:T(8,128)(2,1)S(1)}, u32[]{:S(2)}) copy-start(bf16[1024,128]{1,0:T(8,128)(2,1)S(1)} %get-tuple-element.25) | copy-start | bytes 786436
  105.1 4.1 %copy-start.20 = (bf16[2048,512]{1,0:T(8,128)(2,1)S(1)}, bf16[2048,512]{1,0:T(8,128)(2,1)}, u32[]{:S(2)}) copy-start(bf16[2048,512]{1,0:T(8,128)(2,1)} %param.17) | copy-start | bytes 6291460
  107.7 2.2 copy-start.3
  109.2 31.9 %copy-start.4 = (f32[8,64,128]{2,1,0:T(8,128)}, f32[8,64,128]{2,1,0:T(8,128)S(1)}, u32[]{:S(2)}) copy-start(f32[8,64,128]{2,1,0:T(8,128)S(1)} %get-tuple-element.15) | copy-start | bytes 786436
  111.4 16.7 %copy-start.9 = (bf16[1024,128]{1,0:T(8,128)(2,1)S(1)}, bf16[1024,128]{1,0:T(8,128)(2,1)}, u32[]{:S(2)}) copy-start(bf16[1024,128]{1,0:T(8,128)(2,1)} %copy-done.8) | copy-start | bytes 786436
  111.4 16.7 %copy-start.10 = (bf16[1024,128]{1,0:T(8,128)(2,1)S(1)}, bf16[1024,128]{1,0:T(8,128)(2,1)}, u32[]{:S(2)}) copy-start(bf16[1024,128]{1,0:T(8,128)(2,1)} %get-tuple-element.26) | copy-start | bytes 786436
  111.4 17.0 %copy-start.16 = (pred[4,256,256]{2,1,0:T(8,128)(4,1)S(1)}, pred[4,256,256]{2,1,0:T(8,128)(4,1)}, u32[]{:S(2)}) copy-start(pred[4,256,256]{2,1,0:T(8,128)(4,1)} %compare_and_fusion) | copy-start | bytes 786436
  112.9 27.9 %collective-permute-start.4 = (f32[8,65,128]{2,1,0:T(8,128)S(1)}, f32[8,65,128]{2,1,0:T(8,128)S(1)}, u32[]{:S(2)}, u32[]{:S(2)}) collective-permute-start(f32[8,65,128]{2,1,0:T(8,128)S(1)} %pad_maximum_fusion.3), channel_id=1, source_target_pairs={{0,32},{8,40},{16,48},{24,56},{32,64},{40,72},{48,80},{56,88},{64,... | collective-permute-start | bytes 798728 | tf_op jit(solution)/shard_map/ppermute | solution.py:18
  117.3 23.5 %collective-permute-start.3 = (f32[8,65,128]{2,1,0:T(8,128)S(1)}, f32[8,65,128]{2,1,0:T(8,128)S(1)}, u32[]{:S(2)}, u32[]{:S(2)}) collective-permute-start(f32[8,65,128]{2,1,0:T(8,128)S(1)} %pad_maximum_fusion.3), channel_id=1, source_target_pairs={{0,24},{8,32},{16,40},{24,48},{32,56},{40,64},{48,72},{56,80},{64,... | collective-permute-start | bytes 798728 | tf_op jit(solution)/shard_map/ppermute | solution.py:18
  124.1 16.7 %collective-permute-start.2 = (f32[8,65,128]{2,1,0:T(8,128)S(1)}, f32[8,65,128]{2,1,0:T(8,128)S(1)}, u32[]{:S(2)}, u32[]{:S(2)}) collective-permute-start(f32[8,65,128]{2,1,0:T(8,128)S(1)} %pad_maximum_fusion.3), channel_id=1, source_target_pairs={{0,16},{8,24},{16,32},{24,40},{32,48},{40,56},{48,64},{56,72},{64,... | collective-permute-start | bytes 798728 | tf_op jit(solution)/shard_map/ppermute | solution.py:18
  125.4 15.4 %collective-permute-start.1 = (f32[8,65,128]{2,1,0:T(8,128)S(1)}, f32[8,65,128]{2,1,0:T(8,128)S(1)}, u32[]{:S(2)}, u32[]{:S(2)}) collective-permute-start(f32[8,65,128]{2,1,0:T(8,128)S(1)} %pad_maximum_fusion.3), channel_id=1, source_target_pairs={{0,8},{8,16},{16,24},{24,32},{32,40},{40,48},{48,56},{56,64},{64,7... | collective-permute-start | bytes 798728 | tf_op jit(solution)/shard_map/ppermute | solution.py:18
  141.1 0.7 copy-start.6
  142.6 20.7 %collective-permute-start.6 = (f32[8,65,128]{2,1,0:T(8,128)}, f32[8,65,128]{2,1,0:T(8,128)}, u32[]{:S(2)}, u32[]{:S(2)}) collective-permute-start(f32[8,65,128]{2,1,0:T(8,128)} %pad_maximum_fusion.4), channel_id=1, source_target_pairs={{0,64},{8,72},{16,80},{24,88},{32,96},{40,104},{48,112},{56,120},{... | collective-permute-start | bytes 798728 | tf_op jit(solution)/shard_map/ppermute | solution.py:18
  146.5 16.8 %collective-permute-start.5 = (f32[8,65,128]{2,1,0:T(8,128)}, f32[8,65,128]{2,1,0:T(8,128)}, u32[]{:S(2)}, u32[]{:S(2)}) collective-permute-start(f32[8,65,128]{2,1,0:T(8,128)} %pad_maximum_fusion.4), channel_id=1, source_target_pairs={{0,32},{8,40},{16,48},{24,56},{32,64},{40,72},{48,80},{56,88},{64,... | collective-permute-start | bytes 798728 | tf_op jit(solution)/shard_map/ppermute | solution.py:18
  160.5 6.7 %copy-start.5 = (f32[8,64,128]{2,1,0:T(8,128)S(1)}, f32[8,64,128]{2,1,0:T(8,128)}, u32[]{:S(2)}) copy-start(f32[8,64,128]{2,1,0:T(8,128)} %copy-done.4) | copy-start | bytes 786436
  160.5 6.7 %copy-start.7 = (f32[8,64,128]{2,1,0:T(8,128)S(1)}, f32[8,64,128]{2,1,0:T(8,128)}, u32[]{:S(2)}) copy-start(f32[8,64,128]{2,1,0:T(8,128)} %copy-done.6) | copy-start | bytes 786436
  160.5 7.5 %copy-start.14 = (f32[512,256]{1,0:T(8,128)S(1)}, f32[512,256]{1,0:T(8,128)}, u32[]{:S(2)}) copy-start(f32[512,256]{1,0:T(8,128)} %copy.81) | copy-start | bytes 1572868
  160.5 7.5 %copy-start.15 = (f32[512,256]{1,0:T(8,128)S(1)}, f32[512,256]{1,0:T(8,128)}, u32[]{:S(2)}) copy-start(f32[512,256]{1,0:T(8,128)} %copy.80) | copy-start | bytes 1572868
  160.7 7.4 %copy-start.1 = (f32[4,256,8,64]{1,0,3,2:T(4,128)S(1)}, f32[4,256,8,64]{1,0,3,2:T(4,128)}, u32[]{:S(2)}) copy-start(f32[4,256,8,64]{1,0,3,2:T(4,128)} %reshape.220) | copy-start | bytes 6291460
  160.7 7.4 %copy-start.11 = (bf16[1024,128]{1,0:T(8,128)(2,1)S(1)}, bf16[1024,128]{1,0:T(8,128)(2,1)}, u32[]{:S(2)}) copy-start(bf16[1024,128]{1,0:T(8,128)(2,1)} %get-tuple-element.26) | copy-start | bytes 786436
  160.7 7.4 %copy-start.12 = (f32[512,256]{1,0:T(8,128)S(1)}, f32[512,256]{1,0:T(8,128)}, u32[]{:S(2)}) copy-start(f32[512,256]{1,0:T(8,128)} %copy.83) | copy-start | bytes 1572868
  160.7 7.4 %copy-start.13 = (f32[512,256]{1,0:T(8,128)S(1)}, f32[512,256]{1,0:T(8,128)}, u32[]{:S(2)}) copy-start(f32[512,256]{1,0:T(8,128)} %copy.82) | copy-start | bytes 1572868
  160.7 7.4 %copy-start.22 = (f32[8]{0:T(128)S(1)}, f32[8]{0:T(128)}, u32[]{:S(2)}) copy-start(f32[8]{0:T(128)} %param.27) | copy-start | bytes 100
  160.7 6.5 %collective-permute-start.7 = (f32[8,65,128]{2,1,0:T(8,128)}, f32[8,65,128]{2,1,0:T(8,128)S(1)}, u32[]{:S(2)}, u32[]{:S(2)}) collective-permute-start(f32[8,65,128]{2,1,0:T(8,128)} %pad_maximum_fusion.4), channel_id=1, source_target_pairs={{0,96},{8,104},{16,112},{24,120},{32,128},{40,136},{48,144},{56,15... | collective-permute-start | bytes 798728 | tf_op jit(solution)/shard_map/ppermute | solution.py:18
Sparse Core Ops, SparseCore 0:
  9.7 62.5 all-gather.1
  176.6 58.0 reduce-scatter.1

commit v9 on v8

--- a/solution.py
+++ b/solution.py
@@ -42,6 +42,19 @@
         matches = joined_ids[lag_count - shift_by : lag_count - shift_by + rows_here] == idents
         result = result + jnp.where(matches[:, None], window, 0.0) * weights[shift_by]
     return result + offsets
+
+
+def conv_turned(projected, edge_rows, weights, offsets, idents, earlier):
+    rows_here = projected.shape[1]
+    lag_count = edge_rows.shape[0]
+    joined = jnp.concatenate([edge_rows.T, projected], 1).astype(jnp.float32)
+    joined_ids = jnp.concatenate([earlier, idents], 0)
+    result = joined[:, lag_count:] * weights[0][:, None]
+    for shift_by in range(1, lag_count + 1):
+        window = joined[:, lag_count - shift_by : lag_count - shift_by + rows_here]
+        matches = joined_ids[lag_count - shift_by : lag_count - shift_by + rows_here] == idents
+        result = result + jnp.where(matches[None, :], window, 0.0) * weights[shift_by][:, None]
+    return result + offsets[:, None]
 
 
 def combine(earlier, later):
@@ -78,32 +91,31 @@
     def partial_product(matrix):
         return jnp.dot(piece, matrix, preferred_element_type=jnp.float32)
 
-    x_sum = partial_product(w_x)
+    x_turned = jnp.dot(w_x.T, piece.T, preferred_element_type=jnp.float32).astype(jnp.bfloat16)
     bc_sum = partial_product(w_bc)
     dt_raw = partial_product(w_dt)
-    x_pre = x_sum.astype(jnp.bfloat16)
     bc_pre = bc_sum.astype(jnp.bfloat16)
     idents = lax.dynamic_slice_in_dim(seg_ids, first_row, rows_here)
     earlier = lax.dynamic_slice_in_dim(seg_ids, jnp.maximum(first_row - lag_count, 0), lag_count)
     earlier = jnp.where(device > 0, earlier, -1)
     edges = shifted(
-        jnp.concatenate([x_pre[rows_here - lag_count :], bc_pre[rows_here - lag_count :]], 1),
+        jnp.concatenate([x_turned[:, rows_here - lag_count :].T, bc_pre[rows_here - lag_count :]], 1),
         "seq",
         1,
     )
     edge_x, edge_bc = edges[:, :inner_here], edges[:, inner_here:]
-    x_conv = jax.nn.silu(conv_block(x_pre, edge_x, conv_x, conv_x_bias, idents, earlier)).astype(
-        jnp.bfloat16
-    )
+    x_conv = jax.nn.silu(
+        conv_turned(x_turned, edge_x, conv_x, conv_x_bias, idents, earlier)
+    ).astype(jnp.bfloat16)
     bc_conv = jax.nn.silu(
         conv_block(bc_pre, edge_bc, conv_bc, conv_bc_bias, idents, earlier)
     ).astype(jnp.bfloat16)
     steps_dt = jax.nn.softplus(dt_raw + dt_bias)
     log_decay = -steps_dt * decay_rate
-    x_float = x_conv.astype(jnp.float32).reshape(rows_here, heads_here, head_width)
-    x_scaled = x_float * steps_dt[:, :, None]
+    x_float = x_conv.astype(jnp.float32).reshape(heads_here, head_width, rows_here)
+    x_scaled = x_float * steps_dt.T[:, None, :]
     count = rows_here // GROUP
-    group_x = x_scaled.reshape(count, GROUP, heads_here, head_width)
+    group_x = jnp.transpose(x_scaled.reshape(heads_here, head_width, count, GROUP), (2, 3, 0, 1))
     group_b = bc_conv[:, :state_width].astype(jnp.float32).reshape(count, GROUP, state_width)
     group_c = bc_conv[:, state_width:].astype(jnp.float32).reshape(count, GROUP, state_width)
     group_ids = idents.reshape(count, GROUP)
@@ -190,7 +202,9 @@
     gate_act = jnp.transpose(
         jax.nn.silu(gate_turned).reshape(count, heads_here, head_width, GROUP), (0, 3, 1, 2)
     )
-    direct = skip_gain[:, None] * x_float.reshape(group_shape)
+    direct = jnp.transpose(
+        (skip_gain[:, None, None] * x_float).reshape(heads_here, head_width, count, GROUP), (2, 3, 0, 1)
+    )
     gated = (within + carried + direct) * gate_act
     scaled = (gated * norm_gain.reshape(heads_here, head_width)).astype(jnp.bfloat16)
     partial_out = jnp.einsum(

time: 245 us -> 249 us (1.016)
  matrix products: 33.7 us -> 37.7 us
    mul x1 -> x0, other arithmetic: 2.57 us -> none  [shards(): group_x * tails[:, :, :, None]]
    dot_general x3 -> x2, matrix products: 9.33 us -> 7.35 us  [partial_product(): return jnp.dot(piece, matrix, preferred_element_type=jnp.float32)]
    reshape x2 -> x3, local copies, waits for them, and re-layouts: 6.15 us -> 5.96 us  [the longest x1 3.2 us: shards(): x_conv.astype(jnp.float32).reshape(heads_here, head_width, rows_here)]
  transfers between devices with their start and end apart: 10 -> 10, of which waited for: 4 -> 4; matrix products, arithmetic and copies ran while one was open for 12% -> 14% of each run, Pallas kernels for 0% -> 0%
where the time goes in v9:
time: 249 us
  waiting for transfers between devices  120 us (48%)
  matrix products  37.7 us (15%)
  starting transfers between devices  33.7 us (14%)
  local copies, waits for them, and re-layouts  22.1 us (9%)
  other arithmetic  20.6 us (8%)
  between operations  14.6 us (6%)
    reduce_scatter x1, waiting for transfers between devices, shards(): lax.psum_scatter(joined.astype(jnp.bfloat16), 'head', scatter_dimension=1...  58.2 us
    all_gather x1, waiting for transfers between devices, shards(): piece = lax.all_gather(tokens, 'head', axis=1, tiled=True)  55.6 us
    ppermute x8, starting transfers between devices, shifted(): return lax.ppermute(x, axis, pairs)  33.6 us
    dot_general x1, matrix products, shards(): jnp.einsum('chts,cshp->cthp', decays * scores[:, None, :, :], group_x, pr...  10.9 us
    dot_general x4, local copies, waits for them, and re-layouts, shards(): jnp.dot(w_gate.T, late_piece[group_no * GROUP:(group_no + 1) * GROUP].T,...  8.14 us
    dot_general x4, matrix products, shards(): jnp.dot(w_gate.T, late_piece[group_no * GROUP:(group_no + 1) * GROUP].T,...  7.75 us
    dot_general x2, matrix products, partial_product(): return jnp.dot(piece, matrix, preferred_element_type=jnp.float32)  7.35 us
    ppermute x8, waiting for transfers between devices, shifted(): return lax.ppermute(x, axis, pairs)  5.26 us
  transfers between devices with their start and end apart: 10, of which 4 were waited for; matrix products, arithmetic and copies ran while one was open for 14% of the time, Pallas kernels for 0%

profile of v9, /device:TPU:1, one launch (start us, length us, event | category | flops | bytes accessed | tf_op | source)
XLA Modules:
  0.0 248.5 jit_solution(17277044297272430953)
XLA Ops:
  8.0 1.3 mul.488
  10.0 0.8 broadcast_select_fusion.6
  12.1 0.7 pad_add_fusion.1
  13.0 0.8 fusion.82
  14.0 0.8 fusion.93
  14.9 0.9 fusion.91
  15.7 1.0 compare_and_fusion
  16.7 55.6 %all-gather.2.cloned.1.call-done = bf16[1024,2048]{1,0:T(8,128)(2,1)} async-done(((bf16[1024,256]{1,0:T(8,128)(2,1)}), bf16[1024,2048]{1,0:T(8,128)(2,1)}) %all-gather.2.cloned.1.call-update) | async-done | bytes 4194320 | tf_op jit(solution)/shard_map/all_gather | solution.py:89
  72.3 3.4 %fusion.67 = (f32[1024,8]{0,1:T(8,128)S(1)}, f32[1024,8]{0,1:T(8,128)S(1)}) fusion(f32[8]{0:T(128)} %param.26, f32[8]{0:T(128)} %param.25, bf16[1024,2048]{1,0:T(8,128)(2,1)} %all-gather.2.cloned.1.call-done, bf16[2048,8]{0,1:T(8,128)(2,1)} %param.20), kind=kOutput, calls=%fused_computation.131 | convolution fusion | flops 33628160 | bytes 4292672 | tf_op jit(solution)/shard_map/dot_general | solution.py:92
  75.7 2.3 reduce-window.6
  79.7 3.9 %convolution_convert_fusion.1 = bf16[1024,256]{0,1:T(8,128)(2,1)S(1)} fusion(bf16[1024,2048]{1,0:T(8,128)(2,1)} %all-gather.2.cloned.1.call-done, bf16[2048,256]{1,0:T(8,128)(2,1)} %param.19), kind=kOutput, calls=%fused_computation.36 | convolution fusion | flops 1074003968 | bytes 5767168 | tf_op jit(solution)/shard_map/dot_general | solution.py:92
  84.2 2.4 convolution_convert_fusion
  86.7 7.6 %collective-permute-start = (bf16[3,768]{0,1:T(8,128)(2,1)S(1)}, bf16[3,768]{0,1:T(8,128)(2,1)S(1)}, u32[]{:S(2)}, u32[]{:S(2)}) collective-permute-start(bf16[3,768]{0,1:T(8,128)(2,1)S(1)} %pad_maximum_fusion.5), channel_id=1, source_target_pairs={{0,8},{8,16},{16,24},{24,32},{32,40},{40,48},{48,56},{56,64},{64,7... | collective-permute-start | bytes 13832 | tf_op jit(solution)/shard_map/ppermute | solution.py:18
  95.1 1.6 collective-permute-done
  97.3 3.4 %fusion.42 = f32[512,1024]{1,0:T(8,128)} fusion(f32[512]{0:T(512)S(1)} %copy-done.21, f32[512]{0:T(512)S(1)} %bitcast.199, f32[512,1027]{1,0:T(8,128)S(1)} %maximum_convert_fusion, pred[1024]{0:T(1024)(128)(4,1)S(1)} %get-tuple-element.41, f32[512]{0:T(512)S(1)} %bitcast.200, pred[1024]{0:T(1024)(128)(4,1)S(1)} %get-tuple-element.42, f32[512]{0:T(512)S(1)} %bitcast.198, ...), kind=kLoop, calls=%fused_computation.73 | loop fusion | flops 8912896 | bytes 10499072 | tf_op jit(solution)/shard_map/reshape | solution.py:115
  100.8 3.2 %reshape.229 = f32[8,64,4,256]{3,2,1,0:T(4,128)} reshape(f32[512,1024]{1,0:T(8,128)} %fusion.42) | data formatting | bytes 4194304 | tf_op jit(solution)/shard_map/reshape | solution.py:115
  104.2 1.2 multiply_convert_fusion.2
  105.4 0.7 fusion.90
  106.1 0.9 reshape.226
  107.0 3.0 %fusion.19 = f32[4,8,64,128]{3,2,1,0:T(8,128)S(1)} fusion(f32[8,64,4,256]{3,2,1,0:T(4,128)} %reshape.229, f32[4,256,8]{1,2,0:T(8,128)S(1)} %exponential_select_fusion.1, f32[8,4,256]{2,0,1:T(8,128)S(1)} %bitcast.186, bf16[4,256,128,1]{1,0,2,3:T(4,128)(2,1)} %bitcast.179), kind=kOutput, calls=%fused_computation.30 | convolution fusion | flops 806354944 | bytes 3473408 | tf_op jit(solution)/shard_map/cshp,csn->chpn/dot_general | solution.py:136
  110.1 0.8 broadcast_multiply_fusion
  111.0 3.2 %convolution_bitcast_fusion = f32[512,256]{0,1:T(8,128)} fusion(bf16[2048,512]{1,0:T(8,128)(2,1)} %param.17, bf16[1024,2048]{1,0:T(8,128)(2,1)S(1)} %copy-done.4), kind=kOutput, calls=%fused_computation.37 | convolution fusion | flops 536870912 | bytes 3670016 | tf_op jit(solution)/shard_map/dot_general | solution.py:157
  114.2 1.5 convolution_bitcast_fusion.1
  115.7 4.4 %collective-permute-start.4 = (f32[8,65,128]{2,1,0:T(8,128)S(1)}, f32[8,65,128]{2,1,0:T(8,128)S(1)}, u32[]{:S(2)}, u32[]{:S(2)}) collective-permute-start(f32[8,65,128]{2,1,0:T(8,128)S(1)} %pad_maximum_fusion.3), channel_id=1, source_target_pairs={{0,32},{8,40},{16,48},{24,56},{32,64},{40,72},{48,80},{56,88},{64,... | collective-permute-start | bytes 798728 | tf_op jit(solution)/shard_map/ppermute | solution.py:18
  120.1 7.0 %collective-permute-start.3 = (f32[8,65,128]{2,1,0:T(8,128)S(1)}, f32[8,65,128]{2,1,0:T(8,128)S(1)}, u32[]{:S(2)}, u32[]{:S(2)}) collective-permute-start(f32[8,65,128]{2,1,0:T(8,128)S(1)} %pad_maximum_fusion.3), channel_id=1, source_target_pairs={{0,24},{8,32},{16,40},{24,48},{32,56},{40,64},{48,72},{56,80},{64,... | collective-permute-start | bytes 798728 | tf_op jit(solution)/shard_map/ppermute | solution.py:18
  127.1 1.3 collective-permute-start.2
  128.4 2.5 collective-permute-start.1
  131.3 10.9 %fusion = f32[4,8,64,256]{3,2,1,0:T(8,128)} fusion(f32[4,256,256]{2,1,0:T(8,128)S(1)} %fusion.50, f32[4,8,256]{2,1,0:T(8,128)S(1)} %add_bitcast_fusion.2, pred[4,256,256]{2,1,0:T(8,128)(4,1)S(1)} %copy-done.16, f32[8,64,4,256]{3,2,1,0:T(4,128)S(1)} %copy-done.1, f32[8,4,256]{2,0,1:T(8,128)S(1)} %bitcast.187), kind=kOutput, calls=%fused_computation.1 | convolution fusion | flops 1619525632 | bytes 5570560 | tf_op jit(solution)/shard_map/chts,cshp->cthp/dot_general | solution.py:131
  142.2 1.5 convolution_bitcast_fusion.2
  144.1 0.7 copy-done.8
  144.8 0.7 pad_maximum_fusion.4
  145.5 3.9 %collective-permute-start.6 = (f32[8,65,128]{2,1,0:T(8,128)}, f32[8,65,128]{2,1,0:T(8,128)}, u32[]{:S(2)}, u32[]{:S(2)}) collective-permute-start(f32[8,65,128]{2,1,0:T(8,128)} %pad_maximum_fusion.4), channel_id=1, source_target_pairs={{0,64},{8,72},{16,80},{24,88},{32,96},{40,104},{48,112},{56,120},{... | collective-permute-start | bytes 798728 | tf_op jit(solution)/shard_map/ppermute | solution.py:18
  149.4 4.4 %collective-permute-start.5 = (f32[8,65,128]{2,1,0:T(8,128)}, f32[8,65,128]{2,1,0:T(8,128)}, u32[]{:S(2)}, u32[]{:S(2)}) collective-permute-start(f32[8,65,128]{2,1,0:T(8,128)} %pad_maximum_fusion.4), channel_id=1, source_target_pairs={{0,32},{8,40},{16,48},{24,56},{32,64},{40,72},{48,80},{56,88},{64,... | collective-permute-start | bytes 798728 | tf_op jit(solution)/shard_map/ppermute | solution.py:18
  153.8 1.5 convolution_bitcast_fusion.3
  155.3 1.9 reshape.225
  157.2 2.0 copy.86
  159.2 2.0 copy.85
  161.3 2.0 copy.84
  163.3 2.0 copy.83
  165.6 2.6 %collective-permute-start.7 = (f32[8,65,128]{2,1,0:T(8,128)}, f32[8,65,128]{2,1,0:T(8,128)S(1)}, u32[]{:S(2)}, u32[]{:S(2)}) collective-permute-start(f32[8,65,128]{2,1,0:T(8,128)} %pad_maximum_fusion.4), channel_id=1, source_target_pairs={{0,96},{8,104},{16,112},{24,120},{32,128},{40,136},{48,144},{56,15... | collective-permute-start | bytes 798728 | tf_op jit(solution)/shard_map/ppermute | solution.py:18
  168.3 3.6 %collective-permute-done.7 = f32[8,65,128]{2,1,0:T(8,128)S(1)} collective-permute-done((f32[8,65,128]{2,1,0:T(8,128)}, f32[8,65,128]{2,1,0:T(8,128)S(1)}, u32[]{:S(2)}, u32[]{:S(2)}) %collective-permute-start.7) | collective-permute-done | bytes 266272 | tf_op jit(solution)/shard_map/ppermute | solution.py:18
  171.9 0.8 add_bitcast_fusion
  172.8 3.6 %fusion.20 = (bf16[4,8,8,8,256]{4,3,2,1,0:T(8,128)(2,1)S(1)}, bf16[4,256]{1,0:T(4,128)(2,1)S(1)}) fusion(f32[8,64]{1,0:T(8,128)S(1)} %copy-done.20, f32[1,8,64,256]{3,2,1,0:T(8,128)S(1)} %bitcast.180, f32[1,8,64,256]{3,2,1,0:T(8,128)S(1)} %bitcast.181, f32[1,8,64,256]{3,2,1,0:T(8,128)S(1)} %bitcast.182, f32[1,8,64,256]{3,2,1,0:T(8,128)S(1)} %bitcast.183, ...), kind=kOutput, calls=%fused_computation.43 | convolution fusion | flops 815004672 | bytes 8687792 | tf_op jit(solution)/shard_map/ctn,chpn->cthp/dot_general | solution.py:196
  176.6 2.4 bitcast_convert_fusion
  179.0 2.3 pad_maximum_fusion
  181.3 58.2 %reduce-scatter.2.cloned.1.call-done = bf16[1028,256]{1,0:T(8,128)(2,1)} async-done(((bf16[1028,2048]{1,0:T(8,128)(2,1)}), bf16[1028,256]{1,0:T(8,128)(2,1)}) %reduce-scatter.2.cloned.1.call-update) | async-done | bytes 526352 | tf_op jit(solution)/shard_map/reduce_scatter | solution.py:219
  239.6 1.1 convert_element_type.38
  240.7 1.0 fusion.21
  (111 shorter events, 8.4 us)
Async XLA Ops:
  7.2 169.4 %copy-start = (bf16[512,2048]{1,0:T(8,128)(2,1)S(1)}, bf16[512,2048]{1,0:T(8,128)(2,1)}, u32[]{:S(2)}) copy-start(bf16[512,2048]{1,0:T(8,128)(2,1)} %param.29) | copy-start | bytes 6291460
  7.2 65.1 %all-gather.2.cloned.1.call-start = ((), (), s32[]{:S(2)}) async-start(), calls=%async_computation.1 | async-start | bytes 4718592 | tf_op jit(solution)/shard_map/all_gather | solution.py:89
  7.9 231.6 %reduce-scatter.2.cloned.1.call-start = ((), (), s32[]{:S(2)}) async-start(), calls=%async_computation.2 | async-start | bytes 4755456 | tf_op jit(solution)/shard_map/reduce_scatter | solution.py:219
  79.7 4.0 %copy-start.3 = (bf16[1024,2048]{1,0:T(8,128)(2,1)S(1)}, bf16[1024,2048]{1,0:T(8,128)(2,1)}, u32[]{:S(2)}) copy-start(bf16[1024,2048]{1,0:T(8,128)(2,1)} %all-gather.2.cloned.1.call-done) | copy-start | bytes 12582916
  79.7 4.4 %copy-start.24 = (bf16[2048,512]{1,0:T(8,128)(2,1)S(1)}, bf16[2048,512]{1,0:T(8,128)(2,1)}, u32[]{:S(2)}) copy-start(bf16[2048,512]{1,0:T(8,128)(2,1)} %param.18) | copy-start | bytes 6291460
  86.7 10.7 %copy-start.21 = (f32[512]{0:T(512)S(1)}, f32[512]{0:T(512)}, u32[]{:S(2)}) copy-start(f32[512]{0:T(512)} %param.23) | copy-start | bytes 6148
  86.7 10.0 %collective-permute-start = (bf16[3,768]{0,1:T(8,128)(2,1)S(1)}, bf16[3,768]{0,1:T(8,128)(2,1)S(1)}, u32[]{:S(2)}, u32[]{:S(2)}) collective-permute-start(bf16[3,768]{0,1:T(8,128)(2,1)S(1)} %pad_maximum_fusion.5), channel_id=1, source_target_pairs={{0,8},{8,16},{16,24},{24,32},{32,40},{40,48},{48,56},{56,64},{64,7... | collective-permute-start | bytes 13832 | tf_op jit(solution)/shard_map/ppermute | solution.py:18
  100.8 3.5 %copy-start.23 = (f32[256]{0:T(256)S(1)}, f32[256]{0:T(256)}, u32[]{:S(2)}) copy-start(f32[256]{0:T(256)} %param.24) | copy-start | bytes 3076
  106.1 3.9 %copy-start.10 = (bf16[1024,128]{0,1:T(8,128)(2,1)}, bf16[1024,128]{0,1:T(8,128)(2,1)S(1)}, u32[]{:S(2)}) copy-start(bf16[1024,128]{0,1:T(8,128)(2,1)S(1)} %get-tuple-element.24) | copy-start | bytes 786436
  107.0 3.8 %copy-start.18 = (f32[8]{0:T(128)S(1)}, f32[8]{0:T(128)}, u32[]{:S(2)}) copy-start(f32[8]{0:T(128)} %get-tuple-element.13) | copy-start | bytes 100
  107.0 3.9 %copy-start.4 = (bf16[1024,2048]{1,0:T(8,128)(2,1)S(1)}, bf16[1024,2048]{1,0:T(8,128)(2,1)}, u32[]{:S(2)}) copy-start(bf16[1024,2048]{1,0:T(8,128)(2,1)} %all-gather.2.cloned.1.call-done) | copy-start | bytes 12582916
  110.8 33.2 %copy-start.5 = (f32[8,64,128]{2,1,0:T(8,128)}, f32[8,64,128]{2,1,0:T(8,128)S(1)}, u32[]{:S(2)}) copy-start(f32[8,64,128]{2,1,0:T(8,128)S(1)} %get-tuple-element.15) | copy-start | bytes 786436
  111.0 3.3 %copy-start.25 = (bf16[2048,512]{1,0:T(8,128)(2,1)S(1)}, bf16[2048,512]{1,0:T(8,128)(2,1)}, u32[]{:S(2)}) copy-start(bf16[2048,512]{1,0:T(8,128)(2,1)} %param.17) | copy-start | bytes 6291460
  114.2 16.7 %copy-start.7 = (bf16[1024,128]{0,1:T(8,128)(2,1)S(1)}, bf16[1024,128]{0,1:T(8,128)(2,1)}, u32[]{:S(2)}) copy-start(bf16[1024,128]{0,1:T(8,128)(2,1)} %get-tuple-element.23) | copy-start | bytes 786436
  114.2 16.7 %copy-start.11 = (bf16[1024,128]{0,1:T(8,128)(2,1)S(1)}, bf16[1024,128]{0,1:T(8,128)(2,1)}, u32[]{:S(2)}) copy-start(bf16[1024,128]{0,1:T(8,128)(2,1)} %copy-done.10) | copy-start | bytes 786436
  114.2 17.0 %copy-start.1 = (f32[8,64,4,256]{3,2,1,0:T(4,128)S(1)}, f32[8,64,4,256]{3,2,1,0:T(4,128)}, u32[]{:S(2)}) copy-start(f32[8,64,4,256]{3,2,1,0:T(4,128)} %reshape.229) | copy-start | bytes 6291460
  114.2 17.1 %copy-start.16 = (pred[4,256,256]{2,1,0:T(8,128)(4,1)S(1)}, pred[4,256,256]{2,1,0:T(8,128)(4,1)}, u32[]{:S(2)}) copy-start(pred[4,256,256]{2,1,0:T(8,128)(4,1)} %compare_and_fusion) | copy-start | bytes 786436
  115.7 28.0 %collective-permute-start.4 = (f32[8,65,128]{2,1,0:T(8,128)S(1)}, f32[8,65,128]{2,1,0:T(8,128)S(1)}, u32[]{:S(2)}, u32[]{:S(2)}) collective-permute-start(f32[8,65,128]{2,1,0:T(8,128)S(1)} %pad_maximum_fusion.3), channel_id=1, source_target_pairs={{0,32},{8,40},{16,48},{24,56},{32,64},{40,72},{48,80},{56,88},{64,... | collective-permute-start | bytes 798728 | tf_op jit(solution)/shard_map/ppermute | solution.py:18
  120.1 23.6 %collective-permute-start.3 = (f32[8,65,128]{2,1,0:T(8,128)S(1)}, f32[8,65,128]{2,1,0:T(8,128)S(1)}, u32[]{:S(2)}, u32[]{:S(2)}) collective-permute-start(f32[8,65,128]{2,1,0:T(8,128)S(1)} %pad_maximum_fusion.3), channel_id=1, source_target_pairs={{0,24},{8,32},{16,40},{24,48},{32,56},{40,64},{48,72},{56,80},{64,... | collective-permute-start | bytes 798728 | tf_op jit(solution)/shard_map/ppermute | solution.py:18
  127.1 16.6 %collective-permute-start.2 = (f32[8,65,128]{2,1,0:T(8,128)S(1)}, f32[8,65,128]{2,1,0:T(8,128)S(1)}, u32[]{:S(2)}, u32[]{:S(2)}) collective-permute-start(f32[8,65,128]{2,1,0:T(8,128)S(1)} %pad_maximum_fusion.3), channel_id=1, source_target_pairs={{0,16},{8,24},{16,32},{24,40},{32,48},{40,56},{48,64},{56,72},{64,... | collective-permute-start | bytes 798728 | tf_op jit(solution)/shard_map/ppermute | solution.py:18
  128.4 15.3 %collective-permute-start.1 = (f32[8,65,128]{2,1,0:T(8,128)S(1)}, f32[8,65,128]{2,1,0:T(8,128)S(1)}, u32[]{:S(2)}, u32[]{:S(2)}) collective-permute-start(f32[8,65,128]{2,1,0:T(8,128)S(1)} %pad_maximum_fusion.3), channel_id=1, source_target_pairs={{0,8},{8,16},{16,24},{24,32},{32,40},{40,48},{48,56},{56,64},{64,7... | collective-permute-start | bytes 798728 | tf_op jit(solution)/shard_map/ppermute | solution.py:18
  144.1 0.7 copy-start.8
  145.5 22.7 %collective-permute-start.6 = (f32[8,65,128]{2,1,0:T(8,128)}, f32[8,65,128]{2,1,0:T(8,128)}, u32[]{:S(2)}, u32[]{:S(2)}) collective-permute-start(f32[8,65,128]{2,1,0:T(8,128)} %pad_maximum_fusion.4), channel_id=1, source_target_pairs={{0,64},{8,72},{16,80},{24,88},{32,96},{40,104},{48,112},{56,120},{... | collective-permute-start | bytes 798728 | tf_op jit(solution)/shard_map/ppermute | solution.py:18
  149.4 18.8 %collective-permute-start.5 = (f32[8,65,128]{2,1,0:T(8,128)}, f32[8,65,128]{2,1,0:T(8,128)}, u32[]{:S(2)}, u32[]{:S(2)}) collective-permute-start(f32[8,65,128]{2,1,0:T(8,128)} %pad_maximum_fusion.4), channel_id=1, source_target_pairs={{0,32},{8,40},{16,48},{24,56},{32,64},{40,72},{48,80},{56,88},{64,... | collective-permute-start | bytes 798728 | tf_op jit(solution)/shard_map/ppermute | solution.py:18
  163.3 8.6 %copy-start.19 = (f32[8]{0:T(128)S(1)}, f32[8]{0:T(128)}, u32[]{:S(2)}) copy-start(f32[8]{0:T(128)} %get-tuple-element.13) | copy-start | bytes 100
  165.3 6.6 %copy-start.6 = (f32[8,64,128]{2,1,0:T(8,128)S(1)}, f32[8,64,128]{2,1,0:T(8,128)}, u32[]{:S(2)}) copy-start(f32[8,64,128]{2,1,0:T(8,128)} %copy-done.5) | copy-start | bytes 786436
  165.3 6.6 %copy-start.9 = (f32[8,64,128]{2,1,0:T(8,128)S(1)}, f32[8,64,128]{2,1,0:T(8,128)}, u32[]{:S(2)}) copy-start(f32[8,64,128]{2,1,0:T(8,128)} %copy-done.8) | copy-start | bytes 786436
  165.3 7.4 %copy-start.14 = (f32[512,256]{1,0:T(8,128)S(1)}, f32[512,256]{1,0:T(8,128)}, u32[]{:S(2)}) copy-start(f32[512,256]{1,0:T(8,128)} %copy.84) | copy-start | bytes 1572868
  165.3 7.4 %copy-start.15 = (f32[512,256]{1,0:T(8,128)S(1)}, f32[512,256]{1,0:T(8,128)}, u32[]{:S(2)}) copy-start(f32[512,256]{1,0:T(8,128)} %copy.83) | copy-start | bytes 1572868
  165.5 7.3 %copy-start.2 = (f32[8,64,4,256]{3,2,1,0:T(4,128)S(1)}, f32[8,64,4,256]{3,2,1,0:T(4,128)}, u32[]{:S(2)}) copy-start(f32[8,64,4,256]{3,2,1,0:T(4,128)} %reshape.229) | copy-start | bytes 6291460
  165.5 7.3 %copy-start.12 = (f32[512,256]{1,0:T(8,128)S(1)}, f32[512,256]{1,0:T(8,128)}, u32[]{:S(2)}) copy-start(f32[512,256]{1,0:T(8,128)} %copy.86) | copy-start | bytes 1572868
  165.5 7.3 %copy-start.13 = (f32[512,256]{1,0:T(8,128)S(1)}, f32[512,256]{1,0:T(8,128)}, u32[]{:S(2)}) copy-start(f32[512,256]{1,0:T(8,128)} %copy.85) | copy-start | bytes 1572868
  165.5 7.3 %copy-start.17 = (bf16[4,256,128]{1,0,2:T(4,128)(2,1)S(1)}, bf16[4,256,128]{1,0,2:T(4,128)(2,1)}, u32[]{:S(2)}) copy-start(bf16[4,256,128]{1,0,2:T(4,128)(2,1)} %reshape.225) | copy-start | bytes 786436
  165.5 7.3 %copy-start.20 = (f32[8,64]{1,0:T(8,128)S(1)}, f32[8,64]{1,0:T(8,128)}, u32[]{:S(2)}) copy-start(f32[8,64]{1,0:T(8,128)} %mul.488) | copy-start | bytes 6148
  165.5 7.3 %copy-start.22 = (f32[4,8]{1,0:T(4,128)S(1)}, f32[4,8]{1,0:T(4,128)}, u32[]{:S(2)}) copy-start(f32[4,8]{1,0:T(4,128)} %pad_maximum_fusion.6) | copy-start | bytes 388
  165.5 7.3 %copy-start.26 = (f32[8]{0:T(128)S(1)}, f32[8]{0:T(128)}, u32[]{:S(2)}) copy-start(f32[8]{0:T(128)} %param.27) | copy-start | bytes 100
  165.6 7.3 %copy-start.27 = (f32[4]{0:T(128)S(1)}, f32[4]{0:T(128)}, u32[]{:S(2)}) copy-start(f32[4]{0:T(128)} %pad.8.clone) | copy-start | bytes 52
  165.6 6.4 %collective-permute-start.7 = (f32[8,65,128]{2,1,0:T(8,128)}, f32[8,65,128]{2,1,0:T(8,128)S(1)}, u32[]{:S(2)}, u32[]{:S(2)}) collective-permute-start(f32[8,65,128]{2,1,0:T(8,128)} %pad_maximum_fusion.4), channel_id=1, source_target_pairs={{0,96},{8,104},{16,112},{24,120},{32,128},{40,136},{48,144},{56,15... | collective-permute-start | bytes 798728 | tf_op jit(solution)/shard_map/ppermute | solution.py:18
Sparse Core Ops, SparseCore 0:
  9.7 62.5 all-gather.1
  181.4 58.0 reduce-scatter.1

commit v10 on v9

--- a/solution.py
+++ b/solution.py
@@ -152,16 +152,11 @@
     packed = jnp.concatenate([running_state, gain_row], 1)
     identity = jnp.concatenate([0.0 * running_state, 1.0 + 0.0 * gain_row], 1)
     late_piece, packed = lax.optimization_barrier((piece, packed))
-    gate_turned = jnp.stack(
-        [
-            jnp.dot(
-                w_gate.T,
-                late_piece[group_no * GROUP : (group_no + 1) * GROUP].T,
-                preferred_element_type=jnp.float32,
-            )
-            for group_no in range(rows_here // GROUP)
-        ],
-        0,
+    gate_turned = jnp.einsum(
+        "ctd,dk->ckt",
+        late_piece.reshape(rows_here // GROUP, GROUP, late_piece.shape[1]),
+        w_gate,
+        preferred_element_type=jnp.float32,
     )
 
     def joined_of(earlier_part, later_part):

time: 249 us -> 248 us (level)
  waiting for transfers between devices: 120 us -> 127 us
  local copies, waits for them, and re-layouts: 22.1 us -> 16.3 us
    dot_general x4 -> x0, local copies, waits for them, and re-layouts: 8.14 us -> none  [shards(): jnp.dot(w_gate.T, late_piece[group_no * GROUP:(group_no + 1) * GROUP].T,...]
    ppermute x8, waiting for transfers between devices: 5.26 us -> 11.9 us  [shifted(): return lax.ppermute(x, axis, pairs)]
    mul x0 -> x1, local copies, waits for them, and re-layouts: none -> 2.98 us  [shards(): jax.nn.silu(gate_turned).reshape(count, heads_here, head_width, GROUP)]
    dot_general x4 -> x1, matrix products: 7.75 us -> 5.59 us  [shards(): jnp.einsum('ctd,dk->ckt', late_piece.reshape(rows_here // GROUP, GROUP, l...]
  transfers between devices with their start and end apart: 10 -> 10, of which waited for: 4 -> 6; matrix products, arithmetic and copies ran while one was open for 14% -> 12% of each run, Pallas kernels for 0% -> 0%
where the time goes in v10:
time: 248 us
  waiting for transfers between devices  127 us (51%)
  matrix products  35.4 us (14%)
  starting transfers between devices  34.5 us (14%)
  other arithmetic  20.1 us (8%)
  local copies, waits for them, and re-layouts  16.3 us (7%)
  between operations  14.5 us (6%)
    reduce_scatter x1, waiting for transfers between devices, shards(): lax.psum_scatter(joined.astype(jnp.bfloat16), 'head', scatter_dimension=1...  58.2 us
    all_gather x1, waiting for transfers between devices, shards(): piece = lax.all_gather(tokens, 'head', axis=1, tiled=True)  56.2 us
    ppermute x8, starting transfers between devices, shifted(): return lax.ppermute(x, axis, pairs)  34.4 us
    ppermute x8, waiting for transfers between devices, shifted(): return lax.ppermute(x, axis, pairs)  11.9 us
    dot_general x1, matrix products, shards(): jnp.einsum('chts,cshp->cthp', decays * scores[:, None, :, :], group_x, pr...  10.9 us
    dot_general x2, matrix products, partial_product(): return jnp.dot(piece, matrix, preferred_element_type=jnp.float32)  7.35 us
    dot_general x1, matrix products, shards(): jnp.einsum('ctd,dk->ckt', late_piece.reshape(rows_here // GROUP, GROUP, l...  5.59 us
  transfers between devices with their start and end apart: 10, of which 6 were waited for; matrix products, arithmetic and copies ran while one was open for 12% of the time, Pallas kernels for 0%

profile of v10, /device:TPU:1, one launch (start us, length us, event | category | flops | bytes accessed | tf_op | source)
XLA Modules:
  0.0 247.8 jit_solution(17797647431642952932)
XLA Ops:
  7.2 0.7 all-gather.2.cloned.1.call-update
  8.0 0.8 mul.487
  8.7 0.7 dynamic_slice.7
  9.4 0.8 broadcast_select_fusion.6
  11.5 0.7 pad_add_fusion.1
  12.4 0.8 fusion.86
  13.4 0.8 fusion.96
  14.2 0.9 fusion.95
  15.1 0.9 compare_and_fusion
  16.1 56.2 %all-gather.2.cloned.1.call-done = bf16[1024,2048]{1,0:T(8,128)(2,1)} async-done(((bf16[1024,256]{1,0:T(8,128)(2,1)}), bf16[1024,2048]{1,0:T(8,128)(2,1)}) %all-gather.2.cloned.1.call-update) | async-done | bytes 4194320 | tf_op jit(solution)/shard_map/all_gather | solution.py:89
  72.3 3.4 %fusion.71 = (f32[1024,8]{0,1:T(8,128)S(1)}, f32[1024,8]{0,1:T(8,128)S(1)}) fusion(f32[8]{0:T(128)} %param.26, f32[8]{0:T(128)} %param.25, bf16[1024,2048]{1,0:T(8,128)(2,1)} %all-gather.2.cloned.1.call-done, bf16[2048,8]{0,1:T(8,128)(2,1)} %param.20), kind=kOutput, calls=%fused_computation.129 | convolution fusion | flops 33628160 | bytes 4292672 | tf_op jit(solution)/shard_map/dot_general | solution.py:92
  75.7 2.3 reduce-window.6
  78.5 0.6 multiply_add_fusion.2
  79.7 3.9 %convolution_convert_fusion.1 = bf16[1024,256]{0,1:T(8,128)(2,1)S(1)} fusion(bf16[1024,2048]{1,0:T(8,128)(2,1)} %all-gather.2.cloned.1.call-done, bf16[2048,256]{1,0:T(8,128)(2,1)} %param.19), kind=kOutput, calls=%fused_computation.42 | convolution fusion | flops 1074003968 | bytes 5767168 | tf_op jit(solution)/shard_map/dot_general | solution.py:92
  84.2 2.4 convolution_convert_fusion
  86.7 7.4 %collective-permute-start = (bf16[3,768]{0,1:T(8,128)(2,1)S(1)}, bf16[3,768]{0,1:T(8,128)(2,1)S(1)}, u32[]{:S(2)}, u32[]{:S(2)}) collective-permute-start(bf16[3,768]{0,1:T(8,128)(2,1)S(1)} %pad_maximum_fusion.4), channel_id=1, source_target_pairs={{0,8},{8,16},{16,24},{24,32},{32,40},{40,48},{48,56},{56,64},{64,7... | collective-permute-start | bytes 13832 | tf_op jit(solution)/shard_map/ppermute | solution.py:18
  94.3 2.4 collective-permute-done
  96.7 0.6 maximum_convert_fusion
  97.3 3.4 %fusion.46 = f32[512,1024]{1,0:T(8,128)} fusion(f32[512]{0:T(512)S(1)} %copy-done.19, f32[512]{0:T(512)S(1)} %bitcast.198, f32[512,1027]{1,0:T(8,128)S(1)} %maximum_convert_fusion, pred[1024]{0:T(1024)(128)(4,1)S(1)} %get-tuple-element.41, f32[512]{0:T(512)S(1)} %bitcast.199, pred[1024]{0:T(1024)(128)(4,1)S(1)} %get-tuple-element.42, f32[512]{0:T(512)S(1)} %bitcast.197, ...), kind=kLoop, calls=%fused_computation.71 | loop fusion | flops 8912896 | bytes 10499072 | tf_op jit(solution)/shard_map/reshape | solution.py:115
  100.8 3.2 %reshape.228 = f32[8,64,4,256]{3,2,1,0:T(4,128)} reshape(f32[512,1024]{1,0:T(8,128)} %fusion.46) | data formatting | bytes 4194304 | tf_op jit(solution)/shard_map/reshape | solution.py:115
  104.2 1.2 multiply_convert_fusion.2
  105.4 0.7 fusion.94
  106.1 0.9 reshape.223
  107.0 3.0 %fusion.25 = f32[4,8,64,128]{3,2,1,0:T(8,128)S(1)} fusion(f32[8,64,4,256]{3,2,1,0:T(4,128)} %reshape.228, f32[4,256,8]{1,2,0:T(8,128)S(1)} %exponential_select_fusion.1, f32[8,4,256]{2,0,1:T(8,128)S(1)} %bitcast.185, bf16[4,256,128,1]{1,0,2,3:T(4,128)(2,1)} %bitcast.182), kind=kOutput, calls=%fused_computation.36 | convolution fusion | flops 806354944 | bytes 3473408 | tf_op jit(solution)/shard_map/cshp,csn->chpn/dot_general | solution.py:136
  110.1 0.8 broadcast_multiply_fusion
  111.0 4.4 %collective-permute-start.4 = (f32[8,65,128]{2,1,0:T(8,128)S(1)}, f32[8,65,128]{2,1,0:T(8,128)S(1)}, u32[]{:S(2)}, u32[]{:S(2)}) collective-permute-start(f32[8,65,128]{2,1,0:T(8,128)S(1)} %pad_maximum_fusion.2), channel_id=1, source_target_pairs={{0,32},{8,40},{16,48},{24,56},{32,64},{40,72},{48,80},{56,88},{64,... | collective-permute-start | bytes 798728 | tf_op jit(solution)/shard_map/ppermute | solution.py:18
  115.3 7.0 %collective-permute-start.3 = (f32[8,65,128]{2,1,0:T(8,128)S(1)}, f32[8,65,128]{2,1,0:T(8,128)S(1)}, u32[]{:S(2)}, u32[]{:S(2)}) collective-permute-start(f32[8,65,128]{2,1,0:T(8,128)S(1)} %pad_maximum_fusion.2), channel_id=1, source_target_pairs={{0,24},{8,32},{16,40},{24,48},{32,56},{40,64},{48,72},{56,80},{64,... | collective-permute-start | bytes 798728 | tf_op jit(solution)/shard_map/ppermute | solution.py:18
  122.3 1.3 collective-permute-start.2
  123.7 2.6 %collective-permute-start.1 = (f32[8,65,128]{2,1,0:T(8,128)S(1)}, f32[8,65,128]{2,1,0:T(8,128)S(1)}, u32[]{:S(2)}, u32[]{:S(2)}) collective-permute-start(f32[8,65,128]{2,1,0:T(8,128)S(1)} %pad_maximum_fusion.2), channel_id=1, source_target_pairs={{0,8},{8,16},{16,24},{24,32},{32,40},{40,48},{48,56},{56,64},{64,7... | collective-permute-start | bytes 798728 | tf_op jit(solution)/shard_map/ppermute | solution.py:18
  126.4 5.6 %bitcast_multiply_fusion = f32[4,512,256]{1,2,0:T(8,128)} fusion(bf16[4,256,2048]{2,1,0:T(8,128)(2,1)S(1)} %bitcast.178, bf16[2048,512]{1,0:T(8,128)(2,1)} %param.17), kind=kOutput, calls=%fused_computation.24 | convolution fusion | flops 2149580800 | bytes 8388608 | tf_op jit(solution)/shard_map/ctd,dk->ckt/dot_general | solution.py:155
  132.3 2.5 %collective-permute-done.2 = f32[8,65,128]{2,1,0:T(8,128)S(1)} collective-permute-done((f32[8,65,128]{2,1,0:T(8,128)S(1)}, f32[8,65,128]{2,1,0:T(8,128)S(1)}, u32[]{:S(2)}, u32[]{:S(2)}) %collective-permute-start.2) | collective-permute-done | bytes 266272 | tf_op jit(solution)/shard_map/ppermute | solution.py:18
  134.8 3.2 %collective-permute-done.1 = f32[8,65,128]{2,1,0:T(8,128)S(1)} collective-permute-done((f32[8,65,128]{2,1,0:T(8,128)S(1)}, f32[8,65,128]{2,1,0:T(8,128)S(1)}, u32[]{:S(2)}, u32[]{:S(2)}) %collective-permute-start.1) | collective-permute-done | bytes 266272 | tf_op jit(solution)/shard_map/ppermute | solution.py:18
  138.4 0.7 copy-done.9
  139.1 0.7 pad_maximum_fusion.3
  139.8 3.8 %collective-permute-start.6 = (f32[8,65,128]{2,1,0:T(8,128)}, f32[8,65,128]{2,1,0:T(8,128)}, u32[]{:S(2)}, u32[]{:S(2)}) collective-permute-start(f32[8,65,128]{2,1,0:T(8,128)} %pad_maximum_fusion.3), channel_id=1, source_target_pairs={{0,64},{8,72},{16,80},{24,88},{32,96},{40,104},{48,112},{56,120},{... | collective-permute-start | bytes 798728 | tf_op jit(solution)/shard_map/ppermute | solution.py:18
  143.6 4.9 %collective-permute-start.5 = (f32[8,65,128]{2,1,0:T(8,128)}, f32[8,65,128]{2,1,0:T(8,128)}, u32[]{:S(2)}, u32[]{:S(2)}) collective-permute-start(f32[8,65,128]{2,1,0:T(8,128)} %pad_maximum_fusion.3), channel_id=1, source_target_pairs={{0,32},{8,40},{16,48},{24,56},{32,64},{40,72},{48,80},{56,88},{64,... | collective-permute-start | bytes 798728 | tf_op jit(solution)/shard_map/ppermute | solution.py:18
  148.6 10.9 %fusion = f32[4,8,64,256]{3,2,1,0:T(8,128)} fusion(f32[4,256,256]{2,1,0:T(8,128)S(1)} %fusion.54, f32[4,8,256]{2,1,0:T(8,128)S(1)} %add_bitcast_fusion.2, pred[4,256,256]{2,1,0:T(8,128)(4,1)S(1)} %copy-done.14, f32[8,64,4,256]{3,2,1,0:T(4,128)S(1)} %copy-done.1, f32[8,4,256]{2,0,1:T(8,128)S(1)} %bitcast.186), kind=kOutput, calls=%fused_computation.1 | convolution fusion | flops 1619525632 | bytes 5570560 | tf_op jit(solution)/shard_map/chts,cshp->cthp/dot_general | solution.py:131
  159.5 1.8 reshape.222
  161.3 3.0 %copy.71 = f32[4,512,256]{2,1,0:T(8,128)} copy(f32[4,512,256]{1,2,0:T(8,128)} %bitcast_multiply_fusion) | data formatting | bytes 4194304 | tf_op jit(solution)/shard_map/jit(silu)/mul | solution.py:198
  164.5 3.0 %collective-permute-start.7 = (f32[8,65,128]{2,1,0:T(8,128)}, f32[8,65,128]{2,1,0:T(8,128)S(1)}, u32[]{:S(2)}, u32[]{:S(2)}) collective-permute-start(f32[8,65,128]{2,1,0:T(8,128)} %pad_maximum_fusion.3), channel_id=1, source_target_pairs={{0,96},{8,104},{16,112},{24,120},{32,128},{40,136},{48,144},{56,15... | collective-permute-start | bytes 798728 | tf_op jit(solution)/shard_map/ppermute | solution.py:18
  167.6 3.8 %collective-permute-done.7 = f32[8,65,128]{2,1,0:T(8,128)S(1)} collective-permute-done((f32[8,65,128]{2,1,0:T(8,128)}, f32[8,65,128]{2,1,0:T(8,128)S(1)}, u32[]{:S(2)}, u32[]{:S(2)}) %collective-permute-start.7) | collective-permute-done | bytes 266272 | tf_op jit(solution)/shard_map/ppermute | solution.py:18
  171.4 0.8 add_bitcast_fusion
  172.3 3.4 %fusion.28 = (bf16[4,8,8,8,256]{4,3,2,1,0:T(8,128)(2,1)S(1)}, bf16[4,256]{1,0:T(4,128)(2,1)S(1)}) fusion(f32[8,64]{1,0:T(8,128)S(1)} %mul.487, f32[4,256,8,64]{1,3,2,0:T(8,128)S(1)} %bitcast.177, f32[8,64,4,256]{3,2,1,0:T(4,128)S(1)} %copy-done.2, f32[8]{0:T(128)S(1)} %copy-done.21, f32[4,256,8]{1,2,0:T(8,128)S(1)} %get-tuple-element.16, ...), kind=kOutput, calls=%fused_computation.45 | convolution fusion | flops 811334656 | bytes 8687792 | tf_op jit(solution)/shard_map/ctn,chpn->cthp/dot_general | solution.py:191
  175.8 2.4 bitcast_convert_fusion
  178.2 2.3 pad_maximum_fusion
  180.6 58.2 %reduce-scatter.2.cloned.1.call-done = bf16[1028,256]{1,0:T(8,128)(2,1)} async-done(((bf16[1028,2048]{1,0:T(8,128)(2,1)}), bf16[1028,256]{1,0:T(8,128)(2,1)}) %reduce-scatter.2.cloned.1.call-update) | async-done | bytes 526352 | tf_op jit(solution)/shard_map/reduce_scatter | solution.py:214
  238.8 1.1 convert_element_type.38
  239.9 1.0 fusion.29
  (97 shorter events, 5.3 us)
Async XLA Ops:
  7.2 168.7 %copy-start = (bf16[512,2048]{1,0:T(8,128)(2,1)S(1)}, bf16[512,2048]{1,0:T(8,128)(2,1)}, u32[]{:S(2)}) copy-start(bf16[512,2048]{1,0:T(8,128)(2,1)} %param.29) | copy-start | bytes 6291460
  7.2 65.1 %all-gather.2.cloned.1.call-start = ((), (), s32[]{:S(2)}) async-start(), calls=%async_computation.1 | async-start | bytes 4718592 | tf_op jit(solution)/shard_map/all_gather | solution.py:89
  7.9 230.9 %reduce-scatter.2.cloned.1.call-start = ((), (), s32[]{:S(2)}) async-start(), calls=%async_computation.2 | async-start | bytes 4755456 | tf_op jit(solution)/shard_map/reduce_scatter | solution.py:214
  79.7 4.0 %copy-start.4 = (bf16[1024,2048]{1,0:T(8,128)(2,1)S(1)}, bf16[1024,2048]{1,0:T(8,128)(2,1)}, u32[]{:S(2)}) copy-start(bf16[1024,2048]{1,0:T(8,128)(2,1)} %all-gather.2.cloned.1.call-done) | copy-start | bytes 12582916
  79.7 4.4 %copy-start.23 = (bf16[2048,512]{1,0:T(8,128)(2,1)S(1)}, bf16[2048,512]{1,0:T(8,128)(2,1)}, u32[]{:S(2)}) copy-start(bf16[2048,512]{1,0:T(8,128)(2,1)} %param.18) | copy-start | bytes 6291460
  86.7 10.7 %copy-start.19 = (f32[512]{0:T(512)S(1)}, f32[512]{0:T(512)}, u32[]{:S(2)}) copy-start(f32[512]{0:T(512)} %param.23) | copy-start | bytes 6148
  86.7 10.0 %collective-permute-start = (bf16[3,768]{0,1:T(8,128)(2,1)S(1)}, bf16[3,768]{0,1:T(8,128)(2,1)S(1)}, u32[]{:S(2)}, u32[]{:S(2)}) collective-permute-start(bf16[3,768]{0,1:T(8,128)(2,1)S(1)} %pad_maximum_fusion.4), channel_id=1, source_target_pairs={{0,8},{8,16},{16,24},{24,32},{32,40},{40,48},{48,56},{56,64},{64,7... | collective-permute-start | bytes 13832 | tf_op jit(solution)/shard_map/ppermute | solution.py:18
  100.8 3.4 %copy-start.20 = (f32[256]{0:T(256)S(1)}, f32[256]{0:T(256)}, u32[]{:S(2)}) copy-start(f32[256]{0:T(256)} %param.24) | copy-start | bytes 3076
  106.1 3.9 %copy-start.11 = (bf16[1024,128]{0,1:T(8,128)(2,1)}, bf16[1024,128]{0,1:T(8,128)(2,1)S(1)}, u32[]{:S(2)}) copy-start(bf16[1024,128]{0,1:T(8,128)(2,1)S(1)} %get-tuple-element.24) | copy-start | bytes 786436
  107.0 3.8 %copy-start.17 = (f32[8]{0:T(128)S(1)}, f32[8]{0:T(128)}, u32[]{:S(2)}) copy-start(f32[8]{0:T(128)} %get-tuple-element.13) | copy-start | bytes 100
  107.0 19.3 %copy-start.5 = (bf16[1024,2048]{1,0:T(8,128)(2,1)S(1)}, bf16[1024,2048]{1,0:T(8,128)(2,1)}, u32[]{:S(2)}) copy-start(bf16[1024,2048]{1,0:T(8,128)(2,1)} %all-gather.2.cloned.1.call-done) | copy-start | bytes 12582916
  110.8 27.4 %copy-start.6 = (f32[8,64,128]{2,1,0:T(8,128)}, f32[8,64,128]{2,1,0:T(8,128)S(1)}, u32[]{:S(2)}) copy-start(f32[8,64,128]{2,1,0:T(8,128)S(1)} %get-tuple-element.15) | copy-start | bytes 786436
  111.0 21.3 %collective-permute-start.4 = (f32[8,65,128]{2,1,0:T(8,128)S(1)}, f32[8,65,128]{2,1,0:T(8,128)S(1)}, u32[]{:S(2)}, u32[]{:S(2)}) collective-permute-start(f32[8,65,128]{2,1,0:T(8,128)S(1)} %pad_maximum_fusion.2), channel_id=1, source_target_pairs={{0,32},{8,40},{16,48},{24,56},{32,64},{40,72},{48,80},{56,88},{64,... | collective-permute-start | bytes 798728 | tf_op jit(solution)/shard_map/ppermute | solution.py:18
  115.3 17.0 %collective-permute-start.3 = (f32[8,65,128]{2,1,0:T(8,128)S(1)}, f32[8,65,128]{2,1,0:T(8,128)S(1)}, u32[]{:S(2)}, u32[]{:S(2)}) collective-permute-start(f32[8,65,128]{2,1,0:T(8,128)S(1)} %pad_maximum_fusion.2), channel_id=1, source_target_pairs={{0,24},{8,32},{16,40},{24,48},{32,56},{40,64},{48,72},{56,80},{64,... | collective-permute-start | bytes 798728 | tf_op jit(solution)/shard_map/ppermute | solution.py:18
  122.3 12.5 %collective-permute-start.2 = (f32[8,65,128]{2,1,0:T(8,128)S(1)}, f32[8,65,128]{2,1,0:T(8,128)S(1)}, u32[]{:S(2)}, u32[]{:S(2)}) collective-permute-start(f32[8,65,128]{2,1,0:T(8,128)S(1)} %pad_maximum_fusion.2), channel_id=1, source_target_pairs={{0,16},{8,24},{16,32},{24,40},{32,48},{40,56},{48,64},{56,72},{64,... | collective-permute-start | bytes 798728 | tf_op jit(solution)/shard_map/ppermute | solution.py:18
  123.7 14.3 %collective-permute-start.1 = (f32[8,65,128]{2,1,0:T(8,128)S(1)}, f32[8,65,128]{2,1,0:T(8,128)S(1)}, u32[]{:S(2)}, u32[]{:S(2)}) collective-permute-start(f32[8,65,128]{2,1,0:T(8,128)S(1)} %pad_maximum_fusion.2), channel_id=1, source_target_pairs={{0,8},{8,16},{16,24},{24,32},{32,40},{40,48},{48,56},{56,64},{64,7... | collective-permute-start | bytes 798728 | tf_op jit(solution)/shard_map/ppermute | solution.py:18
  126.3 5.6 %copy-start.8 = (bf16[1024,128]{0,1:T(8,128)(2,1)S(1)}, bf16[1024,128]{0,1:T(8,128)(2,1)}, u32[]{:S(2)}) copy-start(bf16[1024,128]{0,1:T(8,128)(2,1)} %get-tuple-element.23) | copy-start | bytes 786436
  126.3 5.6 %copy-start.12 = (bf16[1024,128]{0,1:T(8,128)(2,1)S(1)}, bf16[1024,128]{0,1:T(8,128)(2,1)}, u32[]{:S(2)}) copy-start(bf16[1024,128]{0,1:T(8,128)(2,1)} %copy-done.11) | copy-start | bytes 786436
  126.3 11.6 %copy-start.16 = (f32[8]{0:T(128)S(1)}, f32[8]{0:T(128)}, u32[]{:S(2)}) copy-start(f32[8]{0:T(128)} %get-tuple-element.12) | copy-start | bytes 100
  138.0 10.5 %copy-start.1 = (f32[8,64,4,256]{3,2,1,0:T(4,128)S(1)}, f32[8,64,4,256]{3,2,1,0:T(4,128)}, u32[]{:S(2)}) copy-start(f32[8,64,4,256]{3,2,1,0:T(4,128)} %reshape.228) | copy-start | bytes 6291460
  138.0 10.5 %copy-start.14 = (pred[4,256,256]{2,1,0:T(8,128)(4,1)S(1)}, pred[4,256,256]{2,1,0:T(8,128)(4,1)}, u32[]{:S(2)}) copy-start(pred[4,256,256]{2,1,0:T(8,128)(4,1)} %compare_and_fusion) | copy-start | bytes 786436
  138.4 0.7 copy-start.9
  139.8 27.7 %collective-permute-start.6 = (f32[8,65,128]{2,1,0:T(8,128)}, f32[8,65,128]{2,1,0:T(8,128)}, u32[]{:S(2)}, u32[]{:S(2)}) collective-permute-start(f32[8,65,128]{2,1,0:T(8,128)} %pad_maximum_fusion.3), channel_id=1, source_target_pairs={{0,64},{8,72},{16,80},{24,88},{32,96},{40,104},{48,112},{56,120},{... | collective-permute-start | bytes 798728 | tf_op jit(solution)/shard_map/ppermute | solution.py:18
  143.6 23.9 %collective-permute-start.5 = (f32[8,65,128]{2,1,0:T(8,128)}, f32[8,65,128]{2,1,0:T(8,128)}, u32[]{:S(2)}, u32[]{:S(2)}) collective-permute-start(f32[8,65,128]{2,1,0:T(8,128)} %pad_maximum_fusion.3), channel_id=1, source_target_pairs={{0,32},{8,40},{16,48},{24,56},{32,64},{40,72},{48,80},{56,88},{64,... | collective-permute-start | bytes 798728 | tf_op jit(solution)/shard_map/ppermute | solution.py:18
  161.3 3.0 %copy-start.15 = (f32[8]{0:T(128)S(1)}, f32[8]{0:T(128)}, u32[]{:S(2)}) copy-start(f32[8]{0:T(128)} %get-tuple-element.53) | copy-start | bytes 100
  164.3 7.1 %copy-start.7 = (f32[8,64,128]{2,1,0:T(8,128)S(1)}, f32[8,64,128]{2,1,0:T(8,128)}, u32[]{:S(2)}) copy-start(f32[8,64,128]{2,1,0:T(8,128)} %copy-done.6) | copy-start | bytes 786436
  164.3 7.1 %copy-start.10 = (f32[8,64,128]{2,1,0:T(8,128)S(1)}, f32[8,64,128]{2,1,0:T(8,128)}, u32[]{:S(2)}) copy-start(f32[8,64,128]{2,1,0:T(8,128)} %copy-done.9) | copy-start | bytes 786436
  164.3 7.1 %copy-start.18 = (f32[8]{0:T(128)S(1)}, f32[8]{0:T(128)}, u32[]{:S(2)}) copy-start(f32[8]{0:T(128)} %get-tuple-element.13) | copy-start | bytes 100
  164.3 8.0 %copy-start.3 = (f32[4,512,256]{2,1,0:T(8,128)S(1)}, f32[4,512,256]{2,1,0:T(8,128)}, u32[]{:S(2)}) copy-start(f32[4,512,256]{2,1,0:T(8,128)} %copy.71) | copy-start | bytes 6291460
  164.5 7.8 %copy-start.2 = (f32[8,64,4,256]{3,2,1,0:T(4,128)S(1)}, f32[8,64,4,256]{3,2,1,0:T(4,128)}, u32[]{:S(2)}) copy-start(f32[8,64,4,256]{3,2,1,0:T(4,128)} %reshape.228) | copy-start | bytes 6291460
  164.5 7.8 %copy-start.13 = (bf16[4,256,128]{1,0,2:T(4,128)(2,1)S(1)}, bf16[4,256,128]{1,0,2:T(4,128)(2,1)}, u32[]{:S(2)}) copy-start(bf16[4,256,128]{1,0,2:T(4,128)(2,1)} %reshape.222) | copy-start | bytes 786436
  164.5 7.8 %copy-start.21 = (f32[8]{0:T(128)S(1)}, f32[8]{0:T(128)}, u32[]{:S(2)}) copy-start(f32[8]{0:T(128)} %param.27) | copy-start | bytes 100
  164.5 7.8 %copy-start.22 = (f32[4]{0:T(128)S(1)}, f32[4]{0:T(128)}, u32[]{:S(2)}) copy-start(f32[4]{0:T(128)} %pad.4.clone) | copy-start | bytes 52
  164.5 6.9 %collective-permute-start.7 = (f32[8,65,128]{2,1,0:T(8,128)}, f32[8,65,128]{2,1,0:T(8,128)S(1)}, u32[]{:S(2)}, u32[]{:S(2)}) collective-permute-start(f32[8,65,128]{2,1,0:T(8,128)} %pad_maximum_fusion.3), channel_id=1, source_target_pairs={{0,96},{8,104},{16,112},{24,120},{32,128},{40,136},{48,144},{56,15... | collective-permute-start | bytes 798728 | tf_op jit(solution)/shard_map/ppermute | solution.py:18
Sparse Core Ops, SparseCore 0:
  9.7 62.5 all-gather.1
  180.7 58.0 reduce-scatter.1

commit v11 on v8

--- a/solution.py
+++ b/solution.py
@@ -204,9 +204,11 @@
     joined = jnp.concatenate([partial_out, jnp.tile(square_rows, (1, heads_n))], 0)
     summed = lax.psum_scatter(
         joined.astype(jnp.bfloat16), "head", scatter_dimension=1, tiled=True
-    ).astype(jnp.float32)
-    mean_square = (summed[rows_here:].reshape(rows_here) / INNER)[:, None]
-    mixed = (summed[:rows_here] * lax.rsqrt(mean_square + EPSILON)).astype(jnp.bfloat16)
+    )
+    mean_square = (summed[rows_here:].astype(jnp.float32).reshape(rows_here) / INNER)[:, None]
+    mixed = (summed[:rows_here].astype(jnp.float32) * lax.rsqrt(mean_square + EPSILON)).astype(
+        jnp.bfloat16
+    )
     return (mixed, end_state)
 
 

time: 245 us -> 245 us (level)
  no operation moved by 1% of the time
where the time goes in v11:
time: 245 us; the launch traced here: 244 us
  waiting for transfers between devices  120 us (49%)
  matrix products  33.7 us (14%)
  starting transfers between devices  33.4 us (14%)
  local copies, waits for them, and re-layouts  21.8 us (9%)
  other arithmetic  20.9 us (9%)
  between operations  14.6 us (6%)
    reduce_scatter x1, waiting for transfers between devices, shards(): lax.psum_scatter(joined.astype(jnp.bfloat16), 'head', scatter_dimension=1...  58.2 us
    all_gather x1, waiting for transfers between devices, shards(): piece = lax.all_gather(tokens, 'head', axis=1, tiled=True)  56.7 us
    ppermute x8, starting transfers between devices, shifted(): return lax.ppermute(x, axis, pairs)  33.3 us
    dot_general x1, matrix products, shards(): jnp.einsum('chts,cshp->cthp', decays * scores[:, None, :, :], group_x, pr...  10.9 us
    dot_general x3, matrix products, partial_product(): return jnp.dot(piece, matrix, preferred_element_type=jnp.float32)  9.33 us
    dot_general x4, local copies, waits for them, and re-layouts, shards(): jnp.dot(w_gate.T, late_piece[group_no * GROUP:(group_no + 1) * GROUP].T,...  8.17 us
    reshape x2, local copies, waits for them, and re-layouts, shards(): x_conv.astype(jnp.float32).reshape(rows_here, heads_here, head_width)  6.15 us
    dot_general x4, matrix products, shards(): jnp.dot(w_gate.T, late_piece[group_no * GROUP:(group_no + 1) * GROUP].T,...  6 us
  transfers between devices with their start and end apart: 10, of which 4 were waited for; matrix products, arithmetic and copies ran while one was open for 12% of the time, Pallas kernels for 0%

profile of v11, /device:TPU:1, one launch (start us, length us, event | category | flops | bytes accessed | tf_op | source)
XLA Modules:
  0.0 244.3 jit_solution(11795505480750723899)
XLA Ops:
  7.2 0.7 all-gather.2.cloned.1.call-update
  8.0 0.8 mul.487
  8.7 0.7 dynamic_slice.7
  9.4 0.8 broadcast_select_fusion.6
  11.0 0.7 pad_add_fusion.1
  11.9 0.8 fusion.64
  12.9 0.8 fusion.75
  13.7 0.9 fusion.73
  14.6 1.0 compare_and_fusion
  15.6 56.7 %all-gather.2.cloned.1.call-done = bf16[1024,2048]{1,0:T(8,128)(2,1)} async-done(((bf16[1024,256]{1,0:T(8,128)(2,1)}), bf16[1024,2048]{1,0:T(8,128)(2,1)}) %all-gather.2.cloned.1.call-update) | async-done | bytes 4194320 | tf_op jit(solution)/shard_map/all_gather | solution.py:76
  72.3 3.4 %negate_multiply_fusion = (f32[1024,8]{0,1:T(8,128)S(1)}, f32[1024,8]{0,1:T(8,128)S(1)}) fusion(f32[8]{0:T(128)} %param.26, f32[8]{0:T(128)} %param.25, bf16[1024,2048]{1,0:T(8,128)(2,1)} %all-gather.2.cloned.1.call-done, bf16[2048,8]{0,1:T(8,128)(2,1)} %param.20), kind=kOutput, calls=%fused_computation.119 | convolution fusion | flops 33628160 | bytes 4292672 | tf_op jit(solution)/shard_map/dot_general | solution.py:79
  75.7 2.3 reduce-window.6
  78.6 3.6 %convolution_convert_fusion.1 = bf16[1024,256]{1,0:T(8,128)(2,1)S(1)} fusion(bf16[1024,2048]{1,0:T(8,128)(2,1)} %all-gather.2.cloned.1.call-done, bf16[2048,256]{1,0:T(8,128)(2,1)S(1)} %copy-done.21), kind=kOutput, calls=%fused_computation.36 | convolution fusion | flops 1074003968 | bytes 5767168 | tf_op jit(solution)/shard_map/dot_general | solution.py:79
  82.8 2.3 convolution_convert_fusion
  85.1 7.4 %collective-permute-start = (bf16[3,768]{1,0:T(4,128)(2,1)S(1)}, bf16[3,768]{1,0:T(4,128)(2,1)S(1)}, u32[]{:S(2)}, u32[]{:S(2)}) collective-permute-start(bf16[3,768]{1,0:T(4,128)(2,1)S(1)} %pad_maximum_fusion.5), channel_id=1, source_target_pairs={{0,8},{8,16},{16,24},{24,32},{32,40},{40,48},{48,56},{56,64},{64,7... | collective-permute-start | bytes 13832 | tf_op jit(solution)/shard_map/ppermute | solution.py:18
  93.4 1.3 multiply_convert_fusion.3
  94.7 0.8 fusion.72
  95.8 3.1 %fusion.40 = f32[1024,512]{1,0:T(8,128)} fusion(f32[512]{0:T(512)S(1)} %copy-done.17, f32[512]{0:T(512)S(1)} %bitcast.171, f32[1027,512]{1,0:T(8,128)S(1)} %maximum_convert_fusion, pred[1024]{0:T(1024)(128)(4,1)S(1)} %get-tuple-element.43, f32[512]{0:T(512)S(1)} %bitcast.172, pred[1024]{0:T(1024)(128)(4,1)S(1)} %get-tuple-element.44, f32[512]{0:T(512)S(1)} %bitcast.170, ...), kind=kLoop, calls=%fused_computation.71 | loop fusion | flops 8912896 | bytes 10499072 | tf_op jit(solution)/shard_map/reshape | solution.py:103
  99.0 3.0 %copy.72 = f32[1024,512]{0,1:T(8,128)} copy(f32[1024,512]{1,0:T(8,128)} %fusion.40) | data formatting | bytes 4194304 | tf_op jit(solution)/shard_map/reshape | solution.py:103
  102.0 3.2 %reshape.220 = f32[4,256,8,64]{1,0,3,2:T(4,128)} reshape(f32[1024,512]{0,1:T(8,128)} %copy.72) | data formatting | bytes 4194304 | tf_op jit(solution)/shard_map/reshape | solution.py:103
  105.1 2.6 %broadcast_multiply_fusion = (f32[4,256,8,64]{1,0,3,2:T(4,128)S(1)}, f32[4,256,8,64]{1,0,3,2:T(4,128)S(1)}) fusion(f32[4,256,8]{1,0,2:T(4,128)S(1)} %copy.77, f32[4,256,8,64]{1,0,3,2:T(4,128)} %reshape.220, f32[4,256,8]{1,0,2:T(4,128)S(1)} %copy.73), kind=kLoop, calls=%fused_computation.67 | loop fusion | flops 1048576 | bytes 6356992 | tf_op jit(solution)/shard_map/mul | solution.py:125
  107.7 1.3 fusion.19
  109.9 1.5 convolution_bitcast_fusion
  111.4 1.5 convolution_bitcast_fusion.1
  112.9 4.3 %collective-permute-start.4 = (f32[8,65,128]{2,1,0:T(8,128)S(1)}, f32[8,65,128]{2,1,0:T(8,128)S(1)}, u32[]{:S(2)}, u32[]{:S(2)}) collective-permute-start(f32[8,65,128]{2,1,0:T(8,128)S(1)} %pad_maximum_fusion.3), channel_id=1, source_target_pairs={{0,32},{8,40},{16,48},{24,56},{32,64},{40,72},{48,80},{56,88},{64,... | collective-permute-start | bytes 798728 | tf_op jit(solution)/shard_map/ppermute | solution.py:18
  117.3 6.8 %collective-permute-start.3 = (f32[8,65,128]{2,1,0:T(8,128)S(1)}, f32[8,65,128]{2,1,0:T(8,128)S(1)}, u32[]{:S(2)}, u32[]{:S(2)}) collective-permute-start(f32[8,65,128]{2,1,0:T(8,128)S(1)} %pad_maximum_fusion.3), channel_id=1, source_target_pairs={{0,24},{8,32},{16,40},{24,48},{32,56},{40,64},{48,72},{56,80},{64,... | collective-permute-start | bytes 798728 | tf_op jit(solution)/shard_map/ppermute | solution.py:18
  124.1 1.3 collective-permute-start.2
  125.4 2.6 %collective-permute-start.1 = (f32[8,65,128]{2,1,0:T(8,128)S(1)}, f32[8,65,128]{2,1,0:T(8,128)S(1)}, u32[]{:S(2)}, u32[]{:S(2)}) collective-permute-start(f32[8,65,128]{2,1,0:T(8,128)S(1)} %pad_maximum_fusion.3), channel_id=1, source_target_pairs={{0,8},{8,16},{16,24},{24,32},{32,40},{40,48},{48,56},{56,64},{64,7... | collective-permute-start | bytes 798728 | tf_op jit(solution)/shard_map/ppermute | solution.py:18
  128.4 10.9 %fusion = f32[4,8,64,256]{3,2,1,0:T(8,128)} fusion(f32[4,256,256]{2,1,0:T(8,128)S(1)} %fusion.77, f32[4,8,256]{2,1,0:T(8,128)S(1)} %add_bitcast_fusion.2, pred[4,256,256]{2,1,0:T(8,128)(4,1)S(1)} %copy-done.16, f32[4,256,8,64]{1,0,3,2:T(4,128)S(1)} %get-tuple-element.22), kind=kOutput, calls=%fused_computation.1 | convolution fusion | flops 1619001344 | bytes 5537792 | tf_op jit(solution)/shard_map/chts,cshp->cthp/dot_general | solution.py:119
  139.2 1.5 convolution_bitcast_fusion.2
  141.1 0.7 copy-done.6
  141.8 0.8 pad_maximum_fusion.4
  142.6 3.9 %collective-permute-start.6 = (f32[8,65,128]{2,1,0:T(8,128)}, f32[8,65,128]{2,1,0:T(8,128)}, u32[]{:S(2)}, u32[]{:S(2)}) collective-permute-start(f32[8,65,128]{2,1,0:T(8,128)} %pad_maximum_fusion.4), channel_id=1, source_target_pairs={{0,64},{8,72},{16,80},{24,88},{32,96},{40,104},{48,112},{56,120},{... | collective-permute-start | bytes 798728 | tf_op jit(solution)/shard_map/ppermute | solution.py:18
  146.5 4.4 %collective-permute-start.5 = (f32[8,65,128]{2,1,0:T(8,128)}, f32[8,65,128]{2,1,0:T(8,128)}, u32[]{:S(2)}, u32[]{:S(2)}) collective-permute-start(f32[8,65,128]{2,1,0:T(8,128)} %pad_maximum_fusion.4), channel_id=1, source_target_pairs={{0,32},{8,40},{16,48},{24,56},{32,64},{40,72},{48,80},{56,88},{64,... | collective-permute-start | bytes 798728 | tf_op jit(solution)/shard_map/ppermute | solution.py:18
  150.8 1.5 convolution_bitcast_fusion.3
  152.3 2.0 copy.83
  154.4 2.0 copy.82
  156.4 2.0 copy.81
  158.5 2.1 copy.80
  160.7 2.5 %collective-permute-start.7 = (f32[8,65,128]{2,1,0:T(8,128)}, f32[8,65,128]{2,1,0:T(8,128)S(1)}, u32[]{:S(2)}, u32[]{:S(2)}) collective-permute-start(f32[8,65,128]{2,1,0:T(8,128)} %pad_maximum_fusion.4), channel_id=1, source_target_pairs={{0,96},{8,104},{16,112},{24,120},{32,128},{40,136},{48,144},{56,15... | collective-permute-start | bytes 798728 | tf_op jit(solution)/shard_map/ppermute | solution.py:18
  163.4 3.8 %collective-permute-done.7 = f32[8,65,128]{2,1,0:T(8,128)S(1)} collective-permute-done((f32[8,65,128]{2,1,0:T(8,128)}, f32[8,65,128]{2,1,0:T(8,128)S(1)}, u32[]{:S(2)}, u32[]{:S(2)}) %collective-permute-start.7) | collective-permute-done | bytes 266272 | tf_op jit(solution)/shard_map/ppermute | solution.py:18
  167.2 0.8 add_bitcast_fusion
  168.1 3.5 %fusion.22 = (bf16[4,8,8,8,256]{4,3,2,1,0:T(8,128)(2,1)S(1)}, bf16[4,256]{1,0:T(4,128)(2,1)S(1)}) fusion(f32[8,64]{1,0:T(8,128)S(1)} %mul.487, f32[1,8,64,256]{3,2,1,0:T(8,128)S(1)} %bitcast.154, f32[1,8,64,256]{3,2,1,0:T(8,128)S(1)} %bitcast.155, f32[1,8,64,256]{3,2,1,0:T(8,128)S(1)} %bitcast.156, f32[1,8,64,256]{3,2,1,0:T(8,128)S(1)} %bitcast.157, ...), kind=kOutput, calls=%fused_computation.43 | convolution fusion | flops 815004672 | bytes 8687792 | tf_op jit(solution)/shard_map/ctn,chpn->cthp/dot_general | solution.py:184
  171.8 2.4 bitcast_convert_fusion
  174.2 2.3 pad_maximum_fusion
  176.5 58.2 %reduce-scatter.2.cloned.1.call-done = bf16[1028,256]{1,0:T(8,128)(2,1)} async-done(((bf16[1028,2048]{1,0:T(8,128)(2,1)}), bf16[1028,256]{1,0:T(8,128)(2,1)}) %reduce-scatter.2.cloned.1.call-update) | async-done | bytes 526352 | tf_op jit(solution)/shard_map/reduce_scatter | solution.py:205
  234.7 0.7 rsqrt_bitcast_fusion
  235.4 2.0 multiply_convert_fusion.2
  (101 shorter events, 5.5 us)
Async XLA Ops:
  7.2 164.6 %copy-start = (bf16[512,2048]{1,0:T(8,128)(2,1)S(1)}, bf16[512,2048]{1,0:T(8,128)(2,1)}, u32[]{:S(2)}) copy-start(bf16[512,2048]{1,0:T(8,128)(2,1)} %param.29) | copy-start | bytes 6291460
  7.2 65.1 %all-gather.2.cloned.1.call-start = ((), (), s32[]{:S(2)}) async-start(), calls=%async_computation.1 | async-start | bytes 4718592 | tf_op jit(solution)/shard_map/all_gather | solution.py:76
  7.9 226.8 %reduce-scatter.2.cloned.1.call-start = ((), (), s32[]{:S(2)}) async-start(), calls=%async_computation.2 | async-start | bytes 4755456 | tf_op jit(solution)/shard_map/reduce_scatter | solution.py:205
  15.6 63.1 %copy-start.21 = (bf16[2048,256]{1,0:T(8,128)(2,1)S(1)}, bf16[2048,256]{1,0:T(8,128)(2,1)}, u32[]{:S(2)}) copy-start(bf16[2048,256]{1,0:T(8,128)(2,1)} %param.19) | copy-start | bytes 3145732
  78.6 3.6 %copy-start.2 = (bf16[1024,2048]{1,0:T(8,128)(2,1)S(1)}, bf16[1024,2048]{1,0:T(8,128)(2,1)}, u32[]{:S(2)}) copy-start(bf16[1024,2048]{1,0:T(8,128)(2,1)} %all-gather.2.cloned.1.call-done) | copy-start | bytes 12582916
  78.6 4.1 %copy-start.19 = (bf16[2048,512]{1,0:T(8,128)(2,1)S(1)}, bf16[2048,512]{1,0:T(8,128)(2,1)}, u32[]{:S(2)}) copy-start(bf16[2048,512]{1,0:T(8,128)(2,1)} %param.18) | copy-start | bytes 6291460
  82.8 10.6 %copy-start.18 = (f32[256]{0:T(256)S(1)}, f32[256]{0:T(256)}, u32[]{:S(2)}) copy-start(f32[256]{0:T(256)} %param.24) | copy-start | bytes 3076
  85.1 8.1 %collective-permute-start = (bf16[3,768]{1,0:T(4,128)(2,1)S(1)}, bf16[3,768]{1,0:T(4,128)(2,1)S(1)}, u32[]{:S(2)}, u32[]{:S(2)}) collective-permute-start(bf16[3,768]{1,0:T(4,128)(2,1)S(1)} %pad_maximum_fusion.5), channel_id=1, source_target_pairs={{0,8},{8,16},{16,24},{24,32},{32,40},{40,48},{48,56},{56,64},{64,7... | collective-permute-start | bytes 13832 | tf_op jit(solution)/shard_map/ppermute | solution.py:18
  94.7 1.1 copy-start.17
  95.5 12.2 %copy-start.8 = (bf16[1024,128]{1,0:T(8,128)(2,1)}, bf16[1024,128]{1,0:T(8,128)(2,1)S(1)}, u32[]{:S(2)}) copy-start(bf16[1024,128]{1,0:T(8,128)(2,1)S(1)} %get-tuple-element.25) | copy-start | bytes 786436
  105.1 4.1 %copy-start.20 = (bf16[2048,512]{1,0:T(8,128)(2,1)S(1)}, bf16[2048,512]{1,0:T(8,128)(2,1)}, u32[]{:S(2)}) copy-start(bf16[2048,512]{1,0:T(8,128)(2,1)} %param.17) | copy-start | bytes 6291460
  107.7 2.2 copy-start.3
  109.2 31.9 %copy-start.4 = (f32[8,64,128]{2,1,0:T(8,128)}, f32[8,64,128]{2,1,0:T(8,128)S(1)}, u32[]{:S(2)}) copy-start(f32[8,64,128]{2,1,0:T(8,128)S(1)} %get-tuple-element.15) | copy-start | bytes 786436
  111.4 16.7 %copy-start.9 = (bf16[1024,128]{1,0:T(8,128)(2,1)S(1)}, bf16[1024,128]{1,0:T(8,128)(2,1)}, u32[]{:S(2)}) copy-start(bf16[1024,128]{1,0:T(8,128)(2,1)} %copy-done.8) | copy-start | bytes 786436
  111.4 16.7 %copy-start.10 = (bf16[1024,128]{1,0:T(8,128)(2,1)S(1)}, bf16[1024,128]{1,0:T(8,128)(2,1)}, u32[]{:S(2)}) copy-start(bf16[1024,128]{1,0:T(8,128)(2,1)} %get-tuple-element.26) | copy-start | bytes 786436
  111.4 17.0 %copy-start.16 = (pred[4,256,256]{2,1,0:T(8,128)(4,1)S(1)}, pred[4,256,256]{2,1,0:T(8,128)(4,1)}, u32[]{:S(2)}) copy-start(pred[4,256,256]{2,1,0:T(8,128)(4,1)} %compare_and_fusion) | copy-start | bytes 786436
  112.9 27.9 %collective-permute-start.4 = (f32[8,65,128]{2,1,0:T(8,128)S(1)}, f32[8,65,128]{2,1,0:T(8,128)S(1)}, u32[]{:S(2)}, u32[]{:S(2)}) collective-permute-start(f32[8,65,128]{2,1,0:T(8,128)S(1)} %pad_maximum_fusion.3), channel_id=1, source_target_pairs={{0,32},{8,40},{16,48},{24,56},{32,64},{40,72},{48,80},{56,88},{64,... | collective-permute-start | bytes 798728 | tf_op jit(solution)/shard_map/ppermute | solution.py:18
  117.3 23.5 %collective-permute-start.3 = (f32[8,65,128]{2,1,0:T(8,128)S(1)}, f32[8,65,128]{2,1,0:T(8,128)S(1)}, u32[]{:S(2)}, u32[]{:S(2)}) collective-permute-start(f32[8,65,128]{2,1,0:T(8,128)S(1)} %pad_maximum_fusion.3), channel_id=1, source_target_pairs={{0,24},{8,32},{16,40},{24,48},{32,56},{40,64},{48,72},{56,80},{64,... | collective-permute-start | bytes 798728 | tf_op jit(solution)/shard_map/ppermute | solution.py:18
  124.1 16.7 %collective-permute-start.2 = (f32[8,65,128]{2,1,0:T(8,128)S(1)}, f32[8,65,128]{2,1,0:T(8,128)S(1)}, u32[]{:S(2)}, u32[]{:S(2)}) collective-permute-start(f32[8,65,128]{2,1,0:T(8,128)S(1)} %pad_maximum_fusion.3), channel_id=1, source_target_pairs={{0,16},{8,24},{16,32},{24,40},{32,48},{40,56},{48,64},{56,72},{64,... | collective-permute-start | bytes 798728 | tf_op jit(solution)/shard_map/ppermute | solution.py:18
  125.4 15.4 %collective-permute-start.1 = (f32[8,65,128]{2,1,0:T(8,128)S(1)}, f32[8,65,128]{2,1,0:T(8,128)S(1)}, u32[]{:S(2)}, u32[]{:S(2)}) collective-permute-start(f32[8,65,128]{2,1,0:T(8,128)S(1)} %pad_maximum_fusion.3), channel_id=1, source_target_pairs={{0,8},{8,16},{16,24},{24,32},{32,40},{40,48},{48,56},{56,64},{64,7... | collective-permute-start | bytes 798728 | tf_op jit(solution)/shard_map/ppermute | solution.py:18
  141.1 0.7 copy-start.6
  142.6 20.7 %collective-permute-start.6 = (f32[8,65,128]{2,1,0:T(8,128)}, f32[8,65,128]{2,1,0:T(8,128)}, u32[]{:S(2)}, u32[]{:S(2)}) collective-permute-start(f32[8,65,128]{2,1,0:T(8,128)} %pad_maximum_fusion.4), channel_id=1, source_target_pairs={{0,64},{8,72},{16,80},{24,88},{32,96},{40,104},{48,112},{56,120},{... | collective-permute-start | bytes 798728 | tf_op jit(solution)/shard_map/ppermute | solution.py:18
  146.5 16.8 %collective-permute-start.5 = (f32[8,65,128]{2,1,0:T(8,128)}, f32[8,65,128]{2,1,0:T(8,128)}, u32[]{:S(2)}, u32[]{:S(2)}) collective-permute-start(f32[8,65,128]{2,1,0:T(8,128)} %pad_maximum_fusion.4), channel_id=1, source_target_pairs={{0,32},{8,40},{16,48},{24,56},{32,64},{40,72},{48,80},{56,88},{64,... | collective-permute-start | bytes 798728 | tf_op jit(solution)/shard_map/ppermute | solution.py:18
  160.5 6.7 %copy-start.5 = (f32[8,64,128]{2,1,0:T(8,128)S(1)}, f32[8,64,128]{2,1,0:T(8,128)}, u32[]{:S(2)}) copy-start(f32[8,64,128]{2,1,0:T(8,128)} %copy-done.4) | copy-start | bytes 786436
  160.5 6.7 %copy-start.7 = (f32[8,64,128]{2,1,0:T(8,128)S(1)}, f32[8,64,128]{2,1,0:T(8,128)}, u32[]{:S(2)}) copy-start(f32[8,64,128]{2,1,0:T(8,128)} %copy-done.6) | copy-start | bytes 786436
  160.5 7.5 %copy-start.14 = (f32[512,256]{1,0:T(8,128)S(1)}, f32[512,256]{1,0:T(8,128)}, u32[]{:S(2)}) copy-start(f32[512,256]{1,0:T(8,128)} %copy.81) | copy-start | bytes 1572868
  160.5 7.5 %copy-start.15 = (f32[512,256]{1,0:T(8,128)S(1)}, f32[512,256]{1,0:T(8,128)}, u32[]{:S(2)}) copy-start(f32[512,256]{1,0:T(8,128)} %copy.80) | copy-start | bytes 1572868
  160.7 7.4 %copy-start.1 = (f32[4,256,8,64]{1,0,3,2:T(4,128)S(1)}, f32[4,256,8,64]{1,0,3,2:T(4,128)}, u32[]{:S(2)}) copy-start(f32[4,256,8,64]{1,0,3,2:T(4,128)} %reshape.220) | copy-start | bytes 6291460
  160.7 7.4 %copy-start.11 = (bf16[1024,128]{1,0:T(8,128)(2,1)S(1)}, bf16[1024,128]{1,0:T(8,128)(2,1)}, u32[]{:S(2)}) copy-start(bf16[1024,128]{1,0:T(8,128)(2,1)} %get-tuple-element.26) | copy-start | bytes 786436
  160.7 7.4 %copy-start.12 = (f32[512,256]{1,0:T(8,128)S(1)}, f32[512,256]{1,0:T(8,128)}, u32[]{:S(2)}) copy-start(f32[512,256]{1,0:T(8,128)} %copy.83) | copy-start | bytes 1572868
  160.7 7.4 %copy-start.13 = (f32[512,256]{1,0:T(8,128)S(1)}, f32[512,256]{1,0:T(8,128)}, u32[]{:S(2)}) copy-start(f32[512,256]{1,0:T(8,128)} %copy.82) | copy-start | bytes 1572868
  160.7 7.4 %copy-start.22 = (f32[8]{0:T(128)S(1)}, f32[8]{0:T(128)}, u32[]{:S(2)}) copy-start(f32[8]{0:T(128)} %param.27) | copy-start | bytes 100
  160.7 6.5 %collective-permute-start.7 = (f32[8,65,128]{2,1,0:T(8,128)}, f32[8,65,128]{2,1,0:T(8,128)S(1)}, u32[]{:S(2)}, u32[]{:S(2)}) collective-permute-start(f32[8,65,128]{2,1,0:T(8,128)} %pad_maximum_fusion.4), channel_id=1, source_target_pairs={{0,96},{8,104},{16,112},{24,120},{32,128},{40,136},{48,144},{56,15... | collective-permute-start | bytes 798728 | tf_op jit(solution)/shard_map/ppermute | solution.py:18
Sparse Core Ops, SparseCore 0:
  9.7 62.5 all-gather.1
  176.6 58.0 reduce-scatter.1
